TPU v7x, 32 devices: a whole 2x2x4 slice. The times are simulated.
32 devices in a mesh: gx: 4 (over z), gy: 8 (over y, x, core).
Axes of the slice: x: 2, y: 2, z: 4, core: 2. Of those that a mesh axis runs over, the one named last changes fastest.
Arguments:
- flow: float32 [19, 32, 64, 512], P(None, 'gx', 'gy'), may hold values from 0.0116 to 0.467, as said below
- field: float32 [7, 32, 64, 512], P(None, 'gx', 'gy'), may hold values from -0.45 to 0.45, as said below
- adj_flow_in: float32 [19, 32, 64, 512], P(None, 'gx', 'gy'), may hold values from -6 to 6
- adj_field_in: float32 [7, 32, 64, 512], P(None, 'gx', 'gy'), may hold values from -6 to 6
- profile: float32 [32, 64, 512], P('gx', 'gy'), may hold values from 0.5 to 1.5
- strengths: float32 [32], replicated, may hold values from 0.5 to 2
- wall: int32 [32, 64, 512], P('gx', 'gy'), may hold values 0 or 1
- magnet: int32 [32, 64, 512], P('gx', 'gy'), may hold values from 0 to 31
Outputs:
- new_flow: float32 [19, 32, 64, 512], P(None, 'gx', 'gy')
- new_field: float32 [7, 32, 64, 512], P(None, 'gx', 'gy')
- adj_flow: float32 [19, 32, 64, 512], P(None, 'gx', 'gy')
- adj_field: float32 [7, 32, 64, 512], P(None, 'gx', 'gy')
- magnet_grad: float32 [32], replicated
Inputs may be any that keep to these rules, and one draw needn't show every extreme that they name: flow populations are positive, near w_i times a density of order one. field populations are v_k times a local field value plus noise.
All inputs are finite; a program needn't handle non-finite values. No bound on the sum of `wall` on one device may be relied on, other than what follows from the above.
Results may differ from a plain program's by a relative error of at most 0.00023.
Values sent between devices are 32-bit elements; how exact they have to be, the bound alone decides.
No kernel may reach another device: no remote copies, remote signals or barrier semaphores. Data moves between devices by JAX's collectives and lax.ppermute only.
A program may use at most 64 MiB of HBM per device.

v0:
```python
import math

import jax
import jax.numpy as jnp
import numpy as np
from jax import lax
from jax.sharding import PartitionSpec as P

LATTICE = np.array(
    [
        [0, 0, 0],
        [1, 0, 0],
        [-1, 0, 0],
        [0, 1, 0],
        [0, -1, 0],
        [0, 0, 1],
        [0, 0, -1],
        [1, 1, 0],
        [-1, -1, 0],
        [1, -1, 0],
        [-1, 1, 0],
        [1, 0, 1],
        [-1, 0, -1],
        [1, 0, -1],
        [-1, 0, 1],
        [0, 1, 1],
        [0, -1, -1],
        [0, 1, -1],
        [0, -1, 1],
    ]
)
OPPOSITE = [0, 2, 1, 4, 3, 6, 5, 8, 7, 10, 9, 12, 11, 14, 13, 16, 15, 18, 17]
WEIGHTS_FLOW = [1.0 / 3.0] + [1.0 / 18.0] * 6 + [1.0 / 36.0] * 12
WEIGHTS_FIELD = [0.25] + [0.125] * 6
OMEGA_PLUS = 1.25
OMEGA_MINUS = 1.0 / 1.125
TAU_PLUS = 0.8
COUPLE = 2.0
SOURCE = 2.0


def with_halo(block, sides, width):
    for axis, dim in sides:
        count = lax.axis_size(axis)
        forward = [(i, i + 1) for i in range(count - 1)]
        forward.append((count - 1, 0))
        backward = [(target, source) for source, target in forward]
        low = lax.ppermute(
            lax.slice_in_dim(block, block.shape[dim] - width, None, axis=dim), axis, forward
        )
        high = lax.ppermute(lax.slice_in_dim(block, 0, width, axis=dim), axis, backward)
        block = jnp.concatenate([low, block, high], axis=dim)
    return block


def column(values, ndim):
    return jnp.array([float(v) for v in values], jnp.float32).reshape(
        (len(values),) + (1,) * (ndim - 1)
    )


def collide(flow, field, bfield, fluid):
    ndim = flow.ndim
    velx = column(LATTICE[:, 0], ndim)
    vely = column(LATTICE[:, 1], ndim)
    velz = column(LATTICE[:, 2], ndim)
    weight = column(WEIGHTS_FLOW, ndim)
    weight_b = column(WEIGHTS_FIELD, ndim)
    rho = jnp.sum(flow, 0) + (1.0 - fluid)
    momx = jnp.sum(velx * flow, 0)
    momy = jnp.sum(vely * flow, 0)
    momz = jnp.sum(velz * flow, 0)
    speed_x = momx / rho
    speed_y = momy / rho
    speed_z = momz / rho
    bvalue = jnp.sum(field, 0)
    current = jnp.sum(vely[:7] * field, 0) - bvalue * speed_y
    shear = jnp.sum(velx * vely * flow, 0) - momx * speed_y
    force = COUPLE * bfield * current
    shifted = speed_x + TAU_PLUS * force / rho
    along = velx * shifted + vely * speed_y + velz * speed_z
    square = shifted * shifted + speed_y * speed_y + speed_z * speed_z
    equil = weight * rho * (1.0 + 3.0 * along + 4.5 * along * along - 1.5 * square)
    offset = flow - equil
    flipped = jnp.stack([offset[k] for k in OPPOSITE], 0)
    post_flow = (
        flow - 0.5 * OMEGA_PLUS * (offset + flipped) - 0.5 * OMEGA_MINUS * (offset - flipped)
    )
    along_b = velx[:7] * speed_x + vely[:7] * speed_y + velz[:7] * speed_z
    post_field = weight_b * bvalue * (1.0 + 4.0 * along_b) + weight_b * SOURCE * bfield * shear
    return (post_flow, post_field)


def pull_stream(pad_pops, pad_fluid, post, fluid, count):
    size_x, size_y, size_z = fluid.shape
    parts = []
    for i in range(count):
        cx, cy, cz = (int(v) for v in LATTICE[i])
        near = pad_fluid[
            1 - cx : 1 - cx + size_x, 1 - cy : 1 - cy + size_y, 1 - cz : 1 - cz + size_z
        ]
        moved = pad_pops[
            i, 1 - cx : 1 - cx + size_x, 1 - cy : 1 - cy + size_y, 1 - cz : 1 - cz + size_z
        ]
        parts.append(fluid * (near * moved + (1.0 - near) * post[OPPOSITE[i]]))
    return jnp.stack(parts, 0)


def push_adjoint(pad_pops, pad_fluid, local, fluid, count):
    size_x, size_y, size_z = fluid.shape
    parts = []
    for i in range(count):
        cx, cy, cz = (int(v) for v in LATTICE[i])
        near = pad_fluid[
            1 + cx : 1 + cx + size_x, 1 + cy : 1 + cy + size_y, 1 + cz : 1 + cz + size_z
        ]
        moved = pad_pops[
            i, 1 + cx : 1 + cx + size_x, 1 + cy : 1 + cy + size_y, 1 + cz : 1 + cz + size_z
        ]
        parts.append(fluid * (near * moved + (1.0 - near) * local[OPPOSITE[i]]))
    return jnp.stack(parts, 0)


def close_ends(padded):
    return jnp.pad(padded, ((0, 0), (0, 0), (0, 0), (1, 1)))


def wall_rims(pad_fluid):
    rows = lax.broadcasted_iota(jnp.int32, pad_fluid.shape, 1)
    here = lax.axis_index("gy")
    last = lax.axis_size("gy") - 1
    outside = (rows == 0) & (here == 0) | (rows == pad_fluid.shape[1] - 1) & (here == last)
    return jnp.where(outside, 0.0, pad_fluid)


def on_device(flow, field, adj_flow_in, adj_field_in, profile, strengths, wall, magnet):
    count_mag = strengths.shape[0]
    fluid = (1 - wall).astype(jnp.float32)
    table = (
        magnet[None] == lax.broadcasted_iota(jnp.int32, (count_mag,) + magnet.shape, 0)
    ).astype(jnp.float32)
    bcell = jnp.tensordot(strengths, table, axes=1, precision=lax.Precision.HIGHEST) * profile
    post_flow, post_field = collide(flow, field, bcell, fluid)
    joined = jnp.concatenate([post_flow, post_field, fluid[None]], 0)
    padded = close_ends(with_halo(joined, (("gx", 1), ("gy", 2)), 1))
    pad_fluid = wall_rims(padded[26])
    pad_state = padded[:26]
    incoming = jnp.concatenate([adj_flow_in, adj_field_in], 0)
    pad_adj = close_ends(with_halo(incoming, (("gx", 1), ("gy", 2)), 1))
    new_flow = pull_stream(pad_state[:19], pad_fluid, post_flow, fluid, 19)
    new_field = pull_stream(pad_state[19:], pad_fluid, post_field, fluid, 7)
    ast_flow = push_adjoint(pad_adj[:19], pad_fluid, adj_flow_in, fluid, 19)
    ast_field = push_adjoint(pad_adj[19:], pad_fluid, adj_field_in, fluid, 7)

    def local_collide(first, second, third):
        return collide(first, second, third, fluid)

    _, pullback = jax.vjp(local_collide, new_flow, new_field, bcell)
    adj_flow, adj_field, dcell = pullback((ast_flow, ast_field))
    shares = jnp.tensordot(table, dcell * profile, axes=3, precision=lax.Precision.HIGHEST)
    totals = lax.psum(shares, ("gx", "gy"))
    cells = (
        flow.shape[1] * lax.axis_size("gx") * flow.shape[2] * lax.axis_size("gy") * flow.shape[3]
    )
    magnet_grad = totals / math.sqrt(cells / count_mag)
    return (new_flow, new_field, adj_flow, adj_field, magnet_grad)


def solution(mesh):
    return jax.shard_map(
        on_device,
        mesh=mesh,
        in_specs=(
            P(None, "gx", "gy", None),
            P(None, "gx", "gy", None),
            P(None, "gx", "gy", None),
            P(None, "gx", "gy", None),
            P("gx", "gy", None),
            P(),
            P("gx", "gy", None),
            P("gx", "gy", None),
        ),
        out_specs=(
            P(None, "gx", "gy", None),
            P(None, "gx", "gy", None),
            P(None, "gx", "gy", None),
            P(None, "gx", "gy", None),
            P(),
        ),
        check_vma=False,
    )
```

profile of v0, /device:TPU:0, one launch (start us, length us, event | category | flops | bytes accessed | tf_op | source)
XLA Modules:
  0.0 164.3 jit_solution(2467456283072510997)
XLA Ops:
  0.7 2.0 %constant_dynamic-update-slice_fusion.46 = f32[26,8,8,512]{3,2,1,0:T(8,128)S(1)} fusion(f32[19,8,8,512]{3,2,1,0:T(8,128)} %param.20), kind=kLoop, calls=%fused_computation.129 | loop fusion | bytes 4980736
  3.8 3.0 %collective-permute-start.5 = (f32[26,1,8,512]{3,2,1,0:T(8,128)}, f32[26,1,8,512]{3,2,1,0:T(8,128)}, u32[]{:S(2)}, u32[]{:S(2)}) collective-permute-start(f32[26,1,8,512]{3,2,1,0:T(8,128)} %get-tuple-element.112), channel_id=1, source_target_pairs={{0,8},{8,16},{16,24},{24,0},{1,9},{9,17},{17,25},{25,1},{2,10},{10... | collective-permute-start | bytes 1277960 | tf_op jit(solution)/shard_map/ppermute | solution.py:48
  6.8 2.1 %collective-permute-start.4 = (f32[26,1,8,512]{3,2,1,0:T(8,128)}, f32[26,1,8,512]{3,2,1,0:T(8,128)}, u32[]{:S(2)}, u32[]{:S(2)}) collective-permute-start(f32[26,1,8,512]{3,2,1,0:T(8,128)} %get-tuple-element.113), channel_id=1, source_target_pairs={{8,0},{16,8},{24,16},{0,24},{9,1},{17,9},{25,17},{1,25},{10,2},{18... | collective-permute-start | bytes 1277960 | tf_op jit(solution)/shard_map/ppermute | solution.py:51
  9.7 1.6 fusion.4
  12.6 1.3 fusion.16
  14.3 1.8 %multiply_subtract_fusion = f32[19,8,8,512]{3,2,1,0:T(8,128)S(1)} fusion(f32[19,8,8,512]{3,2,1,0:T(8,128)S(1)} %constant_dynamic-update-slice_fusion, f32[19,8,8,512]{3,2,1,0:T(8,128)S(1)} %copy-done.7, f32[8,8,512]{2,1,0:T(8,128)S(1)} %get-tuple-element.77, f32[8,8,512]{2,1,0:T(8,128)S(1)} %get-tuple-element.81, f32[19]{0:T(128)S(1)} %copy-done.44, ...), kind=kLoop, calls=%fused_computation.48 | loop fusion | flops 12451840 | bytes 8126768 | tf_op jit(solution)/shard_map/sub | solution.py:87
  18.3 3.8 %collective-permute-start.1 = (f32[27,1,8,512]{3,2,1,0:T(8,128)}, f32[27,1,8,512]{3,2,1,0:T(8,128)}, u32[]{:S(2)}, u32[]{:S(2)}) collective-permute-start(f32[27,1,8,512]{3,2,1,0:T(8,128)} %get-tuple-element.111), channel_id=1, source_target_pairs={{8,0},{16,8},{24,16},{0,24},{9,1},{17,9},{25,17},{1,25},{10,2},{18... | collective-permute-start | bytes 1327112 | tf_op jit(solution)/shard_map/ppermute | solution.py:51
  22.1 7.0 %collective-permute-done.4 = f32[26,1,8,512]{3,2,1,0:T(8,128)} collective-permute-done((f32[26,1,8,512]{3,2,1,0:T(8,128)}, f32[26,1,8,512]{3,2,1,0:T(8,128)}, u32[]{:S(2)}, u32[]{:S(2)}) %collective-permute-start.4) | collective-permute-done | bytes 426016 | tf_op jit(solution)/shard_map/ppermute | solution.py:51
  29.1 4.5 %pad_maximum_fusion.5 = (f32[26,10,1,512]{3,2,1,0:T(1,128)S(1)}, f32[26,10,1,512]{3,2,1,0:T(1,128)S(1)}) fusion(f32[26,1,8,512]{3,2,1,0:T(8,128)} %collective-permute-done.4, f32[26,8,8,512]{3,2,1,0:T(8,128)} %copy-done.2, f32[26,1,8,512]{3,2,1,0:T(8,128)} %collective-permute-done.5), kind=kLoop, calls=%fused_computation.72 | loop fusion | flops 532480 | bytes 5324800 | tf_op jit(solution)/shard_map/concatenate | solution.py:52
  33.7 2.6 %collective-permute-start.6 = (f32[26,10,1,512]{3,2,1,0:T(1,128)S(1)}, f32[26,10,1,512]{3,2,1,0:T(1,128)S(1)}, u32[]{:S(2)}, u32[]{:S(2)}) collective-permute-start(f32[26,10,1,512]{3,2,1,0:T(1,128)S(1)} %get-tuple-element.109), channel_id=1, source_target_pairs={{1,0},{2,1},{3,2},{4,3},{5,4},{6,5},{7,6},{0,7},{9,8},{10,9},{11,1... | collective-permute-start | bytes 1597448 | tf_op jit(solution)/shard_map/ppermute | solution.py:51
  36.3 2.2 %collective-permute-done = f32[27,1,8,512]{3,2,1,0:T(8,128)} collective-permute-done((f32[27,1,8,512]{3,2,1,0:T(8,128)}, f32[27,1,8,512]{3,2,1,0:T(8,128)}, u32[]{:S(2)}, u32[]{:S(2)}) %collective-permute-start) | collective-permute-done | bytes 442400 | tf_op jit(solution)/shard_map/ppermute | solution.py:48
  38.5 8.1 %collective-permute-done.1 = f32[27,1,8,512]{3,2,1,0:T(8,128)} collective-permute-done((f32[27,1,8,512]{3,2,1,0:T(8,128)}, f32[27,1,8,512]{3,2,1,0:T(8,128)}, u32[]{:S(2)}, u32[]{:S(2)}) %collective-permute-start.1) | collective-permute-done | bytes 442400 | tf_op jit(solution)/shard_map/ppermute | solution.py:51
  46.6 2.2 %pad_maximum_fusion.4 = (f32[27,10,1,512]{3,2,1,0:T(1,128)S(1)}, f32[27,10,1,512]{3,2,1,0:T(1,128)S(1)}) fusion(f32[27,1,8,512]{3,2,1,0:T(8,128)} %collective-permute-done.1, f32[27,1,8,512]{3,2,1,0:T(8,128)} %collective-permute-done, f32[1,8,8,512]{3,2,1,0:T(8,128)S(1)} %copy-done.9, f32[7,8,8,512]{3,2,1,0:T(8,128)S(1)} %fusion.21, ...), kind=kLoop, calls=%fused_computation.71 | loop fusion | flops 1105920 | bytes 5529600 | tf_op jit(solution)/shard_map/slice | solution.py:49
  48.8 2.6 %collective-permute-start.3 = (f32[27,10,1,512]{3,2,1,0:T(1,128)S(1)}, f32[27,10,1,512]{3,2,1,0:T(1,128)S(1)}, u32[]{:S(2)}, u32[]{:S(2)}) collective-permute-start(f32[27,10,1,512]{3,2,1,0:T(1,128)S(1)} %get-tuple-element.103), channel_id=1, source_target_pairs={{1,0},{2,1},{3,2},{4,3},{5,4},{6,5},{7,6},{0,7},{9,8},{10,9},{11,1... | collective-permute-start | bytes 1658888 | tf_op jit(solution)/shard_map/ppermute | solution.py:51
  51.5 13.1 %select_maximum_fusion.6 = f32[26,10,10,514]{3,2,1,0:T(8,128)S(1)} fusion(f32[26,10,1,512]{3,2,1,0:T(1,128)S(1)} %collective-permute-done.6, f32[26,10,1,512]{3,2,1,0:T(1,128)S(1)} %collective-permute-done.7, f32[26,1,8,512]{3,2,1,0:T(8,128)} %collective-permute-done.4, f32[26,8,8,512]{3,2,1,0:T(8,128)S(1)} %copy-done.3, ...), kind=kLoop, calls=%fused_computation.11 | loop fusion | flops 16036800 | bytes 10670400 | tf_op jit(solution)/shard_map/concatenate | solution.py:52
  64.6 21.7 %select_maximum_fusion = f32[27,10,10,514]{3,2,1,0:T(8,128)S(1)} fusion(f32[27,10,1,512]{3,2,1,0:T(1,128)S(1)} %collective-permute-done.3, f32[27,10,1,512]{3,2,1,0:T(1,128)S(1)} %collective-permute-done.2, f32[27,1,8,512]{3,2,1,0:T(8,128)} %collective-permute-done.1, f32[27,1,8,512]{3,2,1,0:T(8,128)} %collective-permute-done, ...), kind=kLoop, calls=%fused_computation.4 | loop fusion | flops 22204800 | bytes 11080800 | tf_op jit(solution)/shard_map/concatenate | solution.py:52
  104.4 2.6 %fusion.7 = (f32[19,8,8,512]{3,2,1,0:T(8,128)S(1)}, f32[19,8,8,512]{3,2,1,0:T(8,128)S(1)}) fusion(f32[8,8,512]{2,1,0:T(8,128)S(1)} %get-tuple-element.47, f32[8,8,512]{2,1,0:T(8,128)S(1)} %get-tuple-element.40, f32[8,8,512]{2,1,0:T(8,128)S(1)} %get-tuple-element.43, f32[8,8,512]{2,1,0:T(8,128)S(1)} %get-tuple-element.41, f32[19]{0:T(128)S(1)} %copy-done.44, ...), kind=kLoop, calls=%fused_computation.25 | loop fusion | flops 25526272 | bytes 10355011 | tf_op jit(solution)/shard_map/transpose(jvp())/add_any | solution.py:83
  107.1 3.1 %multiply_reduce_fusion.3 = (f32[8,8,512]{2,1,0:T(8,128)}, f32[8,8,512]{2,1,0:T(8,128)S(1)}, f32[8,8,512]{2,1,0:T(8,128)}, f32[8,8,512]{2,1,0:T(8,128)S(1)}, f32[8,8,512]{2,1,0:T(8,128)}) fusion(f32[19,8,8,512]{3,2,1,0:T(8,128)S(1)} %get-tuple-element.48, f32[19]{0:T(128)S(1)} %copy-done.44, f32[19]{0:T(128)S(1)} %copy-done.46, f32[19]{0:T(128)S(1)} %copy-done.45, ...), kind=kLoop, calls=%fused_computation.39 | loop fusion | flops 14778368 | bytes 6291760 | tf_op jit(solution)/shard_map/transpose(jvp())/reduce_sum | solution.py:81
  110.3 1.6 multiply_reduce_fusion.11
  112.6 5.1 %fusion.18 = f32[32]{0:T(128)} fusion(pred[32,8,8,512]{3,2,1,0:T(8,128)(4,1)S(1)} %copy-done.35, f32[8,8,512,1]{2,1,0,3:T(8,128)S(1)} %get-tuple-element.33), kind=kOutput, calls=%fused_computation.55 | convolution fusion | flops 12582912 | bytes 1179776 | tf_op jit(solution)/shard_map/dot_general | solution.py:160
  117.7 39.0 %psum.7 = f32[32]{0:T(128)} all-reduce(f32[32]{0:T(128)} %fusion.18), channel_id=1, replica_groups=mesh['gx'=4,'gy'=8] {'gx','gy'}, use_global_device_ids=true, to_apply=%region_23.24 | all-reduce | flops 32 | bytes 256 | tf_op jit(solution)/shard_map/psum | solution.py:161
  156.8 1.2 broadcast_multiply_fusion
  160.2 1.2 fusion.239
  161.8 2.5 %add_add_fusion = f32[19,8,8,512]{3,2,1,0:T(8,128)} fusion(f32[19,8,8,512]{3,2,1,0:T(8,128)S(1)} %copy-done.6, f32[19,8,8,512]{3,2,1,0:T(8,128)S(1)} %get-tuple-element.49, f32[8,8,512]{2,1,0:T(8,128)S(1)} %get-tuple-element.133, f32[8,8,512]{2,1,0:T(8,128)S(1)} %get-tuple-element.138, f32[8,8,512]{2,1,0:T(8,128)S(1)} %get-tuple-element.37, ...), kind=kLoop, calls=%fused_computation.36 | loop fusion | flops 6225920 | bytes 8126768 | tf_op jit(solution)/shard_map/transpose(jvp())/add_any | solution.py:69
  (218 shorter events, 26.3 us)
Async XLA Ops:
  0.6 9.1 %copy-start = (f32[32]{0:T(128)S(1)}, f32[32]{0:T(128)}, u32[]{:S(2)}) copy-start(f32[32]{0:T(128)} %param.23) | copy-start | bytes 388
  2.7 6.8 %copy-start.36 = (f32[7,8,8,512]{3,2,1,0:T(8,128)S(1)}, f32[7,8,8,512]{3,2,1,0:T(8,128)}, u32[]{:S(2)}) copy-start(f32[7,8,8,512]{3,2,1,0:T(8,128)} %param.19) | copy-start | bytes 2752516
  2.8 8.5 %copy-start.2 = (f32[26,8,8,512]{3,2,1,0:T(8,128)}, f32[26,8,8,512]{3,2,1,0:T(8,128)S(1)}, u32[]{:S(2)}) copy-start(f32[26,8,8,512]{3,2,1,0:T(8,128)S(1)} %constant_dynamic-update-slice_fusion.45) | copy-start | bytes 10223620
  3.8 18.4 %collective-permute-start.5 = (f32[26,1,8,512]{3,2,1,0:T(8,128)}, f32[26,1,8,512]{3,2,1,0:T(8,128)}, u32[]{:S(2)}, u32[]{:S(2)}) collective-permute-start(f32[26,1,8,512]{3,2,1,0:T(8,128)} %get-tuple-element.112), channel_id=1, source_target_pairs={{0,8},{8,16},{16,24},{24,0},{1,9},{9,17},{17,25},{25,1},{2,10},{10... | collective-permute-start | bytes 1277960 | tf_op jit(solution)/shard_map/ppermute | solution.py:48
  6.8 22.3 %collective-permute-start.4 = (f32[26,1,8,512]{3,2,1,0:T(8,128)}, f32[26,1,8,512]{3,2,1,0:T(8,128)}, u32[]{:S(2)}, u32[]{:S(2)}) collective-permute-start(f32[26,1,8,512]{3,2,1,0:T(8,128)} %get-tuple-element.113), channel_id=1, source_target_pairs={{8,0},{16,8},{24,16},{0,24},{9,1},{17,9},{25,17},{1,25},{10,2},{18... | collective-permute-start | bytes 1277960 | tf_op jit(solution)/shard_map/ppermute | solution.py:51
  18.3 20.2 %collective-permute-start = (f32[27,1,8,512]{3,2,1,0:T(8,128)}, f32[27,1,8,512]{3,2,1,0:T(8,128)}, u32[]{:S(2)}, u32[]{:S(2)}) collective-permute-start(f32[27,1,8,512]{3,2,1,0:T(8,128)} %get-tuple-element.110), channel_id=1, source_target_pairs={{0,8},{8,16},{16,24},{24,0},{1,9},{9,17},{17,25},{25,1},{2,10},{10... | collective-permute-start | bytes 1327112 | tf_op jit(solution)/shard_map/ppermute | solution.py:48
  18.3 28.2 %collective-permute-start.1 = (f32[27,1,8,512]{3,2,1,0:T(8,128)}, f32[27,1,8,512]{3,2,1,0:T(8,128)}, u32[]{:S(2)}, u32[]{:S(2)}) collective-permute-start(f32[27,1,8,512]{3,2,1,0:T(8,128)} %get-tuple-element.111), channel_id=1, source_target_pairs={{8,0},{16,8},{24,16},{0,24},{9,1},{17,9},{25,17},{1,25},{10,2},{18... | collective-permute-start | bytes 1327112 | tf_op jit(solution)/shard_map/ppermute | solution.py:51
  22.1 24.4 %copy-start.9 = (f32[1,8,8,512]{3,2,1,0:T(8,128)S(1)}, f32[1,8,8,512]{3,2,1,0:T(8,128)}, u32[]{:S(2)}) copy-start(f32[1,8,8,512]{3,2,1,0:T(8,128)} %copy-done.8) | copy-start | bytes 393220
  33.6 17.9 %collective-permute-start.7 = (f32[26,10,1,512]{3,2,1,0:T(1,128)S(1)}, f32[26,10,1,512]{3,2,1,0:T(1,128)S(1)}, u32[]{:S(2)}, u32[]{:S(2)}) collective-permute-start(f32[26,10,1,512]{3,2,1,0:T(1,128)S(1)} %get-tuple-element.108), channel_id=1, source_target_pairs={{0,1},{1,2},{2,3},{3,4},{4,5},{5,6},{6,7},{7,0},{8,9},{9,10},{10,1... | collective-permute-start | bytes 1597448 | tf_op jit(solution)/shard_map/ppermute | solution.py:48
  33.7 17.8 %collective-permute-start.6 = (f32[26,10,1,512]{3,2,1,0:T(1,128)S(1)}, f32[26,10,1,512]{3,2,1,0:T(1,128)S(1)}, u32[]{:S(2)}, u32[]{:S(2)}) collective-permute-start(f32[26,10,1,512]{3,2,1,0:T(1,128)S(1)} %get-tuple-element.109), channel_id=1, source_target_pairs={{1,0},{2,1},{3,2},{4,3},{5,4},{6,5},{7,6},{0,7},{9,8},{10,9},{11,1... | collective-permute-start | bytes 1597448 | tf_op jit(solution)/shard_map/ppermute | solution.py:51
  36.3 15.2 %copy-start.3 = (f32[26,8,8,512]{3,2,1,0:T(8,128)S(1)}, f32[26,8,8,512]{3,2,1,0:T(8,128)}, u32[]{:S(2)}) copy-start(f32[26,8,8,512]{3,2,1,0:T(8,128)} %copy-done.2) | copy-start | bytes 10223620
  48.8 15.8 %collective-permute-start.2 = (f32[27,10,1,512]{3,2,1,0:T(1,128)S(1)}, f32[27,10,1,512]{3,2,1,0:T(1,128)S(1)}, u32[]{:S(2)}, u32[]{:S(2)}) collective-permute-start(f32[27,10,1,512]{3,2,1,0:T(1,128)S(1)} %get-tuple-element.102), channel_id=1, source_target_pairs={{0,1},{1,2},{2,3},{3,4},{4,5},{5,6},{6,7},{7,0},{8,9},{9,10},{10,1... | collective-permute-start | bytes 1658888 | tf_op jit(solution)/shard_map/ppermute | solution.py:48
  48.8 15.7 %collective-permute-start.3 = (f32[27,10,1,512]{3,2,1,0:T(1,128)S(1)}, f32[27,10,1,512]{3,2,1,0:T(1,128)S(1)}, u32[]{:S(2)}, u32[]{:S(2)}) collective-permute-start(f32[27,10,1,512]{3,2,1,0:T(1,128)S(1)} %get-tuple-element.103), channel_id=1, source_target_pairs={{1,0},{2,1},{3,2},{4,3},{5,4},{6,5},{7,6},{0,7},{9,8},{10,9},{11,1... | collective-permute-start | bytes 1658888 | tf_op jit(solution)/shard_map/ppermute | solution.py:51
  64.5 21.9 %copy-start.10 = (f32[19,8,8,512]{3,2,1,0:T(8,128)S(1)}, f32[19,8,8,512]{3,2,1,0:T(8,128)}, u32[]{:S(2)}) copy-start(f32[19,8,8,512]{3,2,1,0:T(8,128)} %param.20) | copy-start | bytes 7471108
  64.5 21.9 %copy-start.19 = (f32[7,8,8,512]{3,2,1,0:T(8,128)S(1)}, f32[7,8,8,512]{3,2,1,0:T(8,128)}, u32[]{:S(2)}) copy-start(f32[7,8,8,512]{3,2,1,0:T(8,128)} %param.21) | copy-start | bytes 2752516
  94.5 9.7 %copy-start.5 = (f32[19,8,8,512]{3,2,1,0:T(8,128)}, f32[19,8,8,512]{3,2,1,0:T(8,128)S(1)}, u32[]{:S(2)}) copy-start(f32[19,8,8,512]{3,2,1,0:T(8,128)S(1)} %get-tuple-element.87) | copy-start | bytes 7471108
  103.6 8.3 %copy-start.13 = (f32[8,8,512]{2,1,0:T(8,128)}, f32[8,8,512]{2,1,0:T(8,128)S(1)}, u32[]{:S(2)}) copy-start(f32[8,8,512]{2,1,0:T(8,128)S(1)} %get-tuple-element.41) | copy-start | bytes 393220
  104.3 7.6 %copy-start.30 = (f32[8,8,512]{2,1,0:T(8,128)}, f32[8,8,512]{2,1,0:T(8,128)S(1)}, u32[]{:S(2)}) copy-start(f32[8,8,512]{2,1,0:T(8,128)S(1)} %get-tuple-element.44) | copy-start | bytes 393220
  111.9 46.2 %copy-start.12 = (f32[8,8,512]{2,1,0:T(8,128)S(1)}, f32[8,8,512]{2,1,0:T(8,128)}, u32[]{:S(2)}) copy-start(f32[8,8,512]{2,1,0:T(8,128)} %copy-done.11) | copy-start | bytes 393220
  111.9 46.2 %copy-start.17 = (f32[8,8,512]{2,1,0:T(8,128)S(1)}, f32[8,8,512]{2,1,0:T(8,128)}, u32[]{:S(2)}) copy-start(f32[8,8,512]{2,1,0:T(8,128)} %copy-done.15) | copy-start | bytes 393220
  112.6 45.4 %copy-start.14 = (f32[8,8,512]{2,1,0:T(8,128)S(1)}, f32[8,8,512]{2,1,0:T(8,128)}, u32[]{:S(2)}) copy-start(f32[8,8,512]{2,1,0:T(8,128)} %copy-done.13) | copy-start | bytes 393220
  112.6 47.6 %copy-start.23 = (f32[8,8,512]{2,1,0:T(8,128)S(1)}, f32[8,8,512]{2,1,0:T(8,128)}, u32[]{:S(2)}) copy-start(f32[8,8,512]{2,1,0:T(8,128)} %copy-done.22) | copy-start | bytes 393220
  117.7 43.7 %copy-start.21 = (f32[8,8,512]{2,1,0:T(8,128)S(1)}, f32[8,8,512]{2,1,0:T(8,128)}, u32[]{:S(2)}) copy-start(f32[8,8,512]{2,1,0:T(8,128)} %copy-done.20) | copy-start | bytes 393220
  117.7 43.7 %copy-start.27 = (f32[8,8,512]{2,1,0:T(8,128)S(1)}, f32[8,8,512]{2,1,0:T(8,128)}, u32[]{:S(2)}) copy-start(f32[8,8,512]{2,1,0:T(8,128)} %copy-done.26) | copy-start | bytes 393220
  (50 other events, 152.5 us)
where the time goes:
time: 167 us; the launch traced here: 164 us
  other arithmetic  80.1 us (48%)
  blocking collectives  39 us (23%)
  waiting for transfers between devices  17.2 us (10%)
  starting transfers between devices  14.3 us (9%)
  matrix products  6.66 us (4%)
  local copies, waits for them, and re-layouts  4.91 us (3%)
  between operations  1.99 us (1%)
    concatenate x3, other arithmetic, with_halo(): block = jnp.concatenate([low, block, high], axis=dim)  39.2 us
    psum x1, blocking collectives, on_device(): totals = lax.psum(shares, ('gx', 'gy'))  39 us
    ppermute x4, waiting for transfers between devices, with_halo(): lax.ppermute(lax.slice_in_dim(block, 0, width, axis=dim), axis, backward)  15.1 us
    unnamed x35, other arithmetic  14.2 us
    ppermute x4, starting transfers between devices, with_halo(): lax.ppermute(lax.slice_in_dim(block, 0, width, axis=dim), axis, backward)  11.2 us
    dot_general x1, matrix products, on_device(): jnp.tensordot(table, dcell * profile, axes=3, precision=lax.Precision.HIG...  5.09 us
    unnamed x151, local copies, waits for them, and re-layouts  3.65 us
  transfers between devices with their start and end apart: 8, of which 3 were waited for; matrix products, arithmetic and copies ran while one was open for 17% of the time, Pallas kernels for 0%

commit v1 on v0

v1 whole, which is shorter than its diff:
```python
import functools
import math

import jax
import jax.numpy as jnp
from jax import lax
from jax.experimental import pallas as pl
from jax.experimental.pallas import tpu as pltpu
from jax.sharding import PartitionSpec as P

LATTICE = [
    (0, 0, 0),
    (1, 0, 0),
    (-1, 0, 0),
    (0, 1, 0),
    (0, -1, 0),
    (0, 0, 1),
    (0, 0, -1),
    (1, 1, 0),
    (-1, -1, 0),
    (1, -1, 0),
    (-1, 1, 0),
    (1, 0, 1),
    (-1, 0, -1),
    (1, 0, -1),
    (-1, 0, 1),
    (0, 1, 1),
    (0, -1, -1),
    (0, 1, -1),
    (0, -1, 1),
]
NF, NG = 19, 7
NP = NF + NG
FIRST = [1, 3, 5, 7, 9, 11, 13, 15, 17]
W0, W1, W2 = 1.0 / 3.0, 1.0 / 18.0, 1.0 / 36.0
V0, V1 = 0.25, 0.125
PLUS = 0.625
MINUS = 0.5 / 1.125
TAU_PLUS = 0.8
COUPLE = 2.0
SOURCE = 2.0

UP = [3, 7, 10, 15, 17, NF + 3]
DOWN = [4, 8, 9, 16, 18, NF + 4]
RIGHT = [1, 7, 9, 11, 13, NF + 1]
LEFT = [2, 8, 10, 12, 14, NF + 2]
SLOTS = 13
MASK = 12


def weight(i):
    return W1 if i <= 6 else W2


def gather_strength(table, magnet):
    parts = [
        jnp.take_along_axis(table, magnet[:, z : z + 128], axis=1, mode="promise_in_bounds")
        for z in range(0, magnet.shape[1], 128)
    ]
    return jnp.concatenate(parts, axis=1)


def lane_table(strengths_ref):
    row = strengths_ref[...]
    rest = 128 - row.shape[1]
    if rest:
        row = jnp.concatenate([row, jnp.zeros((1, rest), jnp.float32)], axis=1)
    return jnp.broadcast_to(row, (8, 128))


def vector_sums(pair):
    x = pair[1] + pair[7] + pair[9] + pair[11] + pair[13]
    y = pair[3] + pair[7] - pair[9] + pair[15] + pair[17]
    z = pair[5] + pair[11] - pair[13] + pair[15] - pair[17]
    return x, y, z


def along(i, vx, vy, vz):
    out = None
    for c, v in zip(LATTICE[i], (vx, vy, vz)):
        if c:
            if out is None:
                out = v if c > 0 else -v
            else:
                out = out + v if c > 0 else out - v
    return out


def collide_kernel(
    planes,
    flow_ref,
    field_ref,
    adjf_ref,
    adjg_ref,
    profile_ref,
    strengths_ref,
    wall_ref,
    magnet_ref,
    post_ref,
    first_ref,
    second_ref,
    right_ref,
    left_ref,
):
    step = pl.program_id(0)
    steps = pl.num_programs(0)
    odd = lax.rem(lax.axis_index("gy"), 2)
    table = lane_table(strengths_ref)
    last = flow_ref.shape[2] - 1

    for p in range(planes):
        fluid = 1.0 - wall_ref[p].astype(jnp.float32)
        bcell = gather_strength(table, magnet_ref[p]) * profile_ref[p]
        f = [flow_ref[i, p] for i in range(NF)]
        g = [field_ref[k, p] for k in range(NG)]
        even = {i: f[i] + f[i + 1] for i in FIRST}
        diff = {i: f[i] - f[i + 1] for i in FIRST}
        rho = f[0] + (1.0 - fluid)
        for i in FIRST:
            rho = rho + even[i]
        momx, momy, momz = vector_sums(diff)
        inv = 1.0 / rho
        ux, uy, uz = momx * inv, momy * inv, momz * inv
        bval = g[0] + g[1] + g[2] + g[3] + g[4] + g[5] + g[6]
        current = (g[3] - g[4]) - bval * uy
        shear = (even[7] - even[9]) - momx * uy
        force = (COUPLE * bcell) * current
        vx = ux + TAU_PLUS * force * inv
        base = 1.0 - 1.5 * (vx * vx + uy * uy + uz * uz)
        post_ref[0, p] = f[0] - 2.0 * PLUS * (f[0] - (W0 * rho) * base)
        rho1, rho2 = W1 * rho, W2 * rho
        for i in FIRST:
            wr = rho1 if i <= 6 else rho2
            a = along(i, vx, uy, uz)
            ne = even[i] - (2.0 * wr) * (base + 4.5 * a * a)
            no = diff[i] - (6.0 * wr) * a
            ne = PLUS * ne
            no = MINUS * no
            post_ref[i, p] = f[i] - ne - no
            post_ref[i + 1, p] = f[i + 1] - ne + no
        common = bval + (SOURCE * bcell) * shear
        slope = 4.0 * bval
        post_ref[NF, p] = V0 * common
        for k, u in ((1, ux), (3, uy), (5, uz)):
            su = slope * u
            post_ref[NF + k, p] = V1 * (common + su)
            post_ref[NF + k + 1, p] = V1 * (common - su)

        x = step * planes + p
        here = pl.ds(x, 1)

        def adj_row(i, row):
            return adjf_ref[i, p, pl.ds(row, 1), :]

        for out, side in ((first_ref, odd), (second_ref, 1 - odd)):
            row = (1 - side) * last
            for s in range(6):
                up, down = UP[s], DOWN[s]
                out[s, here, :] = post_ref[up + side * (down - up), p, pl.ds(row, 1), :]
                if up < NF:
                    line = adjf_ref[down + side * (up - down), p, pl.ds(row, 1), :]
                else:
                    line = adjg_ref[down - NF + side * (up - down), p, pl.ds(row, 1), :]
                out[6 + s, here, :] = line
            out[MASK, here, :] = 1.0 - wall_ref[p, pl.ds(row, 1), :].astype(jnp.float32)

    def pack_x(out, p, posts, adjs):
        for s in range(6):
            out[s] = post_ref[posts[s], p]
            j = adjs[s]
            out[6 + s] = adjf_ref[j, p] if j < NF else adjg_ref[j - NF, p]
        out[MASK] = 1.0 - wall_ref[p].astype(jnp.float32)

    @pl.when(step == 0)
    def _():
        pack_x(left_ref, 0, LEFT, RIGHT)

    @pl.when(step == steps - 1)
    def _():
        pack_x(right_ref, planes - 1, RIGHT, LEFT)


def collide_call(flow, field, adjf, adjg, profile, strengths, wall, magnet, planes=2):
    sx, sy, sz = profile.shape
    grid = sx // planes

    def stack(n):
        return pl.BlockSpec((n, planes, sy, sz), lambda x: (0, x, 0, 0))

    one = pl.BlockSpec((planes, sy, sz), lambda x: (x, 0, 0))

    def whole(*shape):
        return pl.BlockSpec(shape, lambda x: (0,) * len(shape))

    rows = jax.ShapeDtypeStruct((SLOTS, sx, sz), jnp.float32)
    faces = jax.ShapeDtypeStruct((SLOTS, sy, sz), jnp.float32)
    return pl.pallas_call(
        functools.partial(collide_kernel, planes),
        grid=(grid,),
        in_specs=[
            stack(NF),
            stack(NG),
            stack(NF),
            stack(NG),
            one,
            whole(*strengths.shape),
            one,
            one,
        ],
        out_specs=[
            stack(NP),
            whole(*rows.shape),
            whole(*rows.shape),
            whole(*faces.shape),
            whole(*faces.shape),
        ],
        out_shape=[
            jax.ShapeDtypeStruct((NP, sx, sy, sz), jnp.float32),
            rows,
            rows,
            faces,
            faces,
        ],
        compiler_params=pltpu.CompilerParams(vmem_limit_bytes=40 << 20),
        name="collide",
    )(flow, field, adjf, adjg, profile, strengths, wall, magnet)


CORNER_RIGHT = ((0, 7, 0, 8), (1, 9, 1, 10))
CORNER_LEFT = ((0, 10, 0, 9), (1, 8, 1, 7))


def corner_slots(side, post, adj):
    posts, adjs = (UP, DOWN) if side == 0 else (DOWN, UP)
    return posts.index(post), 6 + adjs.index(adj), MASK


def corner_kernel(first_ref, second_ref, right_ref, left_ref):
    odd = lax.rem(lax.axis_index("gy"), 2) == 1
    sx = first_ref.shape[1]

    def row(side, slot, x):
        a, b = first_ref[slot, x : x + 1, :], second_ref[slot, x : x + 1, :]
        return jnp.where(odd, a, b) if side == 0 else jnp.where(odd, b, a)

    for out, table, x in ((right_ref, CORNER_RIGHT, sx - 1), (left_ref, CORNER_LEFT, 0)):
        out[...] = jnp.zeros_like(out)
        for side, post, _, adj in table:
            for n, slot in enumerate(corner_slots(side, post, adj)):
                out[2 * n + side : 2 * n + side + 1, :] = row(side, slot, x)


def corner_call(first, second):
    sz = first.shape[2]
    out = jax.ShapeDtypeStruct((8, sz), jnp.float32)
    return pl.pallas_call(corner_kernel, out_shape=[out, out], name="corners")(first, second)


def plane_step(
    x_index, post, post_row, adj, adj_row, mask, mask_row, fluid, bcell, profile, magnet,
    near_ref, new_ref, out_ref, sums_ref, count,
):
    sy, sz = fluid.shape
    yi = lax.broadcasted_iota(jnp.int32, (sy, sz), 0)
    zi = lax.broadcasted_iota(jnp.int32, (sy, sz), 1)
    top, bottom = yi == sy - 1, yi == 0
    zlast, zfirst = zi == sz - 1, zi == 0

    def shift(value, row, dy, dz):
        if dy == -1:
            value = jnp.where(bottom, row(), pltpu.roll(value, 1, 0))
        elif dy == 1:
            value = jnp.where(top, row(), pltpu.roll(value, sy - 1, 0))
        if dz == -1:
            value = pltpu.roll(value, 1, 1)
        elif dz == 1:
            value = pltpu.roll(value, sz - 1, 1)
        return value

    def moved(get, get_row, i, sign):
        dx, dy, dz = (sign * c for c in LATTICE[i if i < NF else i - NF])
        return shift(get(i, dx), lambda: get_row(i, dx, dy), dy, dz)

    def near_of(i, sign):
        dx, dy, dz = (sign * c for c in LATTICE[i])
        value = shift(mask(dx), lambda: mask_row(dx, dy), dy, dz)
        if dz == -1:
            value = jnp.where(zfirst, 0.0, value)
        elif dz == 1:
            value = jnp.where(zlast, 0.0, value)
        return value

    for n, i in enumerate(FIRST):
        near_ref[2 * n] = near_of(i, -1)
        near_ref[2 * n + 1] = near_of(i, 1)

    def near(n):
        return near_ref[2 * n] > 0.5, near_ref[2 * n + 1] > 0.5

    def pull(i, n):
        minus, plus = near(n)
        a = fluid * jnp.where(minus, moved(post, post_row, i, -1), post(i + 1, 0))
        b = fluid * jnp.where(plus, moved(post, post_row, i + 1, -1), post(i, 0))
        new_ref[i, x_index] = a
        new_ref[i + 1, x_index] = b
        return a, b

    f0 = fluid * post(0, 0)
    new_ref[0, x_index] = f0
    rho = f0 + (1.0 - fluid)
    momx = momy = momz = shear0 = 0.0
    for n, i in enumerate(FIRST):
        a, b = pull(i, n)
        s, d = a + b, a - b
        rho = rho + s
        cx, cy, cz = LATTICE[i]
        if cx:
            momx = momx + d
        if cy:
            momy = momy + d if cy > 0 else momy - d
        if cz:
            momz = momz + d if cz > 0 else momz - d
        if cx and cy:
            shear0 = shear0 + s if cx * cy > 0 else shear0 - s
    g0 = fluid * post(NF, 0)
    new_ref[NF, x_index] = g0
    bval = g0
    gy = None
    for n, k in enumerate((1, 3, 5)):
        a, b = pull(NF + k, n)
        bval = bval + (a + b)
        if k == 3:
            gy = a - b
    inv = 1.0 / rho
    ux, uy, uz = momx * inv, momy * inv, momz * inv
    current = gy - bval * uy
    shear = shear0 - momx * uy
    force = (COUPLE * bcell) * current
    vx = ux + TAU_PLUS * force * inv

    def push(i, n):
        minus, plus = near(n)
        a = fluid * jnp.where(plus, moved(adj, adj_row, i, 1), adj(i + 1, 0))
        b = fluid * jnp.where(minus, moved(adj, adj_row, i + 1, 1), adj(i, 0))
        return a, b

    l0 = fluid * adj(0, 0)
    out_ref[0, x_index] = (1.0 - 2.0 * PLUS) * l0
    total = (2.0 * PLUS * W0) * l0
    m1 = [0.0, 0.0, 0.0]
    m2 = {}
    for n, i in enumerate(FIRST):
        a, b = push(i, n)
        s, d = a + b, a - b
        de = (0.5 - PLUS) * s
        do = (0.5 - MINUS) * d
        out_ref[i, x_index] = de + do
        out_ref[i + 1, x_index] = de - do
        w = weight(i)
        s = (2.0 * PLUS * w) * s
        d = (2.0 * MINUS * w) * d
        total = total + s
        c = LATTICE[i]
        for axis in range(3):
            if c[axis]:
                m1[axis] = m1[axis] + d if c[axis] > 0 else m1[axis] - d
            for other in range(axis, 3):
                sign = c[axis] * c[other]
                if sign:
                    old = m2.get((axis, other))
                    if old is None:
                        m2[axis, other] = s if sign > 0 else -s
                    else:
                        m2[axis, other] = old + s if sign > 0 else old - s
    h0 = fluid * adj(NF, 0)
    hsum = V0 * h0
    h1 = []
    hs = None
    for n, k in enumerate((1, 3, 5)):
        a, b = push(NF + k, n)
        hs = a + b if hs is None else hs + (a + b)
        h1.append(V1 * (a - b))
    hsum = hsum + V1 * hs

    base = 1.0 - 1.5 * (vx * vx + uy * uy + uz * uz)
    tx = m2[0, 0] * vx + m2[0, 1] * uy + m2[0, 2] * uz
    ty = m2[0, 1] * vx + m2[1, 1] * uy + m2[1, 2] * uz
    tz = m2[0, 2] * vx + m2[1, 2] * uy + m2[2, 2] * uz
    rhobar = (
        total * base
        + 4.5 * (vx * tx + uy * ty + uz * tz)
        + 3.0 * (m1[0] * vx + m1[1] * uy + m1[2] * uz)
    )
    total3 = 3.0 * total
    vxbar = rho * (9.0 * tx + 3.0 * m1[0] - total3 * vx)
    uybar = rho * (9.0 * ty + 3.0 * m1[1] - total3 * uy)
    uzbar = rho * (9.0 * tz + 3.0 * m1[2] - total3 * uz)
    slope = 4.0 * bval
    forcebar = (TAU_PLUS * vxbar) * inv
    rhobar = rhobar - forcebar * force * inv
    currentbar = (COUPLE * bcell) * forcebar
    shearbar = (SOURCE * bcell) * hsum
    dcell = COUPLE * current * forcebar + SOURCE * shear * hsum
    uxbar = vxbar + slope * h1[0]
    uybar = uybar + slope * h1[1] - bval * currentbar - momx * shearbar
    uzbar = uzbar + slope * h1[2]
    bbar = hsum + 4.0 * (h1[0] * ux + h1[1] * uy + h1[2] * uz) - uy * currentbar
    mxbar = uxbar * inv - uy * shearbar
    mybar = uybar * inv
    mzbar = uzbar * inv
    rhobar = rhobar - (ux * uxbar + uy * uybar + uz * uzbar) * inv

    out_ref[0, x_index] = out_ref[0, x_index] + rhobar
    for i in FIRST:
        cm = along(i, mxbar, mybar, mzbar)
        cx, cy, _ = LATTICE[i]
        common = rhobar
        if cx and cy:
            common = rhobar + shearbar if cx * cy > 0 else rhobar - shearbar
        out_ref[i, x_index] = out_ref[i, x_index] + (common + cm)
        out_ref[i + 1, x_index] = out_ref[i + 1, x_index] + (common - cm)
    for k in range(NG):
        value = bbar
        if k == 3:
            value = bbar + currentbar
        elif k == 4:
            value = bbar - currentbar
        out_ref[NF + k, x_index] = value

    share = dcell * profile
    for m in range(count):
        hit = jnp.where(magnet == m, share, 0.0)
        part = hit[:, 0:128]
        for z in range(128, sz, 128):
            part = part + hit[:, z : z + 128]
        sums_ref[m] = sums_ref[m] + part


def edges():
    here = lax.axis_index("gy")
    keep_low = jnp.where(here == 0, 0.0, 1.0)
    keep_high = jnp.where(here == lax.axis_size("gy") - 1, 0.0, 1.0)
    return keep_low, keep_high


def halo_slot(kind, i, dy):
    names = (UP, DOWN) if (dy == -1) == (kind == 0) else (DOWN, UP)
    return names[0].index(i) + 6 * kind


def face_slot(kind, i, dx):
    names = RIGHT if (dx == -1) == (kind == 0) else LEFT
    return names.index(i) + 6 * kind


def start_all(copies):
    for c in copies:
        c.start()


def load_halo(first_ref, second_ref, halo_ref, sem):
    odd = lax.rem(lax.axis_index("gy"), 2)
    return [
        pltpu.make_async_copy(first_ref, halo_ref.at[1 - odd], sem.at[0]),
        pltpu.make_async_copy(second_ref, halo_ref.at[odd], sem.at[1]),
    ]


def mask_halo(halo_ref):
    keep_low, keep_high = edges()
    halo_ref[0, MASK] = halo_ref[0, MASK] * keep_low
    halo_ref[1, MASK] = halo_ref[1, MASK] * keep_high


def inner_kernel(
    post_ref, adjf_ref, adjg_ref, first_ref, second_ref, profile_ref, strengths_ref, wall_ref,
    magnet_ref,
    newf_ref, newg_ref, outf_ref, outg_ref, sums_ref,
    post_v, adj_v, new_v, out_v, halo_v, near_v,
    post_sem, adjf_sem, adjg_sem, halo_sem, newf_sem, newg_sem, outf_sem, outg_sem,
):
    sx = post_v.shape[1]
    count = sums_ref.shape[0]

    def loads(x):
        return [
            pltpu.make_async_copy(post_ref.at[:, x], post_v.at[:, x], post_sem.at[x]),
            pltpu.make_async_copy(adjf_ref.at[:, x], adj_v.at[pl.ds(0, NF), x], adjf_sem.at[x]),
            pltpu.make_async_copy(adjg_ref.at[:, x], adj_v.at[pl.ds(NF, NG), x], adjg_sem.at[x]),
        ]

    def stores(x):
        return [
            pltpu.make_async_copy(new_v.at[pl.ds(0, NF), x], newf_ref.at[:, x], newf_sem.at[x]),
            pltpu.make_async_copy(new_v.at[pl.ds(NF, NG), x], newg_ref.at[:, x], newg_sem.at[x]),
            pltpu.make_async_copy(out_v.at[pl.ds(0, NF), x], outf_ref.at[:, x], outf_sem.at[x]),
            pltpu.make_async_copy(out_v.at[pl.ds(NF, NG), x], outg_ref.at[:, x], outg_sem.at[x]),
        ]

    def finish(copies):
        for c in copies:
            c.wait()

    halo = load_halo(first_ref, second_ref, halo_v, halo_sem)
    start_all(halo)
    for x in range(sx):
        start_all(loads(x))
    sums_ref[...] = jnp.zeros_like(sums_ref)
    table = lane_table(strengths_ref)
    finish(halo)
    mask_halo(halo_v)
    finish(loads(0))
    finish(loads(1))

    def body(x, carry):
        finish(loads(x + 1))

        def side(dy):
            return 0 if dy == -1 else 1

        def row_of(slot, dx, dy):
            return halo_v[side(dy), slot, pl.ds(x + dx, 1), :]

        def mask(dx):
            return 1.0 - wall_ref[x + dx].astype(jnp.float32)

        magnet = magnet_ref[x]
        profile = profile_ref[x]
        plane_step(
            x,
            lambda i, dx: post_v[i, x + dx],
            lambda i, dx, dy: row_of(halo_slot(0, i, dy), dx, dy),
            lambda i, dx: adj_v[i, x + dx],
            lambda i, dx, dy: row_of(halo_slot(1, i, dy), dx, dy),
            mask,
            lambda dx, dy: row_of(MASK, dx, dy),
            mask(0),
            gather_strength(table, magnet) * profile,
            profile,
            magnet,
            near_v,
            new_v,
            out_v,
            sums_ref,
            count,
        )
        start_all(stores(x))
        return carry

    lax.fori_loop(1, sx - 1, body, 0)
    for x in range(1, sx - 1):
        finish(stores(x))


ANY = pl.BlockSpec(memory_space=pl.ANY)
VMEM = pl.BlockSpec(memory_space=pltpu.VMEM)


def inner_call(post, adjf, adjg, first, second, profile, strengths, wall, magnet):
    sx, sy, sz = profile.shape
    count = strengths.shape[1]
    full = pltpu.VMEM((NP, sx, sy, sz), jnp.float32)
    dma = pltpu.SemaphoreType.DMA
    return pl.pallas_call(
        inner_kernel,
        in_specs=[ANY, ANY, ANY, ANY, ANY, VMEM, VMEM, VMEM, VMEM],
        out_specs=[ANY, ANY, ANY, ANY, VMEM],
        out_shape=[
            jax.ShapeDtypeStruct(adjf.shape, jnp.float32),
            jax.ShapeDtypeStruct(adjg.shape, jnp.float32),
            jax.ShapeDtypeStruct(adjf.shape, jnp.float32),
            jax.ShapeDtypeStruct(adjg.shape, jnp.float32),
            jax.ShapeDtypeStruct((count, 8, 128), jnp.float32),
        ],
        scratch_shapes=[
            full,
            full,
            full,
            full,
            pltpu.VMEM((2, SLOTS, sx, sz), jnp.float32),
            pltpu.VMEM((18, sy, sz), jnp.float32),
            dma((sx,)),
            dma((sx,)),
            dma((sx,)),
            dma((2,)),
            dma((sx,)),
            dma((sx,)),
            dma((sx,)),
            dma((sx,)),
        ],
        compiler_params=pltpu.CompilerParams(vmem_limit_bytes=40 << 20),
        cost_estimate=pl.CostEstimate(
            flops=700 * sx * sy * sz, bytes_accessed=16 * NP * sx * sy * sz, transcendentals=0
        ),
        name="inner",
    )(post, adjf, adjg, first, second, profile, strengths, wall, magnet)


def outer_kernel(
    post_ref, adjf_ref, adjg_ref, first_ref, second_ref, fromleft_ref, fromright_ref,
    cornerleft_ref, cornerright_ref, profile_ref, strengths_ref, wall_ref, magnet_ref,
    partial_ref, newf_in, newg_in, outf_in, outg_in,
    newf_ref, newg_ref, outf_ref, outg_ref, share_ref,
    post_v, adj_v, new_v, out_v, halo_v, near_v, sums_v,
    post_sem, adjf_sem, adjg_sem, halo_sem, store_sem,
):
    del newf_in, newg_in, outf_in, outg_in
    sx = wall_ref.shape[0]
    count = sums_v.shape[0]
    from_planes = (0, 1, sx - 2, sx - 1)
    loads = []
    for n, x in enumerate(from_planes):
        loads += [
            pltpu.make_async_copy(post_ref.at[:, x], post_v.at[:, n], post_sem.at[n]),
            pltpu.make_async_copy(adjf_ref.at[:, x], adj_v.at[pl.ds(0, NF), n], adjf_sem.at[n]),
            pltpu.make_async_copy(adjg_ref.at[:, x], adj_v.at[pl.ds(NF, NG), n], adjg_sem.at[n]),
        ]
    halo = load_halo(first_ref, second_ref, halo_v, halo_sem)
    start_all(halo)
    start_all(loads)
    sums_v[...] = partial_ref[...]
    table = lane_table(strengths_ref)
    keep_low, keep_high = edges()
    for c in halo:
        c.wait()
    mask_halo(halo_v)
    stores = []
    for n, (x, away, here, near_plane) in enumerate(((0, -1, 0, 1), (sx - 1, 1, 3, 2))):
        for c in loads[6 * n : 6 * n + 6]:
            c.wait()
        face_ref, corner_ref = (
            (fromleft_ref, cornerleft_ref) if away == -1 else (fromright_ref, cornerright_ref)
        )

        def get(kind, i, dx, held, here=here, near_plane=near_plane, away=away, face_ref=face_ref):
            if dx == 0:
                return held[i, here]
            if dx == away:
                return face_ref[face_slot(kind, i, dx)]
            return held[i, near_plane]

        def row(kind, i, dx, dy, x=x, away=away, corner_ref=corner_ref):
            side = 0 if dy == -1 else 1
            if dx == away:
                line = corner_ref[2 * kind + side : 2 * kind + side + 1, :]
                if kind == 2:
                    line = line * (keep_low if side == 0 else keep_high)
                return line
            slot = MASK if kind == 2 else halo_slot(kind, i, dy)
            return halo_v[side, slot, x + dx : x + dx + 1, :]

        def mask(dx, x=x, away=away, face_ref=face_ref):
            if dx == away:
                return face_ref[MASK]
            return 1.0 - wall_ref[x + dx].astype(jnp.float32)

        magnet = magnet_ref[x]
        profile = profile_ref[x]
        plane_step(
            n,
            lambda i, dx, get=get: get(0, i, dx, post_v),
            lambda i, dx, dy, row=row: row(0, i, dx, dy),
            lambda i, dx, get=get: get(1, i, dx, adj_v),
            lambda i, dx, dy, row=row: row(1, i, dx, dy),
            mask,
            lambda dx, dy, row=row: row(2, 0, dx, dy),
            mask(0),
            gather_strength(table, magnet) * profile,
            profile,
            magnet,
            near_v,
            new_v,
            out_v,
            sums_v,
            count,
        )
        these = [
            pltpu.make_async_copy(new_v.at[pl.ds(0, NF), n], newf_ref.at[:, x], store_sem.at[n, 0]),
            pltpu.make_async_copy(new_v.at[pl.ds(NF, NG), n], newg_ref.at[:, x], store_sem.at[n, 1]),
            pltpu.make_async_copy(out_v.at[pl.ds(0, NF), n], outf_ref.at[:, x], store_sem.at[n, 2]),
            pltpu.make_async_copy(out_v.at[pl.ds(NF, NG), n], outg_ref.at[:, x], store_sem.at[n, 3]),
        ]
        start_all(these)
        stores += these
    rows = jnp.concatenate(
        [jnp.sum(sums_v[m], axis=0, keepdims=True) for m in range(count)], axis=0
    )
    share_ref[...] = lax.dot_general(
        jnp.ones((8, 128), jnp.float32),
        rows,
        (((1,), (1,)), ((), ())),
        precision=lax.Precision.HIGHEST,
        preferred_element_type=jnp.float32,
    )
    for c in stores:
        c.wait()


def outer_call(
    post, adjf, adjg, first, second, fromleft, fromright, cornerleft, cornerright, profile,
    strengths, wall, magnet, partial, newf, newg, outf, outg,
):
    sx, sy, sz = profile.shape
    count = strengths.shape[1]
    dma = pltpu.SemaphoreType.DMA
    return pl.pallas_call(
        outer_kernel,
        in_specs=[ANY] * 5 + [VMEM] * 9 + [ANY] * 4,
        out_specs=[ANY] * 4 + [VMEM],
        out_shape=[
            jax.ShapeDtypeStruct(adjf.shape, jnp.float32),
            jax.ShapeDtypeStruct(adjg.shape, jnp.float32),
            jax.ShapeDtypeStruct(adjf.shape, jnp.float32),
            jax.ShapeDtypeStruct(adjg.shape, jnp.float32),
            jax.ShapeDtypeStruct((8, count), jnp.float32),
        ],
        input_output_aliases={14: 0, 15: 1, 16: 2, 17: 3},
        scratch_shapes=[
            pltpu.VMEM((NP, 4, sy, sz), jnp.float32),
            pltpu.VMEM((NP, 4, sy, sz), jnp.float32),
            pltpu.VMEM((NP, 2, sy, sz), jnp.float32),
            pltpu.VMEM((NP, 2, sy, sz), jnp.float32),
            pltpu.VMEM((2, SLOTS, sx, sz), jnp.float32),
            pltpu.VMEM((18, sy, sz), jnp.float32),
            pltpu.VMEM((count, 8, 128), jnp.float32),
            dma((4,)),
            dma((4,)),
            dma((4,)),
            dma((2,)),
            dma((2, 4)),
        ],
        compiler_params=pltpu.CompilerParams(vmem_limit_bytes=40 << 20),
        name="outer",
    )(
        post, adjf, adjg, first, second, fromleft, fromright, cornerleft, cornerright, profile,
        strengths, wall, magnet, partial, newf, newg, outf, outg,
    )


def ring(count, step):
    return [(i, (i + step) % count) for i in range(count)]


def butterfly(value):
    for axis in ("gy", "gx"):
        count = lax.axis_size(axis)
        step = 1
        while step < count:
            value = value + lax.ppermute(value, axis, [(i, i ^ step) for i in range(count)])
            step *= 2
    return value


def on_device(flow, field, adj_flow_in, adj_field_in, profile, strengths, wall, magnet):
    across, around = lax.axis_size("gy"), lax.axis_size("gx")
    count = strengths.shape[0]
    table = strengths.reshape(1, count)
    post, mine1, mine2, right, left = collide_call(
        flow, field, adj_flow_in, adj_field_in, profile, table, wall, magnet
    )
    inside = [(i, i ^ 1) for i in range(across)]
    between = [(i, (((i + 1) ^ 1) - 1) % across) for i in range(across)]
    second = lax.ppermute(mine2, "gy", between)
    first = lax.ppermute(mine1, "gy", inside)
    fromleft = lax.ppermute(right, "gx", ring(around, 1))
    fromright = lax.ppermute(left, "gx", ring(around, -1))
    corner_r, corner_l = corner_call(first, second)
    cornerleft = lax.ppermute(corner_r, "gx", ring(around, 1))
    cornerright = lax.ppermute(corner_l, "gx", ring(around, -1))
    newf, newg, outf, outg, partial = inner_call(
        post, adj_flow_in, adj_field_in, first, second, profile, table, wall, magnet
    )
    newf, newg, outf, outg, share = outer_call(
        post, adj_flow_in, adj_field_in, first, second, fromleft, fromright, cornerleft,
        cornerright, profile, table, wall, magnet, partial, newf, newg, outf, outg,
    )
    cells = flow.shape[1] * around * flow.shape[2] * across * flow.shape[3]
    totals = butterfly(share[0])
    return (newf, newg, outf, outg, totals / math.sqrt(cells / count))


def solution(mesh):
    stack = P(None, "gx", "gy", None)
    cell = P("gx", "gy", None)
    return jax.shard_map(
        on_device,
        mesh=mesh,
        in_specs=(stack, stack, stack, stack, cell, P(), cell, cell),
        out_specs=(stack, stack, stack, stack, P()),
        check_vma=False,
    )
```

time: 167 us -> 59.4 us (0.36); the launches traced: 164 us -> 58.9 us
  other arithmetic: 80.1 us -> 0.53 us
  blocking collectives: 39 us -> 0 us
  Pallas kernels: 0 us -> 13.9 us
  local copies, waits for them, and re-layouts: 4.91 us -> 14.6 us
  matrix products: 6.66 us -> 0 us
  waiting for transfers between devices: 17.2 us -> 12.9 us
  starting transfers between devices: 14.3 us -> 16.3 us
    concatenate x3 -> x0, other arithmetic: 39.2 us -> none  [with_halo(): block = jnp.concatenate([low, block, high], axis=dim)]
    psum x1 -> x0, blocking collectives: 39 us -> none  [on_device(): totals = lax.psum(shares, ('gx', 'gy'))]
    unnamed x35 -> x0, other arithmetic: 14.2 us -> none
    pallas_call x0 -> x4, Pallas kernels: none -> 13.9 us  [the longest x1 5.28 us: inner_call(): pl.pallas_call(inner_kernel, in_specs=[ANY, ANY, ANY, ANY, ANY, VMEM, VME...]
    unnamed x151 -> x32, local copies, waits for them, and re-layouts: 3.65 us -> 14.6 us
    add_any x5 -> x0, other arithmetic: 7.72 us -> none  [the longest x1 2.64 us: collide(): 3.0 * along]
    reduce_sum x6 -> x0, other arithmetic: 6.77 us -> none  [the longest x1 3.07 us: collide(): along = velx * shifted + vely * speed_y + velz * speed_z]
    dot_general x2 -> x0, matrix products: 6.66 us -> none  [the longest x1 5.09 us: on_device(): jnp.tensordot(table, dcell * profile, axes=3, precision=lax.Precision.HIG...]
  transfers between devices with their start and end apart: 8 -> 11, of which waited for: 3 -> 6; matrix products, arithmetic and copies ran while one was open for 17% -> 0% of each run, Pallas kernels for 0% -> 12%
where the time goes in v1:
time: 59.4 us; the launch traced here: 58.9 us
  starting transfers between devices  16.3 us (27%)
  local copies, waits for them, and re-layouts  14.6 us (25%)
  Pallas kernels  13.9 us (23%)
  waiting for transfers between devices  12.9 us (22%)
  between operations  0.74 us (1%)
    unnamed x32, local copies, waits for them, and re-layouts  14.6 us
    ppermute x5, waiting for transfers between devices, butterfly(): lax.ppermute(value, axis, [(i, i ^ step) for i in range(count)])  11.6 us
    pallas_call x1, Pallas kernels, inner_call(): pl.pallas_call(inner_kernel, in_specs=[ANY, ANY, ANY, ANY, ANY, VMEM, VME...  5.28 us
    ppermute x5, starting transfers between devices, butterfly(): lax.ppermute(value, axis, [(i, i ^ step) for i in range(count)])  4.65 us
    pallas_call x1, Pallas kernels, outer_call(): pl.pallas_call(outer_kernel, in_specs=[ANY] * 5 + [VMEM] * 9 + [ANY] * 4,...  3.93 us
    ppermute x1, starting transfers between devices, on_device(): second = lax.ppermute(mine2, 'gy', between)  3.56 us
    pallas_call x1, Pallas kernels, collide_call(): pl.pallas_call(functools.partial(collide_kernel, planes), grid=(grid,), i...  2.98 us
    ppermute x1, starting transfers between devices, on_device(): fromright = lax.ppermute(left, 'gx', ring(around, -1))  2.25 us
  transfers between devices with their start and end apart: 11, of which 6 were waited for; matrix products, arithmetic and copies ran while one was open for 0% of the time, Pallas kernels for 12%

profile of v1, /device:TPU:0, one launch (start us, length us, event | category | flops | bytes accessed | tf_op | source)
XLA Modules:
  0.0 58.9 jit_solution(8967872403586393850)
XLA Ops:
  0.6 1.7 %copy-done = f32[19,8,8,512]{3,2,1,0:T(8,128)S(1)} copy-done((f32[19,8,8,512]{3,2,1,0:T(8,128)S(1)}, f32[19,8,8,512]{3,2,1,0:T(8,128)}, u32[]{:S(2)}) %copy-start) | copy-done | bytes 2490392
  2.3 1.2 %copy-done.4 = f32[7,8,8,512]{3,2,1,0:T(8,128)S(1)} copy-done((f32[7,8,8,512]{3,2,1,0:T(8,128)S(1)}, f32[7,8,8,512]{3,2,1,0:T(8,128)}, u32[]{:S(2)}) %copy-start.4) | copy-done | bytes 917528
  3.5 1.7 %copy-done.6 = f32[19,8,8,512]{3,2,1,0:T(8,128)S(1)} copy-done((f32[19,8,8,512]{3,2,1,0:T(8,128)S(1)}, f32[19,8,8,512]{3,2,1,0:T(8,128)}, u32[]{:S(2)}) %copy-start.6) | copy-done | bytes 2490392
  7.9 1.2 %copy-done.13 = f32[7,8,8,512]{3,2,1,0:T(8,128)S(1)} copy-done((f32[7,8,8,512]{3,2,1,0:T(8,128)S(1)}, f32[7,8,8,512]{3,2,1,0:T(8,128)}, u32[]{:S(2)}) %copy-start.13) | copy-done | bytes 917528
  9.8 3.0 %collide.1 = (f32[26,8,8,512]{3,2,1,0:T(8,128)S(1)}, f32[13,8,512]{2,1,0:T(8,128)S(1)}, f32[13,8,512]{2,1,0:T(8,128)S(1)}, f32[13,8,512]{2,1,0:T(8,128)}, f32[13,8,512]{2,1,0:T(8,128)}) custom-call(f32[19,8,8,512]{3,2,1,0:T(8,128)S(1)} %copy-done.6, f32[7,8,8,512]{3,2,1,0:T(8,128)S(1)} %copy-done.13, f32[19,8,8,512]{3,2,1,0:T(8,128)S(1)} %copy-done, ...), custom_call_target="tpu_custom_call" | custom-call | tf_op jit(solution)/shard_map/collide/pallas_call | solution.py:197
  12.8 1.7 %copy-done.2 = f32[26,8,8,512]{3,2,1,0:T(8,128)} copy-done((f32[26,8,8,512]{3,2,1,0:T(8,128)}, f32[26,8,8,512]{3,2,1,0:T(8,128)S(1)}, u32[]{:S(2)}) %copy-start.2) | copy-done | bytes 3407896
  14.9 3.6 %collective-permute-start.1 = (f32[13,8,512]{2,1,0:T(8,128)S(1)}, f32[13,8,512]{2,1,0:T(8,128)}, u32[]{:S(2)}, u32[]{:S(2)}) collective-permute-start(f32[13,8,512]{2,1,0:T(8,128)S(1)} %get-tuple-element.24), channel_id=1, source_target_pairs={{0,7},{1,2},{2,1},{3,4},{4,3},{5,6},{6,5},{7,0},{8,15},{9,10},{10,... | collective-permute-start | bytes 638984 | tf_op jit(solution)/shard_map/ppermute | solution.py:763
  18.5 1.6 %collective-permute-start.2 = (f32[13,8,512]{2,1,0:T(8,128)}, f32[13,8,512]{2,1,0:T(8,128)}, u32[]{:S(2)}, u32[]{:S(2)}) collective-permute-start(f32[13,8,512]{2,1,0:T(8,128)} %get-tuple-element.25), channel_id=1, source_target_pairs={{0,8},{8,16},{16,24},{24,0},{1,9},{9,17},{17,25},{25,1},{2,10},{10... | collective-permute-start | bytes 638984 | tf_op jit(solution)/shard_map/ppermute | solution.py:765
  20.1 2.2 %collective-permute-start.3 = (f32[13,8,512]{2,1,0:T(8,128)}, f32[13,8,512]{2,1,0:T(8,128)}, u32[]{:S(2)}, u32[]{:S(2)}) collective-permute-start(f32[13,8,512]{2,1,0:T(8,128)} %get-tuple-element.26), channel_id=1, source_target_pairs={{0,24},{8,0},{16,8},{24,16},{1,25},{9,1},{17,9},{25,17},{2,26},{10... | collective-permute-start | bytes 638984 | tf_op jit(solution)/shard_map/ppermute | solution.py:766
  22.3 1.3 %collective-permute-done.1.second_ref = f32[13,8,512]{2,1,0:T(8,128)} collective-permute-done((f32[13,8,512]{2,1,0:T(8,128)S(1)}, f32[13,8,512]{2,1,0:T(8,128)}, u32[]{:S(2)}, u32[]{:S(2)}) %collective-permute-start.1) | collective-permute-done | bytes 213024 | tf_op jit(solution)/shard_map/ppermute | solution.py:763
  23.6 1.7 %corners.1 = (f32[8,512]{1,0:T(8,128)}, f32[8,512]{1,0:T(8,128)}) custom-call(f32[13,8,512]{2,1,0:T(8,128)} %collective-permute-done.first_ref, f32[13,8,512]{2,1,0:T(8,128)} %collective-permute-done.1.second_ref), custom_call_target="tpu_custom_call" | custom-call | tf_op jit(solution)/shard_map/corners/pallas_call | solution.py:256
  25.3 1.8 %collective-permute-start.4 = (f32[8,512]{1,0:T(8,128)}, f32[8,512]{1,0:T(8,128)S(1)}, u32[]{:S(2)}, u32[]{:S(2)}) collective-permute-start(f32[8,512]{1,0:T(8,128)} %get-tuple-element.27), channel_id=1, source_target_pairs={{0,8},{8,16},{16,24},{24,0},{1,9},{9,17},{17,25},{25,1},{2,10},{10... | collective-permute-start | bytes 49160 | tf_op jit(solution)/shard_map/ppermute | solution.py:768
  27.0 2.1 %collective-permute-start.5 = (f32[8,512]{1,0:T(8,128)}, f32[8,512]{1,0:T(8,128)S(1)}, u32[]{:S(2)}, u32[]{:S(2)}) collective-permute-start(f32[8,512]{1,0:T(8,128)} %get-tuple-element.28), channel_id=1, source_target_pairs={{0,24},{8,0},{16,8},{24,16},{1,25},{9,1},{17,9},{25,17},{2,26},{10... | collective-permute-start | bytes 49160 | tf_op jit(solution)/shard_map/ppermute | solution.py:769
  29.1 2.0 %copy-done.3 = f32[26,8,8,512]{3,2,1,0:T(8,128)S(1)} copy-done((f32[26,8,8,512]{3,2,1,0:T(8,128)S(1)}, f32[26,8,8,512]{3,2,1,0:T(8,128)}, u32[]{:S(2)}) %copy-start.3) | copy-done | bytes 3407896
  32.9 5.3 %inner.1 = (f32[19,8,8,512]{3,2,1,0:T(8,128)}, f32[7,8,8,512]{3,2,1,0:T(8,128)}, f32[19,8,8,512]{3,2,1,0:T(8,128)}, f32[7,8,8,512]{3,2,1,0:T(8,128)}, f32[32,8,128]{2,1,0:T(8,128)S(1)}) custom-call(f32[26,8,8,512]{3,2,1,0:T(8,128)S(1)} %copy-done.3, f32[19,8,8,512]{3,2,1,0:T(8,128)S(1)} %copy-done.1, f32[7,8,8,512]{3,2,1,0:T(8,128)S(1)} %copy-done.5, ...), custom_call_target="tpu_custom_call" | custom-call | flops 22937600 | bytes 13631488 | tf_op jit(solution)/shard_map/inner/pallas_call | solution.py:564
  38.2 3.9 %outer.1 = (f32[19,8,8,512]{3,2,1,0:T(8,128)}, f32[7,8,8,512]{3,2,1,0:T(8,128)}, f32[19,8,8,512]{3,2,1,0:T(8,128)}, f32[7,8,8,512]{3,2,1,0:T(8,128)}, f32[8,32]{1,0:T(8,128)S(1)}) custom-call(f32[26,8,8,512]{3,2,1,0:T(8,128)S(1)} %copy-done.3, ...), custom_call_target="tpu_custom_call", output_to_operand_aliasing={{0}: (14, {}), {1}: (15, {}), {2}: (16, {}), {3}: (17, {})} | custom-call | tf_op jit(solution)/shard_map/outer/pallas_call | solution.py:706
  42.2 1.1 %collective-permute-done.6 = f32[32]{0:T(128)S(1)} collective-permute-done((f32[32]{0:T(128)S(1)}, f32[32]{0:T(128)S(1)}, u32[]{:S(2)}, u32[]{:S(2)}) %collective-permute-start.6) | collective-permute-done | bytes 160 | tf_op jit(solution)/shard_map/ppermute | solution.py:749
  43.4 1.7 %collective-permute-start.7 = (f32[32]{0:T(128)S(1)}, f32[32]{0:T(128)S(1)}, u32[]{:S(2)}, u32[]{:S(2)}) collective-permute-start(f32[32]{0:T(128)S(1)} %fusion), channel_id=1, source_target_pairs={{0,2},{1,3},{2,0},{3,1},{4,6},{5,7},{6,4},{7,5},{8,10},{9,11},{10,... | collective-permute-start | bytes 392 | tf_op jit(solution)/shard_map/ppermute | solution.py:749
  45.0 1.9 %collective-permute-done.7 = f32[32]{0:T(128)S(1)} collective-permute-done((f32[32]{0:T(128)S(1)}, f32[32]{0:T(128)S(1)}, u32[]{:S(2)}, u32[]{:S(2)}) %collective-permute-start.7) | collective-permute-done | bytes 160 | tf_op jit(solution)/shard_map/ppermute | solution.py:749
  46.9 1.9 %collective-permute-start.8 = (f32[32]{0:T(128)S(1)}, f32[32]{0:T(128)S(1)}, u32[]{:S(2)}, u32[]{:S(2)}) collective-permute-start(f32[32]{0:T(128)S(1)} %add.16), channel_id=1, source_target_pairs={{0,4},{1,5},{2,6},{3,7},{4,0},{5,1},{6,2},{7,3},{8,12},{9,13},{10,... | collective-permute-start | bytes 392 | tf_op jit(solution)/shard_map/ppermute | solution.py:749
  48.8 1.6 %collective-permute-done.8 = f32[32]{0:T(128)S(1)} collective-permute-done((f32[32]{0:T(128)S(1)}, f32[32]{0:T(128)S(1)}, u32[]{:S(2)}, u32[]{:S(2)}) %collective-permute-start.8) | collective-permute-done | bytes 160 | tf_op jit(solution)/shard_map/ppermute | solution.py:749
  50.4 3.5 %collective-permute-done.9 = f32[32]{0:T(128)S(1)} collective-permute-done((f32[32]{0:T(128)S(1)}, f32[32]{0:T(128)S(1)}, u32[]{:S(2)}, u32[]{:S(2)}) %collective-permute-start.9) | collective-permute-done | bytes 160 | tf_op jit(solution)/shard_map/ppermute | solution.py:749
  54.0 1.0 %collective-permute-start.10 = (f32[32]{0:T(128)S(1)}, f32[32]{0:T(128)S(1)}, u32[]{:S(2)}, u32[]{:S(2)}) collective-permute-start(f32[32]{0:T(128)S(1)} %add.18), channel_id=1, source_target_pairs={{0,16},{8,24},{16,0},{24,8},{1,17},{9,25},{17,1},{25,9},{2,18},{10... | collective-permute-start | bytes 392 | tf_op jit(solution)/shard_map/ppermute | solution.py:749
  55.0 3.5 %collective-permute-done.10 = f32[32]{0:T(128)S(1)} collective-permute-done((f32[32]{0:T(128)S(1)}, f32[32]{0:T(128)S(1)}, u32[]{:S(2)}, u32[]{:S(2)}) %collective-permute-start.10) | collective-permute-done | bytes 160 | tf_op jit(solution)/shard_map/ppermute | solution.py:749
  (40 shorter events, 6.3 us)
Async XLA Ops:
  0.6 1.7 %copy-start = (f32[19,8,8,512]{3,2,1,0:T(8,128)S(1)}, f32[19,8,8,512]{3,2,1,0:T(8,128)}, u32[]{:S(2)}) copy-start(f32[19,8,8,512]{3,2,1,0:T(8,128)} %adjf_ref.5) | copy-start | bytes 7471108
  2.3 1.2 %copy-start.4 = (f32[7,8,8,512]{3,2,1,0:T(8,128)S(1)}, f32[7,8,8,512]{3,2,1,0:T(8,128)}, u32[]{:S(2)}) copy-start(f32[7,8,8,512]{3,2,1,0:T(8,128)} %adjg_ref.5) | copy-start | bytes 2752516
  3.5 1.7 %copy-start.6 = (f32[19,8,8,512]{3,2,1,0:T(8,128)S(1)}, f32[19,8,8,512]{3,2,1,0:T(8,128)}, u32[]{:S(2)}) copy-start(f32[19,8,8,512]{3,2,1,0:T(8,128)} %flow_ref.1) | copy-start | bytes 7471108
  5.2 0.9 %copy-start.7 = (f32[8,8,512]{2,1,0:T(8,128)S(1)}, f32[8,8,512]{2,1,0:T(8,128)}, u32[]{:S(2)}) copy-start(f32[8,8,512]{2,1,0:T(8,128)} %profile_ref.5) | copy-start | bytes 393220
  6.1 0.9 %copy-start.9 = (s32[8,8,512]{2,1,0:T(8,128)S(1)}, s32[8,8,512]{2,1,0:T(8,128)}, u32[]{:S(2)}) copy-start(s32[8,8,512]{2,1,0:T(8,128)} %wall_ref.5) | copy-start | bytes 393220
  7.0 0.9 %copy-start.11 = (s32[8,8,512]{2,1,0:T(8,128)S(1)}, s32[8,8,512]{2,1,0:T(8,128)}, u32[]{:S(2)}) copy-start(s32[8,8,512]{2,1,0:T(8,128)} %magnet_ref.5) | copy-start | bytes 393220
  7.9 1.2 %copy-start.13 = (f32[7,8,8,512]{3,2,1,0:T(8,128)S(1)}, f32[7,8,8,512]{3,2,1,0:T(8,128)}, u32[]{:S(2)}) copy-start(f32[7,8,8,512]{3,2,1,0:T(8,128)} %field_ref.1) | copy-start | bytes 2752516
  9.8 19.3 %copy-start.1 = (f32[19,8,8,512]{3,2,1,0:T(8,128)S(1)}, f32[19,8,8,512]{3,2,1,0:T(8,128)}, u32[]{:S(2)}) copy-start(f32[19,8,8,512]{3,2,1,0:T(8,128)} %adjf_ref.5) | copy-start | bytes 7471108
  9.8 19.3 %copy-start.5 = (f32[7,8,8,512]{3,2,1,0:T(8,128)S(1)}, f32[7,8,8,512]{3,2,1,0:T(8,128)}, u32[]{:S(2)}) copy-start(f32[7,8,8,512]{3,2,1,0:T(8,128)} %adjg_ref.5) | copy-start | bytes 2752516
  9.8 19.3 %copy-start.8 = (f32[8,8,512]{2,1,0:T(8,128)S(1)}, f32[8,8,512]{2,1,0:T(8,128)}, u32[]{:S(2)}) copy-start(f32[8,8,512]{2,1,0:T(8,128)} %profile_ref.5) | copy-start | bytes 393220
  9.8 19.3 %copy-start.15 = (f32[32]{0:T(128)S(1)}, f32[32]{0:T(128)}, u32[]{:S(2)}) copy-start(f32[32]{0:T(128)} %param.13) | copy-start | bytes 388
  12.8 1.7 %copy-start.2 = (f32[26,8,8,512]{3,2,1,0:T(8,128)}, f32[26,8,8,512]{3,2,1,0:T(8,128)S(1)}, u32[]{:S(2)}) copy-start(f32[26,8,8,512]{3,2,1,0:T(8,128)S(1)} %get-tuple-element.22.post_ref) | copy-start | bytes 10223620
  14.5 7.8 %collective-permute-start = (f32[13,8,512]{2,1,0:T(8,128)S(1)}, f32[13,8,512]{2,1,0:T(8,128)}, u32[]{:S(2)}, u32[]{:S(2)}) collective-permute-start(f32[13,8,512]{2,1,0:T(8,128)S(1)} %get-tuple-element.23), channel_id=1, source_target_pairs={{0,1},{1,0},{2,3},{3,2},{4,5},{5,4},{6,7},{7,6},{8,9},{9,8},{10,11... | collective-permute-start | bytes 638984 | tf_op jit(solution)/shard_map/ppermute | solution.py:764
  14.9 8.7 %collective-permute-start.1 = (f32[13,8,512]{2,1,0:T(8,128)S(1)}, f32[13,8,512]{2,1,0:T(8,128)}, u32[]{:S(2)}, u32[]{:S(2)}) collective-permute-start(f32[13,8,512]{2,1,0:T(8,128)S(1)} %get-tuple-element.24), channel_id=1, source_target_pairs={{0,7},{1,2},{2,1},{3,4},{4,3},{5,6},{6,5},{7,0},{8,15},{9,10},{10,... | collective-permute-start | bytes 638984 | tf_op jit(solution)/shard_map/ppermute | solution.py:763
  18.5 19.7 %collective-permute-start.2 = (f32[13,8,512]{2,1,0:T(8,128)}, f32[13,8,512]{2,1,0:T(8,128)}, u32[]{:S(2)}, u32[]{:S(2)}) collective-permute-start(f32[13,8,512]{2,1,0:T(8,128)} %get-tuple-element.25), channel_id=1, source_target_pairs={{0,8},{8,16},{16,24},{24,0},{1,9},{9,17},{17,25},{25,1},{2,10},{10... | collective-permute-start | bytes 638984 | tf_op jit(solution)/shard_map/ppermute | solution.py:765
  20.1 18.1 %collective-permute-start.3 = (f32[13,8,512]{2,1,0:T(8,128)}, f32[13,8,512]{2,1,0:T(8,128)}, u32[]{:S(2)}, u32[]{:S(2)}) collective-permute-start(f32[13,8,512]{2,1,0:T(8,128)} %get-tuple-element.26), channel_id=1, source_target_pairs={{0,24},{8,0},{16,8},{24,16},{1,25},{9,1},{17,9},{25,17},{2,26},{10... | collective-permute-start | bytes 638984 | tf_op jit(solution)/shard_map/ppermute | solution.py:766
  25.3 12.9 %collective-permute-start.4 = (f32[8,512]{1,0:T(8,128)}, f32[8,512]{1,0:T(8,128)S(1)}, u32[]{:S(2)}, u32[]{:S(2)}) collective-permute-start(f32[8,512]{1,0:T(8,128)} %get-tuple-element.27), channel_id=1, source_target_pairs={{0,8},{8,16},{16,24},{24,0},{1,9},{9,17},{17,25},{25,1},{2,10},{10... | collective-permute-start | bytes 49160 | tf_op jit(solution)/shard_map/ppermute | solution.py:768
  27.0 11.2 %collective-permute-start.5 = (f32[8,512]{1,0:T(8,128)}, f32[8,512]{1,0:T(8,128)S(1)}, u32[]{:S(2)}, u32[]{:S(2)}) collective-permute-start(f32[8,512]{1,0:T(8,128)} %get-tuple-element.28), channel_id=1, source_target_pairs={{0,24},{8,0},{16,8},{24,16},{1,25},{9,1},{17,9},{25,17},{2,26},{10... | collective-permute-start | bytes 49160 | tf_op jit(solution)/shard_map/ppermute | solution.py:769
  29.1 2.0 %copy-start.3 = (f32[26,8,8,512]{3,2,1,0:T(8,128)S(1)}, f32[26,8,8,512]{3,2,1,0:T(8,128)}, u32[]{:S(2)}) copy-start(f32[26,8,8,512]{3,2,1,0:T(8,128)} %copy-done.2) | copy-start | bytes 10223620
  42.2 1.2 %collective-permute-start.6 = (f32[32]{0:T(128)S(1)}, f32[32]{0:T(128)S(1)}, u32[]{:S(2)}, u32[]{:S(2)}) collective-permute-start(f32[32]{0:T(128)S(1)} %slice_bitcast_fusion), channel_id=1, source_target_pairs={{0,1},{1,0},{2,3},{3,2},{4,5},{5,4},{6,7},{7,6},{8,9},{9,8},{10,11... | collective-permute-start | bytes 392 | tf_op jit(solution)/shard_map/ppermute | solution.py:749
  43.4 3.5 %collective-permute-start.7 = (f32[32]{0:T(128)S(1)}, f32[32]{0:T(128)S(1)}, u32[]{:S(2)}, u32[]{:S(2)}) collective-permute-start(f32[32]{0:T(128)S(1)} %fusion), channel_id=1, source_target_pairs={{0,2},{1,3},{2,0},{3,1},{4,6},{5,7},{6,4},{7,5},{8,10},{9,11},{10,... | collective-permute-start | bytes 392 | tf_op jit(solution)/shard_map/ppermute | solution.py:749
  46.9 3.5 %collective-permute-start.8 = (f32[32]{0:T(128)S(1)}, f32[32]{0:T(128)S(1)}, u32[]{:S(2)}, u32[]{:S(2)}) collective-permute-start(f32[32]{0:T(128)S(1)} %add.16), channel_id=1, source_target_pairs={{0,4},{1,5},{2,6},{3,7},{4,0},{5,1},{6,2},{7,3},{8,12},{9,13},{10,... | collective-permute-start | bytes 392 | tf_op jit(solution)/shard_map/ppermute | solution.py:749
  50.4 3.5 %collective-permute-start.9 = (f32[32]{0:T(128)S(1)}, f32[32]{0:T(128)S(1)}, u32[]{:S(2)}, u32[]{:S(2)}) collective-permute-start(f32[32]{0:T(128)S(1)} %add.17), channel_id=1, source_target_pairs={{0,8},{8,0},{16,24},{24,16},{1,9},{9,1},{17,25},{25,17},{2,10},{10... | collective-permute-start | bytes 392 | tf_op jit(solution)/shard_map/ppermute | solution.py:749
  54.0 4.4 %collective-permute-start.10 = (f32[32]{0:T(128)S(1)}, f32[32]{0:T(128)S(1)}, u32[]{:S(2)}, u32[]{:S(2)}) collective-permute-start(f32[32]{0:T(128)S(1)} %add.18), channel_id=1, source_target_pairs={{0,16},{8,24},{16,0},{24,8},{1,17},{9,25},{17,1},{25,9},{2,18},{10... | collective-permute-start | bytes 392 | tf_op jit(solution)/shard_map/ppermute | solution.py:749
  (3 other events, 2.5 us)

commit v2 on v1

--- a/solution.py
+++ b/solution.py
@@ -221,7 +221,7 @@
             faces,
             faces,
         ],
-        compiler_params=pltpu.CompilerParams(vmem_limit_bytes=40 << 20),
+        compiler_params=pltpu.CompilerParams(vmem_limit_bytes=62 << 20),
         name="collide",
     )(flow, field, adjf, adjg, profile, strengths, wall, magnet)
 
@@ -253,7 +253,7 @@
 def corner_call(first, second):
     sz = first.shape[2]
     out = jax.ShapeDtypeStruct((8, sz), jnp.float32)
-    return pl.pallas_call(corner_kernel, out_shape=[out, out], name="corners")(first, second)
+    return pl.pallas_call(corner_kernel, out_shape=[out, out], compiler_params=pltpu.CompilerParams(vmem_limit_bytes=2 << 20), name="corners")(first, second)
 
 
 def plane_step(
@@ -588,7 +588,7 @@
             dma((sx,)),
             dma((sx,)),
         ],
-        compiler_params=pltpu.CompilerParams(vmem_limit_bytes=40 << 20),
+        compiler_params=pltpu.CompilerParams(vmem_limit_bytes=51 << 20),
         cost_estimate=pl.CostEstimate(
             flops=700 * sx * sy * sz, bytes_accessed=16 * NP * sx * sy * sz, transcendentals=0
         ),
@@ -729,7 +729,7 @@
             dma((2,)),
             dma((2, 4)),
         ],
-        compiler_params=pltpu.CompilerParams(vmem_limit_bytes=40 << 20),
+        compiler_params=pltpu.CompilerParams(vmem_limit_bytes=51 << 20),
         name="outer",
     )(
         post, adjf, adjg, first, second, fromleft, fromright, cornerleft, cornerright, profile,

time: 59.4 us -> 47.2 us (0.79)
  local copies, waits for them, and re-layouts: 14.6 us -> 0.02 us
  Pallas kernels: 13.9 us -> 16.1 us
    unnamed x32 -> x10, local copies, waits for them, and re-layouts: 14.6 us -> 0.02 us
    pallas_call x1, Pallas kernels: 2.98 us -> 6.01 us  [collide_call(): pl.pallas_call(functools.partial(collide_kernel, planes), grid=(grid,), i...]
    pallas_call x1, Pallas kernels: 1.66 us -> 0.01 us  [corner_call(): pl.pallas_call(corner_kernel, out_shape=[out, out], compiler_params=pltpu...]
    pallas_call x1, Pallas kernels: 5.28 us -> 6.19 us  [inner_call(): pl.pallas_call(inner_kernel, in_specs=[ANY, ANY, ANY, ANY, ANY, VMEM, VME...]
  transfers between devices with their start and end apart: 11 -> 11, of which waited for: 6 -> 6; matrix products, arithmetic and copies ran while one was open for 0% -> 0% of each run, Pallas kernels for 12% -> 13%
where the time goes in v2:
time: 47.2 us; the launch traced here: 47 us
  starting transfers between devices  16.5 us (35%)
  Pallas kernels  16.1 us (34%)
  waiting for transfers between devices  13.1 us (28%)
  between operations  0.77 us (2%)
  other arithmetic  0.53 us (1%)
    ppermute x5, waiting for transfers between devices, butterfly(): lax.ppermute(value, axis, [(i, i ^ step) for i in range(count)])  11.7 us
    pallas_call x1, Pallas kernels, inner_call(): pl.pallas_call(inner_kernel, in_specs=[ANY, ANY, ANY, ANY, ANY, VMEM, VME...  6.19 us
    pallas_call x1, Pallas kernels, collide_call(): pl.pallas_call(functools.partial(collide_kernel, planes), grid=(grid,), i...  6.01 us
    ppermute x5, starting transfers between devices, butterfly(): lax.ppermute(value, axis, [(i, i ^ step) for i in range(count)])  4.52 us
    pallas_call x1, Pallas kernels, outer_call(): pl.pallas_call(outer_kernel, in_specs=[ANY] * 5 + [VMEM] * 9 + [ANY] * 4,...  3.85 us
    ppermute x1, starting transfers between devices, on_device(): second = lax.ppermute(mine2, 'gy', between)  3.56 us
    ppermute x1, starting transfers between devices, on_device(): fromright = lax.ppermute(left, 'gx', ring(around, -1))  2.25 us
    ppermute x1, starting transfers between devices, on_device(): cornerright = lax.ppermute(corner_l, 'gx', ring(around, -1))  2.09 us
  transfers between devices with their start and end apart: 11, of which 6 were waited for; matrix products, arithmetic and copies ran while one was open for 0% of the time, Pallas kernels for 13%

profile of v2, /device:TPU:0, one launch (start us, length us, event | category | flops | bytes accessed | tf_op | source)
XLA Modules:
  0.0 47.0 jit_solution(7270631659596833031)
XLA Ops:
  0.7 6.0 %collide.1 = (f32[26,8,8,512]{3,2,1,0:T(8,128)}, f32[13,8,512]{2,1,0:T(8,128)}, f32[13,8,512]{2,1,0:T(8,128)}, f32[13,8,512]{2,1,0:T(8,128)}, f32[13,8,512]{2,1,0:T(8,128)}) custom-call(f32[19,8,8,512]{3,2,1,0:T(8,128)} %flow_ref.1, f32[7,8,8,512]{3,2,1,0:T(8,128)} %field_ref.1, f32[19,8,8,512]{3,2,1,0:T(8,128)} %adjf_ref.5, f32[7,8,8,512]{3,2,1,0:T(8,128)} %adjg_ref.5, ...), custom_call_target="tpu_custom_call" | custom-call | tf_op jit(solution)/shard_map/collide/pallas_call | solution.py:197
  6.7 0.5 %collective-permute-start = (f32[13,8,512]{2,1,0:T(8,128)}, f32[13,8,512]{2,1,0:T(8,128)S(1)}, u32[]{:S(2)}, u32[]{:S(2)}) collective-permute-start(f32[13,8,512]{2,1,0:T(8,128)} %get-tuple-element.23), channel_id=1, source_target_pairs={{0,1},{1,0},{2,3},{3,2},{4,5},{5,4},{6,7},{7,6},{8,9},{9,8},{10,11... | collective-permute-start | bytes 638984 | tf_op jit(solution)/shard_map/ppermute | solution.py:764
  7.2 3.6 %collective-permute-start.1 = (f32[13,8,512]{2,1,0:T(8,128)}, f32[13,8,512]{2,1,0:T(8,128)S(1)}, u32[]{:S(2)}, u32[]{:S(2)}) collective-permute-start(f32[13,8,512]{2,1,0:T(8,128)} %get-tuple-element.24), channel_id=1, source_target_pairs={{0,7},{1,2},{2,1},{3,4},{4,3},{5,6},{6,5},{7,0},{8,15},{9,10},{10,... | collective-permute-start | bytes 638984 | tf_op jit(solution)/shard_map/ppermute | solution.py:763
  10.8 1.6 %collective-permute-start.2 = (f32[13,8,512]{2,1,0:T(8,128)}, f32[13,8,512]{2,1,0:T(8,128)S(1)}, u32[]{:S(2)}, u32[]{:S(2)}) collective-permute-start(f32[13,8,512]{2,1,0:T(8,128)} %get-tuple-element.25), channel_id=1, source_target_pairs={{0,8},{8,16},{16,24},{24,0},{1,9},{9,17},{17,25},{25,1},{2,10},{10... | collective-permute-start | bytes 638984 | tf_op jit(solution)/shard_map/ppermute | solution.py:765
  12.3 2.2 %collective-permute-start.3 = (f32[13,8,512]{2,1,0:T(8,128)}, f32[13,8,512]{2,1,0:T(8,128)S(1)}, u32[]{:S(2)}, u32[]{:S(2)}) collective-permute-start(f32[13,8,512]{2,1,0:T(8,128)} %get-tuple-element.26), channel_id=1, source_target_pairs={{0,24},{8,0},{16,8},{24,16},{1,25},{9,1},{17,9},{25,17},{2,26},{10... | collective-permute-start | bytes 638984 | tf_op jit(solution)/shard_map/ppermute | solution.py:766
  14.6 0.0 collective-permute-done.first_ref
  14.6 1.4 %collective-permute-done.1.second_ref = f32[13,8,512]{2,1,0:T(8,128)S(1)} collective-permute-done((f32[13,8,512]{2,1,0:T(8,128)}, f32[13,8,512]{2,1,0:T(8,128)S(1)}, u32[]{:S(2)}, u32[]{:S(2)}) %collective-permute-start.1) | collective-permute-done | bytes 213024 | tf_op jit(solution)/shard_map/ppermute | solution.py:763
  16.0 2.0 %collective-permute-start.4 = (f32[8,512]{1,0:T(8,128)S(1)}, f32[8,512]{1,0:T(8,128)S(1)}, u32[]{:S(2)}, u32[]{:S(2)}) collective-permute-start(f32[8,512]{1,0:T(8,128)S(1)} %get-tuple-element.27), channel_id=1, source_target_pairs={{0,8},{8,16},{16,24},{24,0},{1,9},{9,17},{17,25},{25,1},{2,10},{10... | collective-permute-start | bytes 49160 | tf_op jit(solution)/shard_map/ppermute | solution.py:768
  18.0 2.1 %collective-permute-start.5 = (f32[8,512]{1,0:T(8,128)S(1)}, f32[8,512]{1,0:T(8,128)S(1)}, u32[]{:S(2)}, u32[]{:S(2)}) collective-permute-start(f32[8,512]{1,0:T(8,128)S(1)} %get-tuple-element.28), channel_id=1, source_target_pairs={{0,24},{8,0},{16,8},{24,16},{1,25},{9,1},{17,9},{25,17},{2,26},{10... | collective-permute-start | bytes 49160 | tf_op jit(solution)/shard_map/ppermute | solution.py:769
  20.1 6.2 %inner.1 = (f32[19,8,8,512]{3,2,1,0:T(8,128)}, f32[7,8,8,512]{3,2,1,0:T(8,128)}, f32[19,8,8,512]{3,2,1,0:T(8,128)}, f32[7,8,8,512]{3,2,1,0:T(8,128)}, f32[32,8,128]{2,1,0:T(8,128)S(1)}) custom-call(f32[26,8,8,512]{3,2,1,0:T(8,128)} %get-tuple-element.22.post_ref, f32[19,8,8,512]{3,2,1,0:T(8,128)} %adjf_ref.5, f32[7,8,8,512]{3,2,1,0:T(8,128)S(1)} %copy-done, ...), custom_call_target="tpu_custom_call" | custom-call | flops 22937600 | bytes 13631488 | tf_op jit(solution)/shard_map/inner/pallas_call | solution.py:564
  26.3 0.0 collective-permute-done.2.fromleft_ref
  26.3 0.0 collective-permute-done.4.cornerleft_ref
  26.3 0.0 collective-permute-done.5.cornerright_ref
  26.3 3.9 %outer.1 = (f32[19,8,8,512]{3,2,1,0:T(8,128)}, f32[7,8,8,512]{3,2,1,0:T(8,128)}, f32[19,8,8,512]{3,2,1,0:T(8,128)}, f32[7,8,8,512]{3,2,1,0:T(8,128)}, f32[8,32]{1,0:T(8,128)S(1)}) custom-call(f32[26,8,8,512]{3,2,1,0:T(8,128)} %get-tuple-element.22.post_ref, ...), custom_call_target="tpu_custom_call", output_to_operand_aliasing={{0}: (14, {}), {1}: (15, {}), {2}: (16, {}), {3}: (17, {})} | custom-call | tf_op jit(solution)/shard_map/outer/pallas_call | solution.py:706
  30.2 0.1 collective-permute-start.6
  30.3 1.1 %collective-permute-done.6 = f32[32]{0:T(128)S(1)} collective-permute-done((f32[32]{0:T(128)S(1)}, f32[32]{0:T(128)S(1)}, u32[]{:S(2)}, u32[]{:S(2)}) %collective-permute-start.6) | collective-permute-done | bytes 160 | tf_op jit(solution)/shard_map/ppermute | solution.py:749
  31.4 1.7 %collective-permute-start.7 = (f32[32]{0:T(128)S(1)}, f32[32]{0:T(128)S(1)}, u32[]{:S(2)}, u32[]{:S(2)}) collective-permute-start(f32[32]{0:T(128)S(1)} %fusion), channel_id=1, source_target_pairs={{0,2},{1,3},{2,0},{3,1},{4,6},{5,7},{6,4},{7,5},{8,10},{9,11},{10,... | collective-permute-start | bytes 392 | tf_op jit(solution)/shard_map/ppermute | solution.py:749
  33.1 1.8 %collective-permute-done.7 = f32[32]{0:T(128)S(1)} collective-permute-done((f32[32]{0:T(128)S(1)}, f32[32]{0:T(128)S(1)}, u32[]{:S(2)}, u32[]{:S(2)}) %collective-permute-start.7) | collective-permute-done | bytes 160 | tf_op jit(solution)/shard_map/ppermute | solution.py:749
  34.9 1.8 %collective-permute-start.8 = (f32[32]{0:T(128)S(1)}, f32[32]{0:T(128)S(1)}, u32[]{:S(2)}, u32[]{:S(2)}) collective-permute-start(f32[32]{0:T(128)S(1)} %add.16), channel_id=1, source_target_pairs={{0,4},{1,5},{2,6},{3,7},{4,0},{5,1},{6,2},{7,3},{8,12},{9,13},{10,... | collective-permute-start | bytes 392 | tf_op jit(solution)/shard_map/ppermute | solution.py:749
  36.7 1.7 %collective-permute-done.8 = f32[32]{0:T(128)S(1)} collective-permute-done((f32[32]{0:T(128)S(1)}, f32[32]{0:T(128)S(1)}, u32[]{:S(2)}, u32[]{:S(2)}) %collective-permute-start.8) | collective-permute-done | bytes 160 | tf_op jit(solution)/shard_map/ppermute | solution.py:749
  38.5 3.5 %collective-permute-done.9 = f32[32]{0:T(128)S(1)} collective-permute-done((f32[32]{0:T(128)S(1)}, f32[32]{0:T(128)S(1)}, u32[]{:S(2)}, u32[]{:S(2)}) %collective-permute-start.9) | collective-permute-done | bytes 160 | tf_op jit(solution)/shard_map/ppermute | solution.py:749
  42.0 0.9 %collective-permute-start.10 = (f32[32]{0:T(128)S(1)}, f32[32]{0:T(128)S(1)}, u32[]{:S(2)}, u32[]{:S(2)}) collective-permute-start(f32[32]{0:T(128)S(1)} %add.18), channel_id=1, source_target_pairs={{0,16},{8,24},{16,0},{24,8},{1,17},{9,25},{17,1},{25,9},{2,18},{10... | collective-permute-start | bytes 392 | tf_op jit(solution)/shard_map/ppermute | solution.py:749
  43.0 3.5 %collective-permute-done.10 = f32[32]{0:T(128)S(1)} collective-permute-done((f32[32]{0:T(128)S(1)}, f32[32]{0:T(128)S(1)}, u32[]{:S(2)}, u32[]{:S(2)}) %collective-permute-start.10) | collective-permute-done | bytes 160 | tf_op jit(solution)/shard_map/ppermute | solution.py:749
  46.5 0.5 %add_multiply_fusion = f32[32]{0:T(128)} fusion(f32[32]{0:T(128)S(1)} %add.18, f32[32]{0:T(128)S(1)} %collective-permute-done.10), kind=kLoop, calls=%fused_computation | loop fusion | flops 64 | bytes 384 | tf_op jit(solution)/shard_map/div | solution.py:779
  (18 shorter events, 0.1 us)
Async XLA Ops:
  0.6 19.4 %copy-start = (f32[7,8,8,512]{3,2,1,0:T(8,128)S(1)}, f32[7,8,8,512]{3,2,1,0:T(8,128)}, u32[]{:S(2)}) copy-start(f32[7,8,8,512]{3,2,1,0:T(8,128)} %adjg_ref.5) | copy-start | bytes 2752516
  0.6 19.4 %copy-start.1 = (f32[8,8,512]{2,1,0:T(8,128)S(1)}, f32[8,8,512]{2,1,0:T(8,128)}, u32[]{:S(2)}) copy-start(f32[8,8,512]{2,1,0:T(8,128)} %profile_ref.5) | copy-start | bytes 393220
  0.7 19.4 %copy-start.2 = (s32[8,8,512]{2,1,0:T(8,128)S(1)}, s32[8,8,512]{2,1,0:T(8,128)}, u32[]{:S(2)}) copy-start(s32[8,8,512]{2,1,0:T(8,128)} %wall_ref.5) | copy-start | bytes 393220
  0.7 19.4 %copy-start.3 = (s32[8,8,512]{2,1,0:T(8,128)S(1)}, s32[8,8,512]{2,1,0:T(8,128)}, u32[]{:S(2)}) copy-start(s32[8,8,512]{2,1,0:T(8,128)} %magnet_ref.5) | copy-start | bytes 393220
  0.7 19.4 %copy-start.4 = (f32[32]{0:T(128)S(1)}, f32[32]{0:T(128)}, u32[]{:S(2)}) copy-start(f32[32]{0:T(128)} %param.13) | copy-start | bytes 388
  6.7 7.9 %collective-permute-start = (f32[13,8,512]{2,1,0:T(8,128)}, f32[13,8,512]{2,1,0:T(8,128)S(1)}, u32[]{:S(2)}, u32[]{:S(2)}) collective-permute-start(f32[13,8,512]{2,1,0:T(8,128)} %get-tuple-element.23), channel_id=1, source_target_pairs={{0,1},{1,0},{2,3},{3,2},{4,5},{5,4},{6,7},{7,6},{8,9},{9,8},{10,11... | collective-permute-start | bytes 638984 | tf_op jit(solution)/shard_map/ppermute | solution.py:764
  7.2 8.8 %collective-permute-start.1 = (f32[13,8,512]{2,1,0:T(8,128)}, f32[13,8,512]{2,1,0:T(8,128)S(1)}, u32[]{:S(2)}, u32[]{:S(2)}) collective-permute-start(f32[13,8,512]{2,1,0:T(8,128)} %get-tuple-element.24), channel_id=1, source_target_pairs={{0,7},{1,2},{2,1},{3,4},{4,3},{5,6},{6,5},{7,0},{8,15},{9,10},{10,... | collective-permute-start | bytes 638984 | tf_op jit(solution)/shard_map/ppermute | solution.py:763
  10.8 15.5 %collective-permute-start.2 = (f32[13,8,512]{2,1,0:T(8,128)}, f32[13,8,512]{2,1,0:T(8,128)S(1)}, u32[]{:S(2)}, u32[]{:S(2)}) collective-permute-start(f32[13,8,512]{2,1,0:T(8,128)} %get-tuple-element.25), channel_id=1, source_target_pairs={{0,8},{8,16},{16,24},{24,0},{1,9},{9,17},{17,25},{25,1},{2,10},{10... | collective-permute-start | bytes 638984 | tf_op jit(solution)/shard_map/ppermute | solution.py:765
  12.3 14.0 %collective-permute-start.3 = (f32[13,8,512]{2,1,0:T(8,128)}, f32[13,8,512]{2,1,0:T(8,128)S(1)}, u32[]{:S(2)}, u32[]{:S(2)}) collective-permute-start(f32[13,8,512]{2,1,0:T(8,128)} %get-tuple-element.26), channel_id=1, source_target_pairs={{0,24},{8,0},{16,8},{24,16},{1,25},{9,1},{17,9},{25,17},{2,26},{10... | collective-permute-start | bytes 638984 | tf_op jit(solution)/shard_map/ppermute | solution.py:766
  16.0 10.3 %collective-permute-start.4 = (f32[8,512]{1,0:T(8,128)S(1)}, f32[8,512]{1,0:T(8,128)S(1)}, u32[]{:S(2)}, u32[]{:S(2)}) collective-permute-start(f32[8,512]{1,0:T(8,128)S(1)} %get-tuple-element.27), channel_id=1, source_target_pairs={{0,8},{8,16},{16,24},{24,0},{1,9},{9,17},{17,25},{25,1},{2,10},{10... | collective-permute-start | bytes 49160 | tf_op jit(solution)/shard_map/ppermute | solution.py:768
  18.0 8.3 %collective-permute-start.5 = (f32[8,512]{1,0:T(8,128)S(1)}, f32[8,512]{1,0:T(8,128)S(1)}, u32[]{:S(2)}, u32[]{:S(2)}) collective-permute-start(f32[8,512]{1,0:T(8,128)S(1)} %get-tuple-element.28), channel_id=1, source_target_pairs={{0,24},{8,0},{16,8},{24,16},{1,25},{9,1},{17,9},{25,17},{2,26},{10... | collective-permute-start | bytes 49160 | tf_op jit(solution)/shard_map/ppermute | solution.py:769
  30.2 1.2 %collective-permute-start.6 = (f32[32]{0:T(128)S(1)}, f32[32]{0:T(128)S(1)}, u32[]{:S(2)}, u32[]{:S(2)}) collective-permute-start(f32[32]{0:T(128)S(1)} %slice_bitcast_fusion), channel_id=1, source_target_pairs={{0,1},{1,0},{2,3},{3,2},{4,5},{5,4},{6,7},{7,6},{8,9},{9,8},{10,11... | collective-permute-start | bytes 392 | tf_op jit(solution)/shard_map/ppermute | solution.py:749
  31.4 3.5 %collective-permute-start.7 = (f32[32]{0:T(128)S(1)}, f32[32]{0:T(128)S(1)}, u32[]{:S(2)}, u32[]{:S(2)}) collective-permute-start(f32[32]{0:T(128)S(1)} %fusion), channel_id=1, source_target_pairs={{0,2},{1,3},{2,0},{3,1},{4,6},{5,7},{6,4},{7,5},{8,10},{9,11},{10,... | collective-permute-start | bytes 392 | tf_op jit(solution)/shard_map/ppermute | solution.py:749
  34.9 3.5 %collective-permute-start.8 = (f32[32]{0:T(128)S(1)}, f32[32]{0:T(128)S(1)}, u32[]{:S(2)}, u32[]{:S(2)}) collective-permute-start(f32[32]{0:T(128)S(1)} %add.16), channel_id=1, source_target_pairs={{0,4},{1,5},{2,6},{3,7},{4,0},{5,1},{6,2},{7,3},{8,12},{9,13},{10,... | collective-permute-start | bytes 392 | tf_op jit(solution)/shard_map/ppermute | solution.py:749
  38.5 3.5 %collective-permute-start.9 = (f32[32]{0:T(128)S(1)}, f32[32]{0:T(128)S(1)}, u32[]{:S(2)}, u32[]{:S(2)}) collective-permute-start(f32[32]{0:T(128)S(1)} %add.17), channel_id=1, source_target_pairs={{0,8},{8,0},{16,24},{24,16},{1,9},{9,1},{17,25},{25,17},{2,10},{10... | collective-permute-start | bytes 392 | tf_op jit(solution)/shard_map/ppermute | solution.py:749
  42.0 4.4 %collective-permute-start.10 = (f32[32]{0:T(128)S(1)}, f32[32]{0:T(128)S(1)}, u32[]{:S(2)}, u32[]{:S(2)}) collective-permute-start(f32[32]{0:T(128)S(1)} %add.18), channel_id=1, source_target_pairs={{0,16},{8,24},{16,0},{24,8},{1,17},{9,25},{17,1},{25,9},{2,18},{10... | collective-permute-start | bytes 392 | tf_op jit(solution)/shard_map/ppermute | solution.py:749

commit v3 on v2

--- a/solution.py
+++ b/solution.py
@@ -686,7 +686,7 @@
         [jnp.sum(sums_v[m], axis=0, keepdims=True) for m in range(count)], axis=0
     )
     share_ref[...] = lax.dot_general(
-        jnp.ones((8, 128), jnp.float32),
+        jnp.ones((share_ref.shape[0], 128), jnp.float32),
         rows,
         (((1,), (1,)), ((), ())),
         precision=lax.Precision.HIGHEST,
@@ -712,7 +712,7 @@
             jax.ShapeDtypeStruct(adjg.shape, jnp.float32),
             jax.ShapeDtypeStruct(adjf.shape, jnp.float32),
             jax.ShapeDtypeStruct(adjg.shape, jnp.float32),
-            jax.ShapeDtypeStruct((8, count), jnp.float32),
+            jax.ShapeDtypeStruct((lax.axis_size(("gx", "gy")), count), jnp.float32),
         ],
         input_output_aliases={14: 0, 15: 1, 16: 2, 17: 3},
         scratch_shapes=[
@@ -739,16 +739,6 @@
 
 def ring(count, step):
     return [(i, (i + step) % count) for i in range(count)]
-
-
-def butterfly(value):
-    for axis in ("gy", "gx"):
-        count = lax.axis_size(axis)
-        step = 1
-        while step < count:
-            value = value + lax.ppermute(value, axis, [(i, i ^ step) for i in range(count)])
-            step *= 2
-    return value
 
 
 def on_device(flow, field, adj_flow_in, adj_field_in, profile, strengths, wall, magnet):
@@ -775,7 +765,7 @@
         cornerright, profile, table, wall, magnet, partial, newf, newg, outf, outg,
     )
     cells = flow.shape[1] * around * flow.shape[2] * across * flow.shape[3]
-    totals = butterfly(share[0])
+    totals = jnp.sum(lax.all_to_all(share, ("gx", "gy"), 0, 0, tiled=True), axis=0)
     return (newf, newg, outf, outg, totals / math.sqrt(cells / count))
 
 

time: 47.2 us -> 41.6 us (0.88)
  waiting for transfers between devices: 13.1 us -> 1.4 us
  blocking collectives: 0 us -> 10.5 us
  starting transfers between devices: 16.5 us -> 12 us
    ppermute x5 -> x0, waiting for transfers between devices: 11.7 us -> none  [butterfly(): lax.ppermute(value, axis, [(i, i ^ step) for i in range(count)])]
    all_to_all x0 -> x1, blocking collectives: none -> 10.5 us  [on_device(): lax.all_to_all(share, ('gx', 'gy'), 0, 0, tiled=True)]
    ppermute x5 -> x0, starting transfers between devices: 4.52 us -> none  [butterfly(): lax.ppermute(value, axis, [(i, i ^ step) for i in range(count)])]
  transfers between devices with their start and end apart: 11 -> 6, of which waited for: 6 -> 1; matrix products, arithmetic and copies ran while one was open for 0% -> 0% of each run, Pallas kernels for 13% -> 15%
where the time goes in v3:
time: 41.6 us; the launch traced here: 41.4 us
  Pallas kernels  16.1 us (39%)
  starting transfers between devices  12 us (29%)
  blocking collectives  10.5 us (25%)
  waiting for transfers between devices  1.4 us (3%)
  between operations  0.75 us (2%)
  other arithmetic  0.57 us (1%)
    all_to_all x1, blocking collectives, on_device(): lax.all_to_all(share, ('gx', 'gy'), 0, 0, tiled=True)  10.5 us
    pallas_call x1, Pallas kernels, inner_call(): pl.pallas_call(inner_kernel, in_specs=[ANY, ANY, ANY, ANY, ANY, VMEM, VME...  6.19 us
    pallas_call x1, Pallas kernels, collide_call(): pl.pallas_call(functools.partial(collide_kernel, planes), grid=(grid,), i...  6 us
    pallas_call x1, Pallas kernels, outer_call(): pl.pallas_call(outer_kernel, in_specs=[ANY] * 5 + [VMEM] * 9 + [ANY] * 4,...  3.93 us
    ppermute x1, starting transfers between devices, on_device(): second = lax.ppermute(mine2, 'gy', between)  3.56 us
    ppermute x1, starting transfers between devices, on_device(): fromright = lax.ppermute(left, 'gx', ring(around, -1))  2.25 us
    ppermute x1, starting transfers between devices, on_device(): cornerright = lax.ppermute(corner_l, 'gx', ring(around, -1))  2.09 us
    ppermute x1, starting transfers between devices, on_device(): cornerleft = lax.ppermute(corner_r, 'gx', ring(around, 1))  1.97 us
  transfers between devices with their start and end apart: 6, of which 1 were waited for; matrix products, arithmetic and copies ran while one was open for 0% of the time, Pallas kernels for 15%

profile of v3, /device:TPU:0, one launch (start us, length us, event | category | flops | bytes accessed | tf_op | source)
XLA Modules:
  0.0 41.4 jit_solution(9653209820744921592)
XLA Ops:
  0.6 0.0 copy-start
  0.6 0.0 copy-start.1
  0.7 0.0 copy-start.2
  0.7 0.0 copy-start.3
  0.7 0.0 copy-start.4
  0.7 6.0 %collide.1 = (f32[26,8,8,512]{3,2,1,0:T(8,128)}, f32[13,8,512]{2,1,0:T(8,128)}, f32[13,8,512]{2,1,0:T(8,128)}, f32[13,8,512]{2,1,0:T(8,128)}, f32[13,8,512]{2,1,0:T(8,128)}) custom-call(f32[19,8,8,512]{3,2,1,0:T(8,128)} %flow_ref.1, f32[7,8,8,512]{3,2,1,0:T(8,128)} %field_ref.1, f32[19,8,8,512]{3,2,1,0:T(8,128)} %adjf_ref.5, f32[7,8,8,512]{3,2,1,0:T(8,128)} %adjg_ref.5, ...), custom_call_target="tpu_custom_call" | custom-call | tf_op jit(solution)/shard_map/collide/pallas_call | solution.py:197
  6.7 0.5 %collective-permute-start = (f32[13,8,512]{2,1,0:T(8,128)}, f32[13,8,512]{2,1,0:T(8,128)S(1)}, u32[]{:S(2)}, u32[]{:S(2)}) collective-permute-start(f32[13,8,512]{2,1,0:T(8,128)} %get-tuple-element.23), channel_id=1, source_target_pairs={{0,1},{1,0},{2,3},{3,2},{4,5},{5,4},{6,7},{7,6},{8,9},{9,8},{10,11... | collective-permute-start | bytes 638984 | tf_op jit(solution)/shard_map/ppermute | solution.py:754
  7.2 3.6 %collective-permute-start.1 = (f32[13,8,512]{2,1,0:T(8,128)}, f32[13,8,512]{2,1,0:T(8,128)S(1)}, u32[]{:S(2)}, u32[]{:S(2)}) collective-permute-start(f32[13,8,512]{2,1,0:T(8,128)} %get-tuple-element.24), channel_id=1, source_target_pairs={{0,7},{1,2},{2,1},{3,4},{4,3},{5,6},{6,5},{7,0},{8,15},{9,10},{10,... | collective-permute-start | bytes 638984 | tf_op jit(solution)/shard_map/ppermute | solution.py:753
  10.8 1.6 %collective-permute-start.2 = (f32[13,8,512]{2,1,0:T(8,128)}, f32[13,8,512]{2,1,0:T(8,128)S(1)}, u32[]{:S(2)}, u32[]{:S(2)}) collective-permute-start(f32[13,8,512]{2,1,0:T(8,128)} %get-tuple-element.25), channel_id=1, source_target_pairs={{0,8},{8,16},{16,24},{24,0},{1,9},{9,17},{17,25},{25,1},{2,10},{10... | collective-permute-start | bytes 638984 | tf_op jit(solution)/shard_map/ppermute | solution.py:755
  12.3 2.2 %collective-permute-start.3 = (f32[13,8,512]{2,1,0:T(8,128)}, f32[13,8,512]{2,1,0:T(8,128)S(1)}, u32[]{:S(2)}, u32[]{:S(2)}) collective-permute-start(f32[13,8,512]{2,1,0:T(8,128)} %get-tuple-element.26), channel_id=1, source_target_pairs={{0,24},{8,0},{16,8},{24,16},{1,25},{9,1},{17,9},{25,17},{2,26},{10... | collective-permute-start | bytes 638984 | tf_op jit(solution)/shard_map/ppermute | solution.py:756
  14.6 0.0 collective-permute-done.first_ref
  14.6 1.4 %collective-permute-done.1.second_ref = f32[13,8,512]{2,1,0:T(8,128)S(1)} collective-permute-done((f32[13,8,512]{2,1,0:T(8,128)}, f32[13,8,512]{2,1,0:T(8,128)S(1)}, u32[]{:S(2)}, u32[]{:S(2)}) %collective-permute-start.1) | collective-permute-done | bytes 213024 | tf_op jit(solution)/shard_map/ppermute | solution.py:753
  16.0 2.0 %collective-permute-start.4 = (f32[8,512]{1,0:T(8,128)S(1)}, f32[8,512]{1,0:T(8,128)S(1)}, u32[]{:S(2)}, u32[]{:S(2)}) collective-permute-start(f32[8,512]{1,0:T(8,128)S(1)} %get-tuple-element.27), channel_id=1, source_target_pairs={{0,8},{8,16},{16,24},{24,0},{1,9},{9,17},{17,25},{25,1},{2,10},{10... | collective-permute-start | bytes 49160 | tf_op jit(solution)/shard_map/ppermute | solution.py:758
  18.0 2.1 %collective-permute-start.5 = (f32[8,512]{1,0:T(8,128)S(1)}, f32[8,512]{1,0:T(8,128)S(1)}, u32[]{:S(2)}, u32[]{:S(2)}) collective-permute-start(f32[8,512]{1,0:T(8,128)S(1)} %get-tuple-element.28), channel_id=1, source_target_pairs={{0,24},{8,0},{16,8},{24,16},{1,25},{9,1},{17,9},{25,17},{2,26},{10... | collective-permute-start | bytes 49160 | tf_op jit(solution)/shard_map/ppermute | solution.py:759
  20.1 0.0 copy-done.2
  20.1 6.2 %inner.1 = (f32[19,8,8,512]{3,2,1,0:T(8,128)}, f32[7,8,8,512]{3,2,1,0:T(8,128)}, f32[19,8,8,512]{3,2,1,0:T(8,128)}, f32[7,8,8,512]{3,2,1,0:T(8,128)}, f32[32,8,128]{2,1,0:T(8,128)S(1)}) custom-call(f32[26,8,8,512]{3,2,1,0:T(8,128)} %get-tuple-element.22.post_ref, f32[19,8,8,512]{3,2,1,0:T(8,128)} %adjf_ref.5, f32[7,8,8,512]{3,2,1,0:T(8,128)S(1)} %copy-done, ...), custom_call_target="tpu_custom_call" | custom-call | flops 22937600 | bytes 13631488 | tf_op jit(solution)/shard_map/inner/pallas_call | solution.py:564
  26.3 0.0 collective-permute-done.2.fromleft_ref
  26.3 0.0 collective-permute-done.3.fromright_ref
  26.3 0.0 collective-permute-done.4.cornerleft_ref
  26.3 0.0 collective-permute-done.5.cornerright_ref
  26.3 3.9 %outer.1 = (f32[19,8,8,512]{3,2,1,0:T(8,128)}, f32[7,8,8,512]{3,2,1,0:T(8,128)}, f32[19,8,8,512]{3,2,1,0:T(8,128)}, f32[7,8,8,512]{3,2,1,0:T(8,128)}, f32[32,32]{1,0:T(8,128)S(1)}) custom-call(f32[26,8,8,512]{3,2,1,0:T(8,128)} %get-tuple-element.22.post_ref, ...), custom_call_target="tpu_custom_call", output_to_operand_aliasing={{0}: (14, {}), {1}: (15, {}), {2}: (16, {}), {3}: (17, {})} | custom-call | tf_op jit(solution)/shard_map/outer/pallas_call | solution.py:706
  30.3 10.5 %all_to_all.9 = f32[32,1,32]{2,1,0:T(1,128)S(1)} all-to-all(f32[32,1,32]{2,1,0:T(1,128)S(1)} %bitcast.4), channel_id=1, replica_groups=mesh['gx'=4,'gy'=8] {'gx','gy'}, dimensions={0} | all-to-all | bytes 8192 | tf_op jit(solution)/shard_map/all_to_all | solution.py:768
  40.8 0.1 reduce_sum.9
  40.8 0.5 %broadcast_multiply_fusion = f32[32]{0:T(128)} fusion(f32[32]{0:T(128)S(1)} %reduce_sum.9), kind=kLoop, calls=%fused_computation | loop fusion | flops 32 | bytes 256 | tf_op jit(solution)/shard_map/div | solution.py:769
  (5 shorter events, 0.0 us)
Async XLA Ops:
  0.6 19.4 %copy-start = (f32[7,8,8,512]{3,2,1,0:T(8,128)S(1)}, f32[7,8,8,512]{3,2,1,0:T(8,128)}, u32[]{:S(2)}) copy-start(f32[7,8,8,512]{3,2,1,0:T(8,128)} %adjg_ref.5) | copy-start | bytes 2752516
  0.6 19.4 %copy-start.1 = (f32[8,8,512]{2,1,0:T(8,128)S(1)}, f32[8,8,512]{2,1,0:T(8,128)}, u32[]{:S(2)}) copy-start(f32[8,8,512]{2,1,0:T(8,128)} %profile_ref.5) | copy-start | bytes 393220
  0.7 19.4 %copy-start.2 = (s32[8,8,512]{2,1,0:T(8,128)S(1)}, s32[8,8,512]{2,1,0:T(8,128)}, u32[]{:S(2)}) copy-start(s32[8,8,512]{2,1,0:T(8,128)} %wall_ref.5) | copy-start | bytes 393220
  0.7 19.4 %copy-start.3 = (s32[8,8,512]{2,1,0:T(8,128)S(1)}, s32[8,8,512]{2,1,0:T(8,128)}, u32[]{:S(2)}) copy-start(s32[8,8,512]{2,1,0:T(8,128)} %magnet_ref.5) | copy-start | bytes 393220
  0.7 19.4 %copy-start.4 = (f32[32]{0:T(128)S(1)}, f32[32]{0:T(128)}, u32[]{:S(2)}) copy-start(f32[32]{0:T(128)} %param.13) | copy-start | bytes 388
  6.7 7.9 %collective-permute-start = (f32[13,8,512]{2,1,0:T(8,128)}, f32[13,8,512]{2,1,0:T(8,128)S(1)}, u32[]{:S(2)}, u32[]{:S(2)}) collective-permute-start(f32[13,8,512]{2,1,0:T(8,128)} %get-tuple-element.23), channel_id=1, source_target_pairs={{0,1},{1,0},{2,3},{3,2},{4,5},{5,4},{6,7},{7,6},{8,9},{9,8},{10,11... | collective-permute-start | bytes 638984 | tf_op jit(solution)/shard_map/ppermute | solution.py:754
  7.2 8.8 %collective-permute-start.1 = (f32[13,8,512]{2,1,0:T(8,128)}, f32[13,8,512]{2,1,0:T(8,128)S(1)}, u32[]{:S(2)}, u32[]{:S(2)}) collective-permute-start(f32[13,8,512]{2,1,0:T(8,128)} %get-tuple-element.24), channel_id=1, source_target_pairs={{0,7},{1,2},{2,1},{3,4},{4,3},{5,6},{6,5},{7,0},{8,15},{9,10},{10,... | collective-permute-start | bytes 638984 | tf_op jit(solution)/shard_map/ppermute | solution.py:753
  10.8 15.5 %collective-permute-start.2 = (f32[13,8,512]{2,1,0:T(8,128)}, f32[13,8,512]{2,1,0:T(8,128)S(1)}, u32[]{:S(2)}, u32[]{:S(2)}) collective-permute-start(f32[13,8,512]{2,1,0:T(8,128)} %get-tuple-element.25), channel_id=1, source_target_pairs={{0,8},{8,16},{16,24},{24,0},{1,9},{9,17},{17,25},{25,1},{2,10},{10... | collective-permute-start | bytes 638984 | tf_op jit(solution)/shard_map/ppermute | solution.py:755
  12.3 14.0 %collective-permute-start.3 = (f32[13,8,512]{2,1,0:T(8,128)}, f32[13,8,512]{2,1,0:T(8,128)S(1)}, u32[]{:S(2)}, u32[]{:S(2)}) collective-permute-start(f32[13,8,512]{2,1,0:T(8,128)} %get-tuple-element.26), channel_id=1, source_target_pairs={{0,24},{8,0},{16,8},{24,16},{1,25},{9,1},{17,9},{25,17},{2,26},{10... | collective-permute-start | bytes 638984 | tf_op jit(solution)/shard_map/ppermute | solution.py:756
  16.0 10.3 %collective-permute-start.4 = (f32[8,512]{1,0:T(8,128)S(1)}, f32[8,512]{1,0:T(8,128)S(1)}, u32[]{:S(2)}, u32[]{:S(2)}) collective-permute-start(f32[8,512]{1,0:T(8,128)S(1)} %get-tuple-element.27), channel_id=1, source_target_pairs={{0,8},{8,16},{16,24},{24,0},{1,9},{9,17},{17,25},{25,1},{2,10},{10... | collective-permute-start | bytes 49160 | tf_op jit(solution)/shard_map/ppermute | solution.py:758
  18.0 8.3 %collective-permute-start.5 = (f32[8,512]{1,0:T(8,128)S(1)}, f32[8,512]{1,0:T(8,128)S(1)}, u32[]{:S(2)}, u32[]{:S(2)}) collective-permute-start(f32[8,512]{1,0:T(8,128)S(1)} %get-tuple-element.28), channel_id=1, source_target_pairs={{0,24},{8,0},{16,8},{24,16},{1,25},{9,1},{17,9},{25,17},{2,26},{10... | collective-permute-start | bytes 49160 | tf_op jit(solution)/shard_map/ppermute | solution.py:759

commit v4 on v3

--- a/solution.py
+++ b/solution.py
@@ -47,6 +47,10 @@
 SLOTS = 13
 MASK = 12
 
+COLLIDE_VMEM = 48 << 20
+INNER_VMEM = 42 << 20
+OUTER_VMEM = 42 << 20
+
 
 def weight(i):
     return W1 if i <= 6 else W2
@@ -86,33 +90,52 @@
     return out
 
 
+def start_all(copies):
+    for c in copies:
+        c.start()
+
+
+def wait_all(copies):
+    for c in copies:
+        c.wait()
+
+
 def collide_kernel(
-    planes,
-    flow_ref,
-    field_ref,
-    adjf_ref,
-    adjg_ref,
-    profile_ref,
-    strengths_ref,
-    wall_ref,
-    magnet_ref,
-    post_ref,
-    first_ref,
-    second_ref,
-    right_ref,
+    flow_ref, field_ref, adjf_ref, adjg_ref, profile_ref, strengths_ref, wall_ref, magnet_ref,
+    post_ref, adj_ref, fluid_ref, bcell_ref, profile_v, magnet_v, first_ref, second_ref, right_ref,
     left_ref,
+    flow_v, field_v, wall_v, plane_sem, adj_sem,
 ):
-    step = pl.program_id(0)
-    steps = pl.num_programs(0)
+    sx, sy = fluid_ref.shape[:2]
     odd = lax.rem(lax.axis_index("gy"), 2)
+
+    def loads(x):
+        pairs = (
+            (wall_ref.at[x], wall_v.at[x]),
+            (magnet_ref.at[x], magnet_v.at[x]),
+            (profile_ref.at[x], profile_v.at[x]),
+            (flow_ref.at[:, x], flow_v.at[:, x]),
+            (field_ref.at[:, x], field_v.at[:, x]),
+        )
+        return [pltpu.make_async_copy(a, b, plane_sem.at[n, x]) for n, (a, b) in enumerate(pairs)]
+
+    for x in range(sx):
+        start_all(loads(x))
+    adj_loads = [
+        pltpu.make_async_copy(adjf_ref, adj_ref.at[pl.ds(0, NF)], adj_sem.at[0]),
+        pltpu.make_async_copy(adjg_ref, adj_ref.at[pl.ds(NF, NG)], adj_sem.at[1]),
+    ]
+    start_all(adj_loads)
     table = lane_table(strengths_ref)
-    last = flow_ref.shape[2] - 1
-
-    for p in range(planes):
-        fluid = 1.0 - wall_ref[p].astype(jnp.float32)
-        bcell = gather_strength(table, magnet_ref[p]) * profile_ref[p]
-        f = [flow_ref[i, p] for i in range(NF)]
-        g = [field_ref[k, p] for k in range(NG)]
+
+    def body(x, carry):
+        wait_all(loads(x))
+        fluid = 1.0 - wall_v[x].astype(jnp.float32)
+        bcell = gather_strength(table, magnet_v[x]) * profile_v[x]
+        fluid_ref[x] = fluid
+        bcell_ref[x] = bcell
+        f = [flow_v[i, x] for i in range(NF)]
+        g = [field_v[k, x] for k in range(NG)]
         even = {i: f[i] + f[i + 1] for i in FIRST}
         diff = {i: f[i] - f[i + 1] for i in FIRST}
         rho = f[0] + (1.0 - fluid)
@@ -127,7 +150,7 @@
         force = (COUPLE * bcell) * current
         vx = ux + TAU_PLUS * force * inv
         base = 1.0 - 1.5 * (vx * vx + uy * uy + uz * uz)
-        post_ref[0, p] = f[0] - 2.0 * PLUS * (f[0] - (W0 * rho) * base)
+        post_ref[0, x] = f[0] - 2.0 * PLUS * (f[0] - (W0 * rho) * base)
         rho1, rho2 = W1 * rho, W2 * rho
         for i in FIRST:
             wr = rho1 if i <= 6 else rho2
@@ -136,92 +159,65 @@
             no = diff[i] - (6.0 * wr) * a
             ne = PLUS * ne
             no = MINUS * no
-            post_ref[i, p] = f[i] - ne - no
-            post_ref[i + 1, p] = f[i + 1] - ne + no
+            post_ref[i, x] = f[i] - ne - no
+            post_ref[i + 1, x] = f[i + 1] - ne + no
         common = bval + (SOURCE * bcell) * shear
         slope = 4.0 * bval
-        post_ref[NF, p] = V0 * common
+        post_ref[NF, x] = V0 * common
         for k, u in ((1, ux), (3, uy), (5, uz)):
             su = slope * u
-            post_ref[NF + k, p] = V1 * (common + su)
-            post_ref[NF + k + 1, p] = V1 * (common - su)
-
-        x = step * planes + p
+            post_ref[NF + k, x] = V1 * (common + su)
+            post_ref[NF + k + 1, x] = V1 * (common - su)
+        return carry
+
+    lax.fori_loop(0, sx, body, 0)
+
+    wait_all(adj_loads)
+
+    def pack(x, carry):
         here = pl.ds(x, 1)
-
-        def adj_row(i, row):
-            return adjf_ref[i, p, pl.ds(row, 1), :]
-
         for out, side in ((first_ref, odd), (second_ref, 1 - odd)):
-            row = (1 - side) * last
+            line = pl.ds((1 - side) * (sy - 1), 1)
             for s in range(6):
                 up, down = UP[s], DOWN[s]
-                out[s, here, :] = post_ref[up + side * (down - up), p, pl.ds(row, 1), :]
-                if up < NF:
-                    line = adjf_ref[down + side * (up - down), p, pl.ds(row, 1), :]
-                else:
-                    line = adjg_ref[down - NF + side * (up - down), p, pl.ds(row, 1), :]
-                out[6 + s, here, :] = line
-            out[MASK, here, :] = 1.0 - wall_ref[p, pl.ds(row, 1), :].astype(jnp.float32)
-
-    def pack_x(out, p, posts, adjs):
+                out[s, here, :] = post_ref[up + side * (down - up), x, line, :]
+                out[6 + s, here, :] = adj_ref[down + side * (up - down), x, line, :]
+            out[MASK, here, :] = fluid_ref[x, line, :]
+        return carry
+
+    lax.fori_loop(0, sx, pack, 0)
+    for out, x, posts, adjs in ((left_ref, 0, LEFT, RIGHT), (right_ref, sx - 1, RIGHT, LEFT)):
         for s in range(6):
-            out[s] = post_ref[posts[s], p]
-            j = adjs[s]
-            out[6 + s] = adjf_ref[j, p] if j < NF else adjg_ref[j - NF, p]
-        out[MASK] = 1.0 - wall_ref[p].astype(jnp.float32)
-
-    @pl.when(step == 0)
-    def _():
-        pack_x(left_ref, 0, LEFT, RIGHT)
-
-    @pl.when(step == steps - 1)
-    def _():
-        pack_x(right_ref, planes - 1, RIGHT, LEFT)
-
-
-def collide_call(flow, field, adjf, adjg, profile, strengths, wall, magnet, planes=2):
+            out[s] = post_ref[posts[s], x]
+            out[6 + s] = adj_ref[adjs[s], x]
+        out[MASK] = fluid_ref[x]
+
+
+ANY = pl.BlockSpec(memory_space=pl.ANY)
+VMEM = pl.BlockSpec(memory_space=pltpu.VMEM)
+
+
+def collide_call(flow, field, adjf, adjg, profile, strengths, wall, magnet):
     sx, sy, sz = profile.shape
-    grid = sx // planes
-
-    def stack(n):
-        return pl.BlockSpec((n, planes, sy, sz), lambda x: (0, x, 0, 0))
-
-    one = pl.BlockSpec((planes, sy, sz), lambda x: (x, 0, 0))
-
-    def whole(*shape):
-        return pl.BlockSpec(shape, lambda x: (0,) * len(shape))
-
-    rows = jax.ShapeDtypeStruct((SLOTS, sx, sz), jnp.float32)
-    faces = jax.ShapeDtypeStruct((SLOTS, sy, sz), jnp.float32)
+    full = pltpu.VMEM((NP, sx, sy, sz), jnp.float32)
+    cells = pltpu.VMEM((sx, sy, sz), jnp.float32)
+    names = pltpu.VMEM((sx, sy, sz), jnp.int32)
+    rows = pltpu.VMEM((SLOTS, sx, sz), jnp.float32)
+    faces = pltpu.VMEM((SLOTS, sy, sz), jnp.float32)
+    dma = pltpu.SemaphoreType.DMA
     return pl.pallas_call(
-        functools.partial(collide_kernel, planes),
-        grid=(grid,),
-        in_specs=[
-            stack(NF),
-            stack(NG),
-            stack(NF),
-            stack(NG),
-            one,
-            whole(*strengths.shape),
-            one,
-            one,
+        collide_kernel,
+        in_specs=[ANY, ANY, ANY, ANY, ANY, VMEM, ANY, ANY],
+        out_specs=[VMEM] * 10,
+        out_shape=[full, full, cells, cells, cells, names, rows, rows, faces, faces],
+        scratch_shapes=[
+            pltpu.VMEM(flow.shape, jnp.float32),
+            pltpu.VMEM(field.shape, jnp.float32),
+            names,
+            dma((5, sx)),
+            dma((2,)),
         ],
-        out_specs=[
-            stack(NP),
-            whole(*rows.shape),
-            whole(*rows.shape),
-            whole(*faces.shape),
-            whole(*faces.shape),
-        ],
-        out_shape=[
-            jax.ShapeDtypeStruct((NP, sx, sy, sz), jnp.float32),
-            rows,
-            rows,
-            faces,
-            faces,
-        ],
-        compiler_params=pltpu.CompilerParams(vmem_limit_bytes=62 << 20),
+        compiler_params=pltpu.CompilerParams(vmem_limit_bytes=COLLIDE_VMEM),
         name="collide",
     )(flow, field, adjf, adjg, profile, strengths, wall, magnet)
 
@@ -436,108 +432,70 @@
         sums_ref[m] = sums_ref[m] + part
 
 
-def edges():
+def halo_slot(kind, i, dy):
+    names = (UP, DOWN) if (dy == -1) == (kind == 0) else (DOWN, UP)
+    return names[0].index(i) + 6 * kind
+
+
+def face_slot(kind, i, dx):
+    names = RIGHT if (dx == -1) == (kind == 0) else LEFT
+    return names.index(i) + 6 * kind
+
+
+def load_halo(first_ref, second_ref, halo_ref):
+    odd = lax.rem(lax.axis_index("gy"), 2)
+    halo_ref[1 - odd] = first_ref[...]
+    halo_ref[odd] = second_ref[...]
     here = lax.axis_index("gy")
     keep_low = jnp.where(here == 0, 0.0, 1.0)
     keep_high = jnp.where(here == lax.axis_size("gy") - 1, 0.0, 1.0)
-    return keep_low, keep_high
-
-
-def halo_slot(kind, i, dy):
-    names = (UP, DOWN) if (dy == -1) == (kind == 0) else (DOWN, UP)
-    return names[0].index(i) + 6 * kind
-
-
-def face_slot(kind, i, dx):
-    names = RIGHT if (dx == -1) == (kind == 0) else LEFT
-    return names.index(i) + 6 * kind
-
-
-def start_all(copies):
-    for c in copies:
-        c.start()
-
-
-def load_halo(first_ref, second_ref, halo_ref, sem):
-    odd = lax.rem(lax.axis_index("gy"), 2)
-    return [
-        pltpu.make_async_copy(first_ref, halo_ref.at[1 - odd], sem.at[0]),
-        pltpu.make_async_copy(second_ref, halo_ref.at[odd], sem.at[1]),
-    ]
-
-
-def mask_halo(halo_ref):
-    keep_low, keep_high = edges()
     halo_ref[0, MASK] = halo_ref[0, MASK] * keep_low
     halo_ref[1, MASK] = halo_ref[1, MASK] * keep_high
+    return keep_low, keep_high
+
+
+def plane_stores(n, x, new_v, out_v, newf_ref, newg_ref, outf_ref, outg_ref, sem):
+    pairs = (
+        (new_v.at[pl.ds(0, NF), n], newf_ref.at[:, x]),
+        (new_v.at[pl.ds(NF, NG), n], newg_ref.at[:, x]),
+        (out_v.at[pl.ds(0, NF), n], outf_ref.at[:, x]),
+        (out_v.at[pl.ds(NF, NG), n], outg_ref.at[:, x]),
+    )
+    return [pltpu.make_async_copy(a, b, sem.at[k, n]) for k, (a, b) in enumerate(pairs)]
 
 
 def inner_kernel(
-    post_ref, adjf_ref, adjg_ref, first_ref, second_ref, profile_ref, strengths_ref, wall_ref,
-    magnet_ref,
+    post_ref, adj_ref, fluid_ref, bcell_ref, first_ref, second_ref, profile_ref, magnet_ref,
     newf_ref, newg_ref, outf_ref, outg_ref, sums_ref,
-    post_v, adj_v, new_v, out_v, halo_v, near_v,
-    post_sem, adjf_sem, adjg_sem, halo_sem, newf_sem, newg_sem, outf_sem, outg_sem,
+    new_v, out_v, halo_v, near_v, store_sem,
 ):
-    sx = post_v.shape[1]
+    sx = fluid_ref.shape[0]
     count = sums_ref.shape[0]
 
-    def loads(x):
-        return [
-            pltpu.make_async_copy(post_ref.at[:, x], post_v.at[:, x], post_sem.at[x]),
-            pltpu.make_async_copy(adjf_ref.at[:, x], adj_v.at[pl.ds(0, NF), x], adjf_sem.at[x]),
-            pltpu.make_async_copy(adjg_ref.at[:, x], adj_v.at[pl.ds(NF, NG), x], adjg_sem.at[x]),
-        ]
-
     def stores(x):
-        return [
-            pltpu.make_async_copy(new_v.at[pl.ds(0, NF), x], newf_ref.at[:, x], newf_sem.at[x]),
-            pltpu.make_async_copy(new_v.at[pl.ds(NF, NG), x], newg_ref.at[:, x], newg_sem.at[x]),
-            pltpu.make_async_copy(out_v.at[pl.ds(0, NF), x], outf_ref.at[:, x], outf_sem.at[x]),
-            pltpu.make_async_copy(out_v.at[pl.ds(NF, NG), x], outg_ref.at[:, x], outg_sem.at[x]),
-        ]
-
-    def finish(copies):
-        for c in copies:
-            c.wait()
-
-    halo = load_halo(first_ref, second_ref, halo_v, halo_sem)
-    start_all(halo)
-    for x in range(sx):
-        start_all(loads(x))
+        return plane_stores(
+            x, x, new_v, out_v, newf_ref, newg_ref, outf_ref, outg_ref, store_sem
+        )
+
     sums_ref[...] = jnp.zeros_like(sums_ref)
-    table = lane_table(strengths_ref)
-    finish(halo)
-    mask_halo(halo_v)
-    finish(loads(0))
-    finish(loads(1))
+    load_halo(first_ref, second_ref, halo_v)
 
     def body(x, carry):
-        finish(loads(x + 1))
-
-        def side(dy):
-            return 0 if dy == -1 else 1
-
         def row_of(slot, dx, dy):
-            return halo_v[side(dy), slot, pl.ds(x + dx, 1), :]
-
-        def mask(dx):
-            return 1.0 - wall_ref[x + dx].astype(jnp.float32)
-
-        magnet = magnet_ref[x]
-        profile = profile_ref[x]
+            return halo_v[0 if dy == -1 else 1, slot, pl.ds(x + dx, 1), :]
+
         plane_step(
             x,
-            lambda i, dx: post_v[i, x + dx],
+            lambda i, dx: post_ref[i, x + dx],
             lambda i, dx, dy: row_of(halo_slot(0, i, dy), dx, dy),
-            lambda i, dx: adj_v[i, x + dx],
+            lambda i, dx: adj_ref[i, x + dx],
             lambda i, dx, dy: row_of(halo_slot(1, i, dy), dx, dy),
-            mask,
+            lambda dx: fluid_ref[x + dx],
             lambda dx, dy: row_of(MASK, dx, dy),
-            mask(0),
-            gather_strength(table, magnet) * profile,
-            profile,
-            magnet,
+            fluid_ref[x],
+            bcell_ref[x],
+            profile_ref[x],
+            magnet_ref[x],
             near_v,
             new_v,
             out_v,
@@ -549,95 +507,56 @@
 
     lax.fori_loop(1, sx - 1, body, 0)
     for x in range(1, sx - 1):
-        finish(stores(x))
-
-
-ANY = pl.BlockSpec(memory_space=pl.ANY)
-VMEM = pl.BlockSpec(memory_space=pltpu.VMEM)
-
-
-def inner_call(post, adjf, adjg, first, second, profile, strengths, wall, magnet):
+        wait_all(stores(x))
+
+
+def inner_call(post, adj, fluid, bcell, first, second, profile, magnet, count):
     sx, sy, sz = profile.shape
-    count = strengths.shape[1]
     full = pltpu.VMEM((NP, sx, sy, sz), jnp.float32)
-    dma = pltpu.SemaphoreType.DMA
+    flow = jax.ShapeDtypeStruct((NF, sx, sy, sz), jnp.float32)
+    field = jax.ShapeDtypeStruct((NG, sx, sy, sz), jnp.float32)
     return pl.pallas_call(
         inner_kernel,
-        in_specs=[ANY, ANY, ANY, ANY, ANY, VMEM, VMEM, VMEM, VMEM],
+        in_specs=[VMEM] * 8,
         out_specs=[ANY, ANY, ANY, ANY, VMEM],
-        out_shape=[
-            jax.ShapeDtypeStruct(adjf.shape, jnp.float32),
-            jax.ShapeDtypeStruct(adjg.shape, jnp.float32),
-            jax.ShapeDtypeStruct(adjf.shape, jnp.float32),
-            jax.ShapeDtypeStruct(adjg.shape, jnp.float32),
-            jax.ShapeDtypeStruct((count, 8, 128), jnp.float32),
-        ],
+        out_shape=[flow, field, flow, field, pltpu.VMEM((count, 8, 128), jnp.float32)],
         scratch_shapes=[
-            full,
-            full,
             full,
             full,
             pltpu.VMEM((2, SLOTS, sx, sz), jnp.float32),
             pltpu.VMEM((18, sy, sz), jnp.float32),
-            dma((sx,)),
-            dma((sx,)),
-            dma((sx,)),
-            dma((2,)),
-            dma((sx,)),
-            dma((sx,)),
-            dma((sx,)),
-            dma((sx,)),
+            pltpu.SemaphoreType.DMA((4, sx)),
         ],
-        compiler_params=pltpu.CompilerParams(vmem_limit_bytes=51 << 20),
+        compiler_params=pltpu.CompilerParams(vmem_limit_bytes=INNER_VMEM),
         cost_estimate=pl.CostEstimate(
             flops=700 * sx * sy * sz, bytes_accessed=16 * NP * sx * sy * sz, transcendentals=0
         ),
         name="inner",
-    )(post, adjf, adjg, first, second, profile, strengths, wall, magnet)
+    )(post, adj, fluid, bcell, first, second, profile, magnet)
 
 
 def outer_kernel(
-    post_ref, adjf_ref, adjg_ref, first_ref, second_ref, fromleft_ref, fromright_ref,
-    cornerleft_ref, cornerright_ref, profile_ref, strengths_ref, wall_ref, magnet_ref,
+    post_ref, adj_ref, fluid_ref, bcell_ref, first_ref, second_ref, fromleft_ref, fromright_ref,
+    cornerleft_ref, cornerright_ref, profile_ref, magnet_ref,
     partial_ref, newf_in, newg_in, outf_in, outg_in,
     newf_ref, newg_ref, outf_ref, outg_ref, share_ref,
-    post_v, adj_v, new_v, out_v, halo_v, near_v, sums_v,
-    post_sem, adjf_sem, adjg_sem, halo_sem, store_sem,
+    new_v, out_v, halo_v, near_v, sums_v, store_sem,
 ):
     del newf_in, newg_in, outf_in, outg_in
-    sx = wall_ref.shape[0]
+    sx = fluid_ref.shape[0]
     count = sums_v.shape[0]
-    from_planes = (0, 1, sx - 2, sx - 1)
-    loads = []
-    for n, x in enumerate(from_planes):
-        loads += [
-            pltpu.make_async_copy(post_ref.at[:, x], post_v.at[:, n], post_sem.at[n]),
-            pltpu.make_async_copy(adjf_ref.at[:, x], adj_v.at[pl.ds(0, NF), n], adjf_sem.at[n]),
-            pltpu.make_async_copy(adjg_ref.at[:, x], adj_v.at[pl.ds(NF, NG), n], adjg_sem.at[n]),
-        ]
-    halo = load_halo(first_ref, second_ref, halo_v, halo_sem)
-    start_all(halo)
-    start_all(loads)
     sums_v[...] = partial_ref[...]
-    table = lane_table(strengths_ref)
-    keep_low, keep_high = edges()
-    for c in halo:
-        c.wait()
-    mask_halo(halo_v)
+    keep_low, keep_high = load_halo(first_ref, second_ref, halo_v)
     stores = []
-    for n, (x, away, here, near_plane) in enumerate(((0, -1, 0, 1), (sx - 1, 1, 3, 2))):
-        for c in loads[6 * n : 6 * n + 6]:
-            c.wait()
+    for n, (x, away) in enumerate(((0, -1), (sx - 1, 1))):
         face_ref, corner_ref = (
             (fromleft_ref, cornerleft_ref) if away == -1 else (fromright_ref, cornerright_ref)
         )
 
-        def get(kind, i, dx, held, here=here, near_plane=near_plane, away=away, face_ref=face_ref):
-            if dx == 0:
-                return held[i, here]
+        def get(kind, i, dx, held, x=x, away=away, face_ref=face_ref):
             if dx == away:
                 return face_ref[face_slot(kind, i, dx)]
-            return held[i, near_plane]
+            return held[i, x + dx]
 
         def row(kind, i, dx, dy, x=x, away=away, corner_ref=corner_ref):
             side = 0 if dy == -1 else 1
@@ -650,36 +569,29 @@
             return halo_v[side, slot, x + dx : x + dx + 1, :]
 
         def mask(dx, x=x, away=away, face_ref=face_ref):
-            if dx == away:
-                return face_ref[MASK]
-            return 1.0 - wall_ref[x + dx].astype(jnp.float32)
-
-        magnet = magnet_ref[x]
-        profile = profile_ref[x]
+            return face_ref[MASK] if dx == away else fluid_ref[x + dx]
+
         plane_step(
             n,
-            lambda i, dx, get=get: get(0, i, dx, post_v),
+            lambda i, dx, get=get: get(0, i, dx, post_ref),
             lambda i, dx, dy, row=row: row(0, i, dx, dy),
-            lambda i, dx, get=get: get(1, i, dx, adj_v),
+            lambda i, dx, get=get: get(1, i, dx, adj_ref),
             lambda i, dx, dy, row=row: row(1, i, dx, dy),
             mask,
             lambda dx, dy, row=row: row(2, 0, dx, dy),
-            mask(0),
-            gather_strength(table, magnet) * profile,
-            profile,
-            magnet,
+            fluid_ref[x],
+            bcell_ref[x],
+            profile_ref[x],
+            magnet_ref[x],
             near_v,
             new_v,
             out_v,
             sums_v,
             count,
         )
-        these = [
-            pltpu.make_async_copy(new_v.at[pl.ds(0, NF), n], newf_ref.at[:, x], store_sem.at[n, 0]),
-            pltpu.make_async_copy(new_v.at[pl.ds(NF, NG), n], newg_ref.at[:, x], store_sem.at[n, 1]),
-            pltpu.make_async_copy(out_v.at[pl.ds(0, NF), n], outf_ref.at[:, x], store_sem.at[n, 2]),
-            pltpu.make_async_copy(out_v.at[pl.ds(NF, NG), n], outg_ref.at[:, x], store_sem.at[n, 3]),
-        ]
+        these = plane_stores(
+            n, x, new_v, out_v, newf_ref, newg_ref, outf_ref, outg_ref, store_sem
+        )
         start_all(these)
         stores += these
     rows = jnp.concatenate(
@@ -692,48 +604,42 @@
         precision=lax.Precision.HIGHEST,
         preferred_element_type=jnp.float32,
     )
-    for c in stores:
-        c.wait()
+    wait_all(stores)
 
 
 def outer_call(
-    post, adjf, adjg, first, second, fromleft, fromright, cornerleft, cornerright, profile,
-    strengths, wall, magnet, partial, newf, newg, outf, outg,
+    post, adj, fluid, bcell, first, second, fromleft, fromright, cornerleft, cornerright, profile,
+    magnet, partial, newf, newg, outf, outg,
 ):
     sx, sy, sz = profile.shape
-    count = strengths.shape[1]
-    dma = pltpu.SemaphoreType.DMA
+    count = partial.shape[0]
+    flow = jax.ShapeDtypeStruct(newf.shape, jnp.float32)
+    field = jax.ShapeDtypeStruct(newg.shape, jnp.float32)
     return pl.pallas_call(
         outer_kernel,
-        in_specs=[ANY] * 5 + [VMEM] * 9 + [ANY] * 4,
+        in_specs=[VMEM] * 13 + [ANY] * 4,
         out_specs=[ANY] * 4 + [VMEM],
         out_shape=[
-            jax.ShapeDtypeStruct(adjf.shape, jnp.float32),
-            jax.ShapeDtypeStruct(adjg.shape, jnp.float32),
-            jax.ShapeDtypeStruct(adjf.shape, jnp.float32),
-            jax.ShapeDtypeStruct(adjg.shape, jnp.float32),
+            flow,
+            field,
+            flow,
+            field,
             jax.ShapeDtypeStruct((lax.axis_size(("gx", "gy")), count), jnp.float32),
         ],
-        input_output_aliases={14: 0, 15: 1, 16: 2, 17: 3},
+        input_output_aliases={13: 0, 14: 1, 15: 2, 16: 3},
         scratch_shapes=[
-            pltpu.VMEM((NP, 4, sy, sz), jnp.float32),
-            pltpu.VMEM((NP, 4, sy, sz), jnp.float32),
             pltpu.VMEM((NP, 2, sy, sz), jnp.float32),
             pltpu.VMEM((NP, 2, sy, sz), jnp.float32),
             pltpu.VMEM((2, SLOTS, sx, sz), jnp.float32),
             pltpu.VMEM((18, sy, sz), jnp.float32),
             pltpu.VMEM((count, 8, 128), jnp.float32),
-            dma((4,)),
-            dma((4,)),
-            dma((4,)),
-            dma((2,)),
-            dma((2, 4)),
+            pltpu.SemaphoreType.DMA((4, 2)),
         ],
-        compiler_params=pltpu.CompilerParams(vmem_limit_bytes=51 << 20),
+        compiler_params=pltpu.CompilerParams(vmem_limit_bytes=OUTER_VMEM),
         name="outer",
     )(
-        post, adjf, adjg, first, second, fromleft, fromright, cornerleft, cornerright, profile,
-        strengths, wall, magnet, partial, newf, newg, outf, outg,
+        post, adj, fluid, bcell, first, second, fromleft, fromright, cornerleft, cornerright,
+        profile, magnet, partial, newf, newg, outf, outg,
     )
 
 
@@ -745,7 +651,7 @@
     across, around = lax.axis_size("gy"), lax.axis_size("gx")
     count = strengths.shape[0]
     table = strengths.reshape(1, count)
-    post, mine1, mine2, right, left = collide_call(
+    post, adj, fluid, bcell, profile, magnet, mine1, mine2, right, left = collide_call(
         flow, field, adj_flow_in, adj_field_in, profile, table, wall, magnet
     )
     inside = [(i, i ^ 1) for i in range(across)]
@@ -758,11 +664,11 @@
     cornerleft = lax.ppermute(corner_r, "gx", ring(around, 1))
     cornerright = lax.ppermute(corner_l, "gx", ring(around, -1))
     newf, newg, outf, outg, partial = inner_call(
-        post, adj_flow_in, adj_field_in, first, second, profile, table, wall, magnet
+        post, adj, fluid, bcell, first, second, profile, magnet, count
     )
     newf, newg, outf, outg, share = outer_call(
-        post, adj_flow_in, adj_field_in, first, second, fromleft, fromright, cornerleft,
-        cornerright, profile, table, wall, magnet, partial, newf, newg, outf, outg,
+        post, adj, fluid, bcell, first, second, fromleft, fromright, cornerleft, cornerright,
+        profile, magnet, partial, newf, newg, outf, outg,
     )
     cells = flow.shape[1] * around * flow.shape[2] * across * flow.shape[3]
     totals = jnp.sum(lax.all_to_all(share, ("gx", "gy"), 0, 0, tiled=True), axis=0)

time: 41.6 us -> 35.3 us (0.85)
  Pallas kernels: 16.1 us -> 10.1 us
    pallas_call x3, Pallas kernels: 16.1 us -> 10.1 us  [the longest x1 4.44 us: collide_call(): pl.pallas_call(collide_kernel, in_specs=[ANY, ANY, ANY, ANY, ANY, VMEM, A...]
    ppermute x1, waiting for transfers between devices: 0.01 us -> 0.48 us  [on_device(): cornerleft = lax.ppermute(corner_r, 'gx', ring(around, 1))]
    all_to_all x1, blocking collectives: 10.5 us -> 10.1 us  [on_device(): lax.all_to_all(share, ('gx', 'gy'), 0, 0, tiled=True)]
  transfers between devices with their start and end apart: 6 -> 6, of which waited for: 1 -> 2; matrix products, arithmetic and copies ran while one was open for 0% -> 0% of each run, Pallas kernels for 15% -> 11%
where the time goes in v4:
time: 35.3 us; the launch traced here: 35 us
  starting transfers between devices  12 us (34%)
  Pallas kernels  10.1 us (29%)
  blocking collectives  10.1 us (29%)
  waiting for transfers between devices  1.68 us (5%)
  between operations  0.69 us (2%)
  other arithmetic  0.57 us (2%)
    all_to_all x1, blocking collectives, on_device(): lax.all_to_all(share, ('gx', 'gy'), 0, 0, tiled=True)  10.1 us
    pallas_call x1, Pallas kernels, collide_call(): pl.pallas_call(collide_kernel, in_specs=[ANY, ANY, ANY, ANY, ANY, VMEM, A...  4.44 us
    pallas_call x1, Pallas kernels, inner_call(): pl.pallas_call(inner_kernel, in_specs=[VMEM] * 8, out_specs=[ANY, ANY, AN...  3.77 us
    ppermute x1, starting transfers between devices, on_device(): second = lax.ppermute(mine2, 'gy', between)  3.56 us
    ppermute x1, starting transfers between devices, on_device(): fromright = lax.ppermute(left, 'gx', ring(around, -1))  2.25 us
    ppermute x1, starting transfers between devices, on_device(): cornerright = lax.ppermute(corner_l, 'gx', ring(around, -1))  2.09 us
    ppermute x1, starting transfers between devices, on_device(): cornerleft = lax.ppermute(corner_r, 'gx', ring(around, 1))  1.97 us
    pallas_call x1, Pallas kernels, outer_call(): pl.pallas_call(outer_kernel, in_specs=[VMEM] * 13 + [ANY] * 4, out_specs=...  1.85 us
  transfers between devices with their start and end apart: 6, of which 2 were waited for; matrix products, arithmetic and copies ran while one was open for 0% of the time, Pallas kernels for 11%

profile of v4, /device:TPU:0, one launch (start us, length us, event | category | flops | bytes accessed | tf_op | source)
XLA Modules:
  0.0 35.0 jit_solution(9694240636682530732)
XLA Ops:
  0.6 4.4 %collide.1 = (f32[26,8,8,512]{3,2,1,0:T(8,128)S(1)}, f32[26,8,8,512]{3,2,1,0:T(8,128)S(1)}, f32[8,8,512]{2,1,0:T(8,128)S(1)}, f32[8,8,512]{2,1,0:T(8,128)S(1)}, ...) custom-call(f32[19,8,8,512]{3,2,1,0:T(8,128)} %flow_ref.1, ...), custom_call_target="tpu_custom_call" | custom-call | tf_op jit(solution)/shard_map/collide/pallas_call | solution.py:208
  5.1 0.5 %collective-permute-start = (f32[13,8,512]{2,1,0:T(8,128)S(1)}, f32[13,8,512]{2,1,0:T(8,128)S(1)}, u32[]{:S(2)}, u32[]{:S(2)}) collective-permute-start(f32[13,8,512]{2,1,0:T(8,128)S(1)} %get-tuple-element.31), channel_id=1, source_target_pairs={{0,1},{1,0},{2,3},{3,2},{4,5},{5,4},{6,7},{7,6},{8,9},{9,8},{10,11... | collective-permute-start | bytes 638984 | tf_op jit(solution)/shard_map/ppermute | solution.py:660
  5.6 3.6 %collective-permute-start.1 = (f32[13,8,512]{2,1,0:T(8,128)S(1)}, f32[13,8,512]{2,1,0:T(8,128)S(1)}, u32[]{:S(2)}, u32[]{:S(2)}) collective-permute-start(f32[13,8,512]{2,1,0:T(8,128)S(1)} %get-tuple-element.32), channel_id=1, source_target_pairs={{0,7},{1,2},{2,1},{3,4},{4,3},{5,6},{6,5},{7,0},{8,15},{9,10},{10,... | collective-permute-start | bytes 638984 | tf_op jit(solution)/shard_map/ppermute | solution.py:659
  9.2 1.6 %collective-permute-start.2 = (f32[13,8,512]{2,1,0:T(8,128)S(1)}, f32[13,8,512]{2,1,0:T(8,128)S(1)}, u32[]{:S(2)}, u32[]{:S(2)}) collective-permute-start(f32[13,8,512]{2,1,0:T(8,128)S(1)} %get-tuple-element.33), channel_id=1, source_target_pairs={{0,8},{8,16},{16,24},{24,0},{1,9},{9,17},{17,25},{25,1},{2,10},{10... | collective-permute-start | bytes 638984 | tf_op jit(solution)/shard_map/ppermute | solution.py:661
  10.7 2.2 %collective-permute-start.3 = (f32[13,8,512]{2,1,0:T(8,128)S(1)}, f32[13,8,512]{2,1,0:T(8,128)S(1)}, u32[]{:S(2)}, u32[]{:S(2)}) collective-permute-start(f32[13,8,512]{2,1,0:T(8,128)S(1)} %get-tuple-element.34), channel_id=1, source_target_pairs={{0,24},{8,0},{16,8},{24,16},{1,25},{9,1},{17,9},{25,17},{2,26},{10... | collective-permute-start | bytes 638984 | tf_op jit(solution)/shard_map/ppermute | solution.py:662
  13.0 0.0 collective-permute-done.first_ref
  13.0 1.2 %collective-permute-done.1.second_ref = f32[13,8,512]{2,1,0:T(8,128)S(1)} collective-permute-done((f32[13,8,512]{2,1,0:T(8,128)S(1)}, f32[13,8,512]{2,1,0:T(8,128)S(1)}, u32[]{:S(2)}, u32[]{:S(2)}) %collective-permute-start.1) | collective-permute-done | bytes 213024 | tf_op jit(solution)/shard_map/ppermute | solution.py:659
  14.2 2.0 %collective-permute-start.4 = (f32[8,512]{1,0:T(8,128)S(1)}, f32[8,512]{1,0:T(8,128)S(1)}, u32[]{:S(2)}, u32[]{:S(2)}) collective-permute-start(f32[8,512]{1,0:T(8,128)S(1)} %get-tuple-element.35), channel_id=1, source_target_pairs={{0,8},{8,16},{16,24},{24,0},{1,9},{9,17},{17,25},{25,1},{2,10},{10... | collective-permute-start | bytes 49160 | tf_op jit(solution)/shard_map/ppermute | solution.py:664
  16.2 2.1 %collective-permute-start.5 = (f32[8,512]{1,0:T(8,128)S(1)}, f32[8,512]{1,0:T(8,128)S(1)}, u32[]{:S(2)}, u32[]{:S(2)}) collective-permute-start(f32[8,512]{1,0:T(8,128)S(1)} %get-tuple-element.36), channel_id=1, source_target_pairs={{0,24},{8,0},{16,8},{24,16},{1,25},{9,1},{17,9},{25,17},{2,26},{10... | collective-permute-start | bytes 49160 | tf_op jit(solution)/shard_map/ppermute | solution.py:665
  18.2 3.8 %inner.1 = (f32[19,8,8,512]{3,2,1,0:T(8,128)}, f32[7,8,8,512]{3,2,1,0:T(8,128)}, f32[19,8,8,512]{3,2,1,0:T(8,128)}, f32[7,8,8,512]{3,2,1,0:T(8,128)}, f32[32,8,128]{2,1,0:T(8,128)S(1)}) custom-call(f32[26,8,8,512]{3,2,1,0:T(8,128)S(1)} %get-tuple-element.27.post_ref, f32[26,8,8,512]{3,2,1,0:T(8,128)S(1)} %get-tuple-element.28.adj_ref, ...), custom_call_target="tpu_custom_call" | custom-call | flops 22937600 | bytes 13631488 | tf_op jit(solution)/shard_map/inner/pallas_call | solution.py:518
  22.0 0.0 collective-permute-done.2.fromleft_ref
  22.0 0.0 collective-permute-done.3.fromright_ref
  22.1 0.5 %collective-permute-done.4.cornerleft_ref = f32[8,512]{1,0:T(8,128)S(1)} collective-permute-done((f32[8,512]{1,0:T(8,128)S(1)}, f32[8,512]{1,0:T(8,128)S(1)}, u32[]{:S(2)}, u32[]{:S(2)}) %collective-permute-start.4) | collective-permute-done | bytes 16416 | tf_op jit(solution)/shard_map/ppermute | solution.py:664
  22.5 0.0 collective-permute-done.5.cornerright_ref
  22.5 1.8 %outer.1 = (f32[19,8,8,512]{3,2,1,0:T(8,128)}, f32[7,8,8,512]{3,2,1,0:T(8,128)}, f32[19,8,8,512]{3,2,1,0:T(8,128)}, f32[7,8,8,512]{3,2,1,0:T(8,128)}, f32[32,32]{1,0:T(8,128)S(1)}) custom-call(f32[26,8,8,512]{3,2,1,0:T(8,128)S(1)} %get-tuple-element.27.post_ref, ...), custom_call_target="tpu_custom_call", output_to_operand_aliasing={{0}: (13, {}), {1}: (14, {}), {2}: (15, {}), {3}: (16, {})} | custom-call | tf_op jit(solution)/shard_map/outer/pallas_call | solution.py:618
  24.4 10.1 %all_to_all.9 = f32[32,1,32]{2,1,0:T(1,128)S(1)} all-to-all(f32[32,1,32]{2,1,0:T(1,128)S(1)} %bitcast.4), channel_id=1, replica_groups=mesh['gx'=4,'gy'=8] {'gx','gy'}, dimensions={0} | all-to-all | bytes 8192 | tf_op jit(solution)/shard_map/all_to_all | solution.py:674
  34.4 0.1 reduce_sum.9
  34.5 0.5 %broadcast_multiply_fusion = f32[32]{0:T(128)} fusion(f32[32]{0:T(128)S(1)} %reduce_sum.9), kind=kLoop, calls=%fused_computation | loop fusion | flops 32 | bytes 256 | tf_op jit(solution)/shard_map/div | solution.py:675
  (1 shorter events, 0.0 us)
Async XLA Ops:
  5.1 7.9 %collective-permute-start = (f32[13,8,512]{2,1,0:T(8,128)S(1)}, f32[13,8,512]{2,1,0:T(8,128)S(1)}, u32[]{:S(2)}, u32[]{:S(2)}) collective-permute-start(f32[13,8,512]{2,1,0:T(8,128)S(1)} %get-tuple-element.31), channel_id=1, source_target_pairs={{0,1},{1,0},{2,3},{3,2},{4,5},{5,4},{6,7},{7,6},{8,9},{9,8},{10,11... | collective-permute-start | bytes 638984 | tf_op jit(solution)/shard_map/ppermute | solution.py:660
  5.6 8.6 %collective-permute-start.1 = (f32[13,8,512]{2,1,0:T(8,128)S(1)}, f32[13,8,512]{2,1,0:T(8,128)S(1)}, u32[]{:S(2)}, u32[]{:S(2)}) collective-permute-start(f32[13,8,512]{2,1,0:T(8,128)S(1)} %get-tuple-element.32), channel_id=1, source_target_pairs={{0,7},{1,2},{2,1},{3,4},{4,3},{5,6},{6,5},{7,0},{8,15},{9,10},{10,... | collective-permute-start | bytes 638984 | tf_op jit(solution)/shard_map/ppermute | solution.py:659
  9.2 12.9 %collective-permute-start.2 = (f32[13,8,512]{2,1,0:T(8,128)S(1)}, f32[13,8,512]{2,1,0:T(8,128)S(1)}, u32[]{:S(2)}, u32[]{:S(2)}) collective-permute-start(f32[13,8,512]{2,1,0:T(8,128)S(1)} %get-tuple-element.33), channel_id=1, source_target_pairs={{0,8},{8,16},{16,24},{24,0},{1,9},{9,17},{17,25},{25,1},{2,10},{10... | collective-permute-start | bytes 638984 | tf_op jit(solution)/shard_map/ppermute | solution.py:661
  10.7 11.3 %collective-permute-start.3 = (f32[13,8,512]{2,1,0:T(8,128)S(1)}, f32[13,8,512]{2,1,0:T(8,128)S(1)}, u32[]{:S(2)}, u32[]{:S(2)}) collective-permute-start(f32[13,8,512]{2,1,0:T(8,128)S(1)} %get-tuple-element.34), channel_id=1, source_target_pairs={{0,24},{8,0},{16,8},{24,16},{1,25},{9,1},{17,9},{25,17},{2,26},{10... | collective-permute-start | bytes 638984 | tf_op jit(solution)/shard_map/ppermute | solution.py:662
  14.2 8.3 %collective-permute-start.4 = (f32[8,512]{1,0:T(8,128)S(1)}, f32[8,512]{1,0:T(8,128)S(1)}, u32[]{:S(2)}, u32[]{:S(2)}) collective-permute-start(f32[8,512]{1,0:T(8,128)S(1)} %get-tuple-element.35), channel_id=1, source_target_pairs={{0,8},{8,16},{16,24},{24,0},{1,9},{9,17},{17,25},{25,1},{2,10},{10... | collective-permute-start | bytes 49160 | tf_op jit(solution)/shard_map/ppermute | solution.py:664
  16.2 6.4 %collective-permute-start.5 = (f32[8,512]{1,0:T(8,128)S(1)}, f32[8,512]{1,0:T(8,128)S(1)}, u32[]{:S(2)}, u32[]{:S(2)}) collective-permute-start(f32[8,512]{1,0:T(8,128)S(1)} %get-tuple-element.36), channel_id=1, source_target_pairs={{0,24},{8,0},{16,8},{24,16},{1,25},{9,1},{17,9},{25,17},{2,26},{10... | collective-permute-start | bytes 49160 | tf_op jit(solution)/shard_map/ppermute | solution.py:665

commit v5 on v4

--- a/solution.py
+++ b/solution.py
@@ -47,6 +47,7 @@
 SLOTS = 13
 MASK = 12
 
+RIM_VMEM = 60 << 20
 COLLIDE_VMEM = 48 << 20
 INNER_VMEM = 42 << 20
 OUTER_VMEM = 42 << 20
@@ -100,14 +101,179 @@
         c.wait()
 
 
+def collide(f, g, fluid, bcell, wanted):
+    even = {i: f[i] + f[i + 1] for i in FIRST}
+    diff = {i: f[i] - f[i + 1] for i in FIRST}
+    rho = f[0] + (1.0 - fluid)
+    for i in FIRST:
+        rho = rho + even[i]
+    momx, momy, momz = vector_sums(diff)
+    inv = 1.0 / rho
+    ux, uy, uz = momx * inv, momy * inv, momz * inv
+    bval = g[0] + g[1] + g[2] + g[3] + g[4] + g[5] + g[6]
+    current = (g[3] - g[4]) - bval * uy
+    shear = (even[7] - even[9]) - momx * uy
+    force = (COUPLE * bcell) * current
+    vx = ux + TAU_PLUS * force * inv
+    base = 1.0 - 1.5 * (vx * vx + uy * uy + uz * uz)
+    post = {}
+    if 0 in wanted:
+        post[0] = f[0] - 2.0 * PLUS * (f[0] - (W0 * rho) * base)
+    rho1, rho2 = W1 * rho, W2 * rho
+    for i in FIRST:
+        if i not in wanted and i + 1 not in wanted:
+            continue
+        wr = rho1 if i <= 6 else rho2
+        a = along(i, vx, uy, uz)
+        ne = PLUS * (even[i] - (2.0 * wr) * (base + 4.5 * a * a))
+        no = MINUS * (diff[i] - (6.0 * wr) * a)
+        if i in wanted:
+            post[i] = f[i] - ne - no
+        if i + 1 in wanted:
+            post[i + 1] = f[i + 1] - ne + no
+    common = bval + (SOURCE * bcell) * shear
+    slope = 4.0 * bval
+    if NF in wanted:
+        post[NF] = V0 * common
+    for k, u in ((1, ux), (3, uy), (5, uz)):
+        if NF + k in wanted:
+            post[NF + k] = V1 * (common + slope * u)
+        if NF + k + 1 in wanted:
+            post[NF + k + 1] = V1 * (common - slope * u)
+    return post
+
+
+def rim_kernel(
+    flow_ref, field_ref, adjf_ref, adjg_ref, profile_ref, strengths_ref, wall_ref, magnet_ref,
+    first_ref, second_ref, right_ref, left_ref,
+    rows_v, faces_v, profile_v, wall_v, magnet_v, message_v, cell_sem, rows_sem, faces_sem, adj_sem,
+):
+    sx, sy = profile_v.shape[:2]
+    odd = lax.rem(lax.axis_index("gy"), 2)
+    ends = (sy - 1, 0)
+    sides = (0, sx - 1)
+
+    def adj_at(i, where):
+        return adjf_ref.at[(i, *where)] if i < NF else adjg_ref.at[(i - NF, *where)]
+
+    rows = []
+    for n, y in enumerate(ends):
+        rows += [
+            pltpu.make_async_copy(
+                flow_ref.at[:, :, y], rows_v.at[n, pl.ds(0, NF)], rows_sem.at[n, 0]
+            ),
+            pltpu.make_async_copy(
+                field_ref.at[:, :, y], rows_v.at[n, pl.ds(NF, NG)], rows_sem.at[n, 1]
+            ),
+        ]
+    cells = [
+        pltpu.make_async_copy(a, b, cell_sem.at[n])
+        for n, (a, b) in enumerate(
+            ((wall_ref, wall_v), (magnet_ref, magnet_v), (profile_ref, profile_v))
+        )
+    ]
+    faces = []
+    for n, x in enumerate(sides):
+        faces += [
+            pltpu.make_async_copy(
+                flow_ref.at[:, x], faces_v.at[n, pl.ds(0, NF)], faces_sem.at[n, 0]
+            ),
+            pltpu.make_async_copy(
+                field_ref.at[:, x], faces_v.at[n, pl.ds(NF, NG)], faces_sem.at[n, 1]
+            ),
+        ]
+    adjs = []
+    for s in range(6):
+        for n, (i, where, out) in enumerate(
+            (
+                (DOWN[s], (slice(None), ends[0]), message_v.at[0]),
+                (UP[s], (slice(None), ends[1]), message_v.at[1]),
+                (RIGHT[s], (sides[0],), left_ref),
+                (LEFT[s], (sides[1],), right_ref),
+            )
+        ):
+            adjs.append(pltpu.make_async_copy(adj_at(i, where), out.at[6 + s], adj_sem.at[n, s]))
+    start_all(rows[:2])
+    start_all(cells)
+    start_all(rows[2:])
+    start_all(faces)
+    start_all(adjs)
+    table = lane_table(strengths_ref)
+    wait_all(cells)
+    for n, (y, wanted) in enumerate(zip(ends, (UP, DOWN))):
+        wait_all(rows[2 * n : 2 * n + 2])
+        fluid = 1.0 - wall_v[:, y, :].astype(jnp.float32)
+        bcell = gather_strength(table, magnet_v[:, y, :]) * profile_v[:, y, :]
+        post = collide(
+            [rows_v[n, i] for i in range(NF)],
+            [rows_v[n, NF + k] for k in range(NG)],
+            fluid,
+            bcell,
+            wanted,
+        )
+        for s in range(6):
+            message_v[n, s] = post[wanted[s]]
+        message_v[n, MASK] = fluid
+    for n, (x, wanted, out) in enumerate(
+        ((sides[0], LEFT, left_ref), (sides[1], RIGHT, right_ref))
+    ):
+        wait_all(faces[2 * n : 2 * n + 2])
+        fluid = 1.0 - wall_v[x].astype(jnp.float32)
+        bcell = gather_strength(table, magnet_v[x]) * profile_v[x]
+        post = collide(
+            [faces_v[n, i] for i in range(NF)],
+            [faces_v[n, NF + k] for k in range(NG)],
+            fluid,
+            bcell,
+            wanted,
+        )
+        for s in range(6):
+            out[s] = post[wanted[s]]
+        out[MASK] = fluid
+    wait_all(adjs)
+    first_ref[...] = message_v[odd]
+    second_ref[...] = message_v[1 - odd]
+
+
+ANY = pl.BlockSpec(memory_space=pl.ANY)
+VMEM = pl.BlockSpec(memory_space=pltpu.VMEM)
+
+
+def rim_call(flow, field, adjf, adjg, profile, strengths, wall, magnet):
+    sx, sy, sz = profile.shape
+    cells = pltpu.VMEM((sx, sy, sz), jnp.float32)
+    names = pltpu.VMEM((sx, sy, sz), jnp.int32)
+    rows = pltpu.VMEM((SLOTS, sx, sz), jnp.float32)
+    faces = pltpu.VMEM((SLOTS, sy, sz), jnp.float32)
+    dma = pltpu.SemaphoreType.DMA
+    return pl.pallas_call(
+        rim_kernel,
+        in_specs=[ANY, ANY, ANY, ANY, ANY, VMEM, ANY, ANY],
+        out_specs=[VMEM] * 4,
+        out_shape=[rows, rows, faces, faces],
+        scratch_shapes=[
+            pltpu.VMEM((2, NP, sx, sz), jnp.float32),
+            pltpu.VMEM((2, NP, sy, sz), jnp.float32),
+            cells,
+            names,
+            names,
+            pltpu.VMEM((2, SLOTS, sx, sz), jnp.float32),
+            dma((3,)),
+            dma((2, 2)),
+            dma((2, 2)),
+            dma((4, 6)),
+        ],
+        compiler_params=pltpu.CompilerParams(vmem_limit_bytes=RIM_VMEM),
+        name="rims",
+    )(flow, field, adjf, adjg, profile, strengths, wall, magnet)
+
+
 def collide_kernel(
     flow_ref, field_ref, adjf_ref, adjg_ref, profile_ref, strengths_ref, wall_ref, magnet_ref,
-    post_ref, adj_ref, fluid_ref, bcell_ref, profile_v, magnet_v, first_ref, second_ref, right_ref,
-    left_ref,
+    post_ref, adj_ref, fluid_ref, bcell_ref, profile_v, magnet_v,
     flow_v, field_v, wall_v, plane_sem, adj_sem,
 ):
-    sx, sy = fluid_ref.shape[:2]
-    odd = lax.rem(lax.axis_index("gy"), 2)
+    sx = fluid_ref.shape[0]
 
     def loads(x):
         pairs = (
@@ -136,65 +302,12 @@
         bcell_ref[x] = bcell
         f = [flow_v[i, x] for i in range(NF)]
         g = [field_v[k, x] for k in range(NG)]
-        even = {i: f[i] + f[i + 1] for i in FIRST}
-        diff = {i: f[i] - f[i + 1] for i in FIRST}
-        rho = f[0] + (1.0 - fluid)
-        for i in FIRST:
-            rho = rho + even[i]
-        momx, momy, momz = vector_sums(diff)
-        inv = 1.0 / rho
-        ux, uy, uz = momx * inv, momy * inv, momz * inv
-        bval = g[0] + g[1] + g[2] + g[3] + g[4] + g[5] + g[6]
-        current = (g[3] - g[4]) - bval * uy
-        shear = (even[7] - even[9]) - momx * uy
-        force = (COUPLE * bcell) * current
-        vx = ux + TAU_PLUS * force * inv
-        base = 1.0 - 1.5 * (vx * vx + uy * uy + uz * uz)
-        post_ref[0, x] = f[0] - 2.0 * PLUS * (f[0] - (W0 * rho) * base)
-        rho1, rho2 = W1 * rho, W2 * rho
-        for i in FIRST:
-            wr = rho1 if i <= 6 else rho2
-            a = along(i, vx, uy, uz)
-            ne = even[i] - (2.0 * wr) * (base + 4.5 * a * a)
-            no = diff[i] - (6.0 * wr) * a
-            ne = PLUS * ne
-            no = MINUS * no
-            post_ref[i, x] = f[i] - ne - no
-            post_ref[i + 1, x] = f[i + 1] - ne + no
-        common = bval + (SOURCE * bcell) * shear
-        slope = 4.0 * bval
-        post_ref[NF, x] = V0 * common
-        for k, u in ((1, ux), (3, uy), (5, uz)):
-            su = slope * u
-            post_ref[NF + k, x] = V1 * (common + su)
-            post_ref[NF + k + 1, x] = V1 * (common - su)
+        for i, value in collide(f, g, fluid, bcell, range(NP)).items():
+            post_ref[i, x] = value
         return carry
 
     lax.fori_loop(0, sx, body, 0)
-
     wait_all(adj_loads)
-
-    def pack(x, carry):
-        here = pl.ds(x, 1)
-        for out, side in ((first_ref, odd), (second_ref, 1 - odd)):
-            line = pl.ds((1 - side) * (sy - 1), 1)
-            for s in range(6):
-                up, down = UP[s], DOWN[s]
-                out[s, here, :] = post_ref[up + side * (down - up), x, line, :]
-                out[6 + s, here, :] = adj_ref[down + side * (up - down), x, line, :]
-            out[MASK, here, :] = fluid_ref[x, line, :]
-        return carry
-
-    lax.fori_loop(0, sx, pack, 0)
-    for out, x, posts, adjs in ((left_ref, 0, LEFT, RIGHT), (right_ref, sx - 1, RIGHT, LEFT)):
-        for s in range(6):
-            out[s] = post_ref[posts[s], x]
-            out[6 + s] = adj_ref[adjs[s], x]
-        out[MASK] = fluid_ref[x]
-
-
-ANY = pl.BlockSpec(memory_space=pl.ANY)
-VMEM = pl.BlockSpec(memory_space=pltpu.VMEM)
 
 
 def collide_call(flow, field, adjf, adjg, profile, strengths, wall, magnet):
@@ -202,14 +315,12 @@
     full = pltpu.VMEM((NP, sx, sy, sz), jnp.float32)
     cells = pltpu.VMEM((sx, sy, sz), jnp.float32)
     names = pltpu.VMEM((sx, sy, sz), jnp.int32)
-    rows = pltpu.VMEM((SLOTS, sx, sz), jnp.float32)
-    faces = pltpu.VMEM((SLOTS, sy, sz), jnp.float32)
     dma = pltpu.SemaphoreType.DMA
     return pl.pallas_call(
         collide_kernel,
         in_specs=[ANY, ANY, ANY, ANY, ANY, VMEM, ANY, ANY],
-        out_specs=[VMEM] * 10,
-        out_shape=[full, full, cells, cells, cells, names, rows, rows, faces, faces],
+        out_specs=[VMEM] * 6,
+        out_shape=[full, full, cells, cells, cells, names],
         scratch_shapes=[
             pltpu.VMEM(flow.shape, jnp.float32),
             pltpu.VMEM(field.shape, jnp.float32),
@@ -218,6 +329,9 @@
             dma((2,)),
         ],
         compiler_params=pltpu.CompilerParams(vmem_limit_bytes=COLLIDE_VMEM),
+        cost_estimate=pl.CostEstimate(
+            flops=300 * sx * sy * sz, bytes_accessed=12 * NP * sx * sy * sz, transcendentals=0
+        ),
         name="collide",
     )(flow, field, adjf, adjg, profile, strengths, wall, magnet)
 
@@ -231,7 +345,8 @@
     return posts.index(post), 6 + adjs.index(adj), MASK
 
 
-def corner_kernel(first_ref, second_ref, right_ref, left_ref):
+def corner_kernel(first_ref, second_ref, after_ref, right_ref, left_ref):
+    del after_ref
     odd = lax.rem(lax.axis_index("gy"), 2) == 1
     sx = first_ref.shape[1]
 
@@ -246,10 +361,17 @@
                 out[2 * n + side : 2 * n + side + 1, :] = row(side, slot, x)
 
 
-def corner_call(first, second):
+def corner_call(first, second, after):
     sz = first.shape[2]
-    out = jax.ShapeDtypeStruct((8, sz), jnp.float32)
-    return pl.pallas_call(corner_kernel, out_shape=[out, out], compiler_params=pltpu.CompilerParams(vmem_limit_bytes=2 << 20), name="corners")(first, second)
+    out = pltpu.VMEM((8, sz), jnp.float32)
+    return pl.pallas_call(
+        corner_kernel,
+        in_specs=[VMEM, VMEM, ANY],
+        out_specs=[VMEM, VMEM],
+        out_shape=[out, out],
+        compiler_params=pltpu.CompilerParams(vmem_limit_bytes=2 << 20),
+        name="corners",
+    )(first, second, after)
 
 
 def plane_step(
@@ -536,7 +658,7 @@
 
 
 def outer_kernel(
-    post_ref, adj_ref, fluid_ref, bcell_ref, first_ref, second_ref, fromleft_ref, fromright_ref,
+    scale, post_ref, adj_ref, fluid_ref, bcell_ref, first_ref, second_ref, fromleft_ref, fromright_ref,
     cornerleft_ref, cornerright_ref, profile_ref, magnet_ref,
     partial_ref, newf_in, newg_in, outf_in, outg_in,
     newf_ref, newg_ref, outf_ref, outg_ref, share_ref,
@@ -599,7 +721,7 @@
     )
     share_ref[...] = lax.dot_general(
         jnp.ones((share_ref.shape[0], 128), jnp.float32),
-        rows,
+        rows * scale,
         (((1,), (1,)), ((), ())),
         precision=lax.Precision.HIGHEST,
         preferred_element_type=jnp.float32,
@@ -609,14 +731,14 @@
 
 def outer_call(
     post, adj, fluid, bcell, first, second, fromleft, fromright, cornerleft, cornerright, profile,
-    magnet, partial, newf, newg, outf, outg,
+    magnet, partial, newf, newg, outf, outg, scale,
 ):
     sx, sy, sz = profile.shape
     count = partial.shape[0]
     flow = jax.ShapeDtypeStruct(newf.shape, jnp.float32)
     field = jax.ShapeDtypeStruct(newg.shape, jnp.float32)
     return pl.pallas_call(
-        outer_kernel,
+        functools.partial(outer_kernel, scale),
         in_specs=[VMEM] * 13 + [ANY] * 4,
         out_specs=[ANY] * 4 + [VMEM],
         out_shape=[
@@ -651,28 +773,28 @@
     across, around = lax.axis_size("gy"), lax.axis_size("gx")
     count = strengths.shape[0]
     table = strengths.reshape(1, count)
-    post, adj, fluid, bcell, profile, magnet, mine1, mine2, right, left = collide_call(
-        flow, field, adj_flow_in, adj_field_in, profile, table, wall, magnet
-    )
+    arrays = (flow, field, adj_flow_in, adj_field_in, profile, table, wall, magnet)
+    mine1, mine2, right, left = rim_call(*arrays)
     inside = [(i, i ^ 1) for i in range(across)]
     between = [(i, (((i + 1) ^ 1) - 1) % across) for i in range(across)]
     second = lax.ppermute(mine2, "gy", between)
     first = lax.ppermute(mine1, "gy", inside)
     fromleft = lax.ppermute(right, "gx", ring(around, 1))
     fromright = lax.ppermute(left, "gx", ring(around, -1))
-    corner_r, corner_l = corner_call(first, second)
+    post, adj, fluid, bcell, profile, magnet = collide_call(*arrays)
+    corner_r, corner_l = corner_call(first, second, bcell)
     cornerleft = lax.ppermute(corner_r, "gx", ring(around, 1))
     cornerright = lax.ppermute(corner_l, "gx", ring(around, -1))
     newf, newg, outf, outg, partial = inner_call(
         post, adj, fluid, bcell, first, second, profile, magnet, count
     )
+    cells = flow.shape[1] * around * flow.shape[2] * across * flow.shape[3]
     newf, newg, outf, outg, share = outer_call(
         post, adj, fluid, bcell, first, second, fromleft, fromright, cornerleft, cornerright,
-        profile, magnet, partial, newf, newg, outf, outg,
+        profile, magnet, partial, newf, newg, outf, outg, 1.0 / math.sqrt(cells / count),
     )
-    cells = flow.shape[1] * around * flow.shape[2] * across * flow.shape[3]
     totals = jnp.sum(lax.all_to_all(share, ("gx", "gy"), 0, 0, tiled=True), axis=0)
-    return (newf, newg, outf, outg, totals / math.sqrt(cells / count))
+    return (newf, newg, outf, outg, totals)
 
 
 def solution(mesh):

time: 35.3 us -> 35 us (level)
  Pallas kernels: 10.1 us -> 12.6 us
  waiting for transfers between devices: 1.68 us -> 0.02 us
  blocking collectives: 10.1 us -> 9.03 us
    pallas_call x2 -> x3, Pallas kernels: 1.86 us -> 4.63 us  [the longest x1 2.76 us: rim_call(): pl.pallas_call(rim_kernel, in_specs=[ANY, ANY, ANY, ANY, ANY, VMEM, ANY,...]
    ppermute x1, starting transfers between devices: 1.97 us -> 0.06 us  [on_device(): cornerleft = lax.ppermute(corner_r, 'gx', ring(around, 1))]
    ppermute x1, starting transfers between devices: 2.09 us -> 3.81 us  [on_device(): cornerright = lax.ppermute(corner_l, 'gx', ring(around, -1))]
    ppermute x1, waiting for transfers between devices: 1.18 us -> 0.01 us  [on_device(): second = lax.ppermute(mine2, 'gy', between)]
    all_to_all x1, blocking collectives: 10.1 us -> 9.03 us  [on_device(): lax.all_to_all(share, ('gx', 'gy'), 0, 0, tiled=True)]
    div x1 -> x0, other arithmetic: 0.52 us -> none  [on_device(): return (newf, newg, outf, outg, totals / math.sqrt(cells / count))]
    reduce_sum x1, other arithmetic: 0.05 us -> 0.56 us  [on_device(): jnp.sum(lax.all_to_all(share, ('gx', 'gy'), 0, 0, tiled=True), axis=0)]
    ppermute x1, waiting for transfers between devices: 0.48 us -> 0.01 us  [on_device(): cornerleft = lax.ppermute(corner_r, 'gx', ring(around, 1))]
  transfers between devices with their start and end apart: 6 -> 6, of which waited for: 2 -> 0; matrix products, arithmetic and copies ran while one was open for 0% -> 0% of each run, Pallas kernels for 11% -> 23%
where the time goes in v5:
time: 35 us; the launch traced here: 34.7 us
  Pallas kernels  12.6 us (36%)
  starting transfers between devices  11.8 us (34%)
  blocking collectives  9.03 us (26%)
  between operations  0.73 us (2%)
  other arithmetic  0.56 us (2%)
    all_to_all x1, blocking collectives, on_device(): lax.all_to_all(share, ('gx', 'gy'), 0, 0, tiled=True)  9.03 us
    pallas_call x1, Pallas kernels, collide_call(): pl.pallas_call(collide_kernel, in_specs=[ANY, ANY, ANY, ANY, ANY, VMEM, A...  4.18 us
    ppermute x1, starting transfers between devices, on_device(): cornerright = lax.ppermute(corner_l, 'gx', ring(around, -1))  3.81 us
    pallas_call x1, Pallas kernels, inner_call(): pl.pallas_call(inner_kernel, in_specs=[VMEM] * 8, out_specs=[ANY, ANY, AN...  3.78 us
    ppermute x1, starting transfers between devices, on_device(): second = lax.ppermute(mine2, 'gy', between)  3.56 us
    pallas_call x1, Pallas kernels, rim_call(): pl.pallas_call(rim_kernel, in_specs=[ANY, ANY, ANY, ANY, ANY, VMEM, ANY,...  2.76 us
    ppermute x1, starting transfers between devices, on_device(): fromright = lax.ppermute(left, 'gx', ring(around, -1))  2.25 us
    pallas_call x1, Pallas kernels, outer_call(): pl.pallas_call(functools.partial(outer_kernel, scale), in_specs=[VMEM] *...  1.85 us
  transfers between devices with their start and end apart: 6, of which 0 were waited for; matrix products, arithmetic and copies ran while one was open for 0% of the time, Pallas kernels for 23%

profile of v5, /device:TPU:0, one launch (start us, length us, event | category | flops | bytes accessed | tf_op | source)
XLA Modules:
  0.0 34.7 jit_solution(12127288041221521221)
XLA Ops:
  0.6 2.8 %rims.1 = (f32[13,8,512]{2,1,0:T(8,128)S(1)}, f32[13,8,512]{2,1,0:T(8,128)S(1)}, f32[13,8,512]{2,1,0:T(8,128)S(1)}, f32[13,8,512]{2,1,0:T(8,128)S(1)}) custom-call(f32[19,8,8,512]{3,2,1,0:T(8,128)} %flow_ref.3, f32[7,8,8,512]{3,2,1,0:T(8,128)} %field_ref.3, f32[19,8,8,512]{3,2,1,0:T(8,128)} %adjf_ref.3, f32[7,8,8,512]{3,2,1,0:T(8,128)} %adjg_ref.3, ...), custom_call_target="tpu_custom_call" | custom-call | tf_op jit(solution)/shard_map/rims/pallas_call | solution.py:249
  3.4 0.5 %collective-permute-start = (f32[13,8,512]{2,1,0:T(8,128)S(1)}, f32[13,8,512]{2,1,0:T(8,128)S(1)}, u32[]{:S(2)}, u32[]{:S(2)}) collective-permute-start(f32[13,8,512]{2,1,0:T(8,128)S(1)} %get-tuple-element.31), channel_id=1, source_target_pairs={{0,1},{1,0},{2,3},{3,2},{4,5},{5,4},{6,7},{7,6},{8,9},{9,8},{10,11... | collective-permute-start | bytes 638984 | tf_op jit(solution)/shard_map/ppermute | solution.py:781
  3.9 3.6 %collective-permute-start.1 = (f32[13,8,512]{2,1,0:T(8,128)S(1)}, f32[13,8,512]{2,1,0:T(8,128)S(1)}, u32[]{:S(2)}, u32[]{:S(2)}) collective-permute-start(f32[13,8,512]{2,1,0:T(8,128)S(1)} %get-tuple-element.32), channel_id=1, source_target_pairs={{0,7},{1,2},{2,1},{3,4},{4,3},{5,6},{6,5},{7,0},{8,15},{9,10},{10,... | collective-permute-start | bytes 638984 | tf_op jit(solution)/shard_map/ppermute | solution.py:780
  7.5 1.6 %collective-permute-start.2 = (f32[13,8,512]{2,1,0:T(8,128)S(1)}, f32[13,8,512]{2,1,0:T(8,128)S(1)}, u32[]{:S(2)}, u32[]{:S(2)}) collective-permute-start(f32[13,8,512]{2,1,0:T(8,128)S(1)} %get-tuple-element.33), channel_id=1, source_target_pairs={{0,8},{8,16},{16,24},{24,0},{1,9},{9,17},{17,25},{25,1},{2,10},{10... | collective-permute-start | bytes 638984 | tf_op jit(solution)/shard_map/ppermute | solution.py:782
  9.1 2.2 %collective-permute-start.3 = (f32[13,8,512]{2,1,0:T(8,128)S(1)}, f32[13,8,512]{2,1,0:T(8,128)S(1)}, u32[]{:S(2)}, u32[]{:S(2)}) collective-permute-start(f32[13,8,512]{2,1,0:T(8,128)S(1)} %get-tuple-element.34), channel_id=1, source_target_pairs={{0,24},{8,0},{16,8},{24,16},{1,25},{9,1},{17,9},{25,17},{2,26},{10... | collective-permute-start | bytes 638984 | tf_op jit(solution)/shard_map/ppermute | solution.py:783
  11.3 4.2 %collide.1 = (f32[26,8,8,512]{3,2,1,0:T(8,128)S(1)}, f32[26,8,8,512]{3,2,1,0:T(8,128)S(1)}, f32[8,8,512]{2,1,0:T(8,128)S(1)}, f32[8,8,512]{2,1,0:T(8,128)S(1)}, ...) custom-call(f32[19,8,8,512]{3,2,1,0:T(8,128)} %flow_ref.3, f32[7,8,8,512]{3,2,1,0:T(8,128)} %field_ref.3, ...), custom_call_target="tpu_custom_call" | custom-call | flops 9830400 | bytes 10223616 | tf_op jit(solution)/shard_map/collide/pallas_call | solution.py:319
  15.5 0.0 collective-permute-done.first_ref
  15.5 0.0 collective-permute-done.1.second_ref
  15.5 0.1 collective-permute-start.4
  15.6 3.8 %collective-permute-start.5 = (f32[8,512]{1,0:T(8,128)S(1)}, f32[8,512]{1,0:T(8,128)S(1)}, u32[]{:S(2)}, u32[]{:S(2)}) collective-permute-start(f32[8,512]{1,0:T(8,128)S(1)} %get-tuple-element.36), channel_id=1, source_target_pairs={{0,24},{8,0},{16,8},{24,16},{1,25},{9,1},{17,9},{25,17},{2,26},{10... | collective-permute-start | bytes 49160 | tf_op jit(solution)/shard_map/ppermute | solution.py:787
  19.4 3.8 %inner.1 = (f32[19,8,8,512]{3,2,1,0:T(8,128)}, f32[7,8,8,512]{3,2,1,0:T(8,128)}, f32[19,8,8,512]{3,2,1,0:T(8,128)}, f32[7,8,8,512]{3,2,1,0:T(8,128)}, f32[32,8,128]{2,1,0:T(8,128)S(1)}) custom-call(f32[26,8,8,512]{3,2,1,0:T(8,128)S(1)} %get-tuple-element.27.post_ref, f32[26,8,8,512]{3,2,1,0:T(8,128)S(1)} %get-tuple-element.28.adj_ref, ...), custom_call_target="tpu_custom_call" | custom-call | flops 22937600 | bytes 13631488 | tf_op jit(solution)/shard_map/inner/pallas_call | solution.py:640
  23.2 0.0 collective-permute-done.2.fromleft_ref
  23.2 0.0 collective-permute-done.3.fromright_ref
  23.2 0.0 collective-permute-done.4.cornerleft_ref
  23.2 0.0 collective-permute-done.5.cornerright_ref
  23.2 1.9 %outer.1 = (f32[19,8,8,512]{3,2,1,0:T(8,128)}, f32[7,8,8,512]{3,2,1,0:T(8,128)}, f32[19,8,8,512]{3,2,1,0:T(8,128)}, f32[7,8,8,512]{3,2,1,0:T(8,128)}, f32[32,32]{1,0:T(8,128)S(1)}) custom-call(f32[26,8,8,512]{3,2,1,0:T(8,128)S(1)} %get-tuple-element.27.post_ref, ...), custom_call_target="tpu_custom_call", output_to_operand_aliasing={{0}: (13, {}), {1}: (14, {}), {2}: (15, {}), {3}: (16, {})} | custom-call | tf_op jit(solution)/shard_map/outer/pallas_call | solution.py:740
  25.1 9.0 %all_to_all.9 = f32[32,1,32]{2,1,0:T(1,128)S(1)} all-to-all(f32[32,1,32]{2,1,0:T(1,128)S(1)} %bitcast.4), channel_id=1, replica_groups=mesh['gx'=4,'gy'=8] {'gx','gy'}, dimensions={0} | all-to-all | bytes 8192 | tf_op jit(solution)/shard_map/all_to_all | solution.py:796
  34.1 0.6 %reduce_sum.9 = f32[32]{0:T(128)} reduce(f32[32,1,32]{2,1,0:T(1,128)S(1)} %all_to_all.9, f32[]{:T(128)} %constant.0.clone.1), dimensions={0,1}, to_apply=%region_0.0 | reduce | flops 992 | bytes 4228 | tf_op jit(solution)/shard_map/reduce_sum | solution.py:796
  (1 shorter events, 0.0 us)
Async XLA Ops:
  3.4 12.1 %collective-permute-start = (f32[13,8,512]{2,1,0:T(8,128)S(1)}, f32[13,8,512]{2,1,0:T(8,128)S(1)}, u32[]{:S(2)}, u32[]{:S(2)}) collective-permute-start(f32[13,8,512]{2,1,0:T(8,128)S(1)} %get-tuple-element.31), channel_id=1, source_target_pairs={{0,1},{1,0},{2,3},{3,2},{4,5},{5,4},{6,7},{7,6},{8,9},{9,8},{10,11... | collective-permute-start | bytes 638984 | tf_op jit(solution)/shard_map/ppermute | solution.py:781
  3.9 11.6 %collective-permute-start.1 = (f32[13,8,512]{2,1,0:T(8,128)S(1)}, f32[13,8,512]{2,1,0:T(8,128)S(1)}, u32[]{:S(2)}, u32[]{:S(2)}) collective-permute-start(f32[13,8,512]{2,1,0:T(8,128)S(1)} %get-tuple-element.32), channel_id=1, source_target_pairs={{0,7},{1,2},{2,1},{3,4},{4,3},{5,6},{6,5},{7,0},{8,15},{9,10},{10,... | collective-permute-start | bytes 638984 | tf_op jit(solution)/shard_map/ppermute | solution.py:780
  7.5 15.7 %collective-permute-start.2 = (f32[13,8,512]{2,1,0:T(8,128)S(1)}, f32[13,8,512]{2,1,0:T(8,128)S(1)}, u32[]{:S(2)}, u32[]{:S(2)}) collective-permute-start(f32[13,8,512]{2,1,0:T(8,128)S(1)} %get-tuple-element.33), channel_id=1, source_target_pairs={{0,8},{8,16},{16,24},{24,0},{1,9},{9,17},{17,25},{25,1},{2,10},{10... | collective-permute-start | bytes 638984 | tf_op jit(solution)/shard_map/ppermute | solution.py:782
  9.1 14.2 %collective-permute-start.3 = (f32[13,8,512]{2,1,0:T(8,128)S(1)}, f32[13,8,512]{2,1,0:T(8,128)S(1)}, u32[]{:S(2)}, u32[]{:S(2)}) collective-permute-start(f32[13,8,512]{2,1,0:T(8,128)S(1)} %get-tuple-element.34), channel_id=1, source_target_pairs={{0,24},{8,0},{16,8},{24,16},{1,25},{9,1},{17,9},{25,17},{2,26},{10... | collective-permute-start | bytes 638984 | tf_op jit(solution)/shard_map/ppermute | solution.py:783
  15.5 7.7 %collective-permute-start.4 = (f32[8,512]{1,0:T(8,128)S(1)}, f32[8,512]{1,0:T(8,128)S(1)}, u32[]{:S(2)}, u32[]{:S(2)}) collective-permute-start(f32[8,512]{1,0:T(8,128)S(1)} %get-tuple-element.35), channel_id=1, source_target_pairs={{0,8},{8,16},{16,24},{24,0},{1,9},{9,17},{17,25},{25,1},{2,10},{10... | collective-permute-start | bytes 49160 | tf_op jit(solution)/shard_map/ppermute | solution.py:786
  15.6 7.6 %collective-permute-start.5 = (f32[8,512]{1,0:T(8,128)S(1)}, f32[8,512]{1,0:T(8,128)S(1)}, u32[]{:S(2)}, u32[]{:S(2)}) collective-permute-start(f32[8,512]{1,0:T(8,128)S(1)} %get-tuple-element.36), channel_id=1, source_target_pairs={{0,24},{8,0},{16,8},{24,16},{1,25},{9,1},{17,9},{25,17},{2,26},{10... | collective-permute-start | bytes 49160 | tf_op jit(solution)/shard_map/ppermute | solution.py:787

commit v6 on v5

--- a/solution.py
+++ b/solution.py
@@ -47,10 +47,10 @@
 SLOTS = 13
 MASK = 12
 
-RIM_VMEM = 60 << 20
-COLLIDE_VMEM = 48 << 20
-INNER_VMEM = 42 << 20
-OUTER_VMEM = 42 << 20
+RIM_VMEM = 58 << 20
+COLLIDE_VMEM = 4 << 20
+INNER_VMEM = 12 << 20
+OUTER_VMEM = 8 << 20
 
 
 def weight(i):
@@ -269,71 +269,40 @@
 
 
 def collide_kernel(
-    flow_ref, field_ref, adjf_ref, adjg_ref, profile_ref, strengths_ref, wall_ref, magnet_ref,
-    post_ref, adj_ref, fluid_ref, bcell_ref, profile_v, magnet_v,
-    flow_v, field_v, wall_v, plane_sem, adj_sem,
+    flow_ref, field_ref, profile_ref, strengths_ref, wall_ref, magnet_ref,
+    post_ref, fluid_ref, bcell_ref,
 ):
-    sx = fluid_ref.shape[0]
-
-    def loads(x):
-        pairs = (
-            (wall_ref.at[x], wall_v.at[x]),
-            (magnet_ref.at[x], magnet_v.at[x]),
-            (profile_ref.at[x], profile_v.at[x]),
-            (flow_ref.at[:, x], flow_v.at[:, x]),
-            (field_ref.at[:, x], field_v.at[:, x]),
-        )
-        return [pltpu.make_async_copy(a, b, plane_sem.at[n, x]) for n, (a, b) in enumerate(pairs)]
-
-    for x in range(sx):
-        start_all(loads(x))
-    adj_loads = [
-        pltpu.make_async_copy(adjf_ref, adj_ref.at[pl.ds(0, NF)], adj_sem.at[0]),
-        pltpu.make_async_copy(adjg_ref, adj_ref.at[pl.ds(NF, NG)], adj_sem.at[1]),
-    ]
-    start_all(adj_loads)
     table = lane_table(strengths_ref)
 
     def body(x, carry):
-        wait_all(loads(x))
-        fluid = 1.0 - wall_v[x].astype(jnp.float32)
-        bcell = gather_strength(table, magnet_v[x]) * profile_v[x]
+        fluid = 1.0 - wall_ref[x].astype(jnp.float32)
+        bcell = gather_strength(table, magnet_ref[x]) * profile_ref[x]
         fluid_ref[x] = fluid
         bcell_ref[x] = bcell
-        f = [flow_v[i, x] for i in range(NF)]
-        g = [field_v[k, x] for k in range(NG)]
+        f = [flow_ref[i, x] for i in range(NF)]
+        g = [field_ref[k, x] for k in range(NG)]
         for i, value in collide(f, g, fluid, bcell, range(NP)).items():
             post_ref[i, x] = value
         return carry
 
-    lax.fori_loop(0, sx, body, 0)
-    wait_all(adj_loads)
-
-
-def collide_call(flow, field, adjf, adjg, profile, strengths, wall, magnet):
+    lax.fori_loop(0, fluid_ref.shape[0], body, 0)
+
+
+def collide_call(flow, field, profile, strengths, wall, magnet):
     sx, sy, sz = profile.shape
     full = pltpu.VMEM((NP, sx, sy, sz), jnp.float32)
     cells = pltpu.VMEM((sx, sy, sz), jnp.float32)
-    names = pltpu.VMEM((sx, sy, sz), jnp.int32)
-    dma = pltpu.SemaphoreType.DMA
     return pl.pallas_call(
         collide_kernel,
-        in_specs=[ANY, ANY, ANY, ANY, ANY, VMEM, ANY, ANY],
-        out_specs=[VMEM] * 6,
-        out_shape=[full, full, cells, cells, cells, names],
-        scratch_shapes=[
-            pltpu.VMEM(flow.shape, jnp.float32),
-            pltpu.VMEM(field.shape, jnp.float32),
-            names,
-            dma((5, sx)),
-            dma((2,)),
-        ],
+        in_specs=[VMEM] * 6,
+        out_specs=[VMEM] * 3,
+        out_shape=[full, cells, cells],
         compiler_params=pltpu.CompilerParams(vmem_limit_bytes=COLLIDE_VMEM),
         cost_estimate=pl.CostEstimate(
             flops=300 * sx * sy * sz, bytes_accessed=12 * NP * sx * sy * sz, transcendentals=0
         ),
         name="collide",
-    )(flow, field, adjf, adjg, profile, strengths, wall, magnet)
+    )(flow, field, profile, strengths, wall, magnet)
 
 
 CORNER_RIGHT = ((0, 7, 0, 8), (1, 9, 1, 10))
@@ -564,6 +533,10 @@
     return names.index(i) + 6 * kind
 
 
+def adj_plane(adjf_ref, adjg_ref, i, x):
+    return adjf_ref[i, x] if i < NF else adjg_ref[i - NF, x]
+
+
 def load_halo(first_ref, second_ref, halo_ref):
     odd = lax.rem(lax.axis_index("gy"), 2)
     halo_ref[1 - odd] = first_ref[...]
@@ -587,7 +560,8 @@
 
 
 def inner_kernel(
-    post_ref, adj_ref, fluid_ref, bcell_ref, first_ref, second_ref, profile_ref, magnet_ref,
+    post_ref, adjf_ref, adjg_ref, fluid_ref, bcell_ref, first_ref, second_ref, profile_ref,
+    magnet_ref,
     newf_ref, newg_ref, outf_ref, outg_ref, sums_ref,
     new_v, out_v, halo_v, near_v, store_sem,
 ):
@@ -610,7 +584,7 @@
             x,
             lambda i, dx: post_ref[i, x + dx],
             lambda i, dx, dy: row_of(halo_slot(0, i, dy), dx, dy),
-            lambda i, dx: adj_ref[i, x + dx],
+            lambda i, dx: adj_plane(adjf_ref, adjg_ref, i, x + dx),
             lambda i, dx, dy: row_of(halo_slot(1, i, dy), dx, dy),
             lambda dx: fluid_ref[x + dx],
             lambda dx, dy: row_of(MASK, dx, dy),
@@ -632,14 +606,14 @@
         wait_all(stores(x))
 
 
-def inner_call(post, adj, fluid, bcell, first, second, profile, magnet, count):
+def inner_call(post, adjf, adjg, fluid, bcell, first, second, profile, magnet, count):
     sx, sy, sz = profile.shape
     full = pltpu.VMEM((NP, sx, sy, sz), jnp.float32)
     flow = jax.ShapeDtypeStruct((NF, sx, sy, sz), jnp.float32)
     field = jax.ShapeDtypeStruct((NG, sx, sy, sz), jnp.float32)
     return pl.pallas_call(
         inner_kernel,
-        in_specs=[VMEM] * 8,
+        in_specs=[VMEM] * 9,
         out_specs=[ANY, ANY, ANY, ANY, VMEM],
         out_shape=[flow, field, flow, field, pltpu.VMEM((count, 8, 128), jnp.float32)],
         scratch_shapes=[
@@ -654,11 +628,11 @@
             flops=700 * sx * sy * sz, bytes_accessed=16 * NP * sx * sy * sz, transcendentals=0
         ),
         name="inner",
-    )(post, adj, fluid, bcell, first, second, profile, magnet)
+    )(post, adjf, adjg, fluid, bcell, first, second, profile, magnet)
 
 
 def outer_kernel(
-    scale, post_ref, adj_ref, fluid_ref, bcell_ref, first_ref, second_ref, fromleft_ref, fromright_ref,
+    scale, post_ref, adjf_ref, adjg_ref, fluid_ref, bcell_ref, first_ref, second_ref, fromleft_ref, fromright_ref,
     cornerleft_ref, cornerright_ref, profile_ref, magnet_ref,
     partial_ref, newf_in, newg_in, outf_in, outg_in,
     newf_ref, newg_ref, outf_ref, outg_ref, share_ref,
@@ -675,10 +649,12 @@
             (fromleft_ref, cornerleft_ref) if away == -1 else (fromright_ref, cornerright_ref)
         )
 
-        def get(kind, i, dx, held, x=x, away=away, face_ref=face_ref):
+        def get(kind, i, dx, x=x, away=away, face_ref=face_ref):
             if dx == away:
                 return face_ref[face_slot(kind, i, dx)]
-            return held[i, x + dx]
+            if kind == 1:
+                return adj_plane(adjf_ref, adjg_ref, i, x + dx)
+            return post_ref[i, x + dx]
 
         def row(kind, i, dx, dy, x=x, away=away, corner_ref=corner_ref):
             side = 0 if dy == -1 else 1
@@ -695,9 +671,9 @@
 
         plane_step(
             n,
-            lambda i, dx, get=get: get(0, i, dx, post_ref),
+            lambda i, dx, get=get: get(0, i, dx),
             lambda i, dx, dy, row=row: row(0, i, dx, dy),
-            lambda i, dx, get=get: get(1, i, dx, adj_ref),
+            lambda i, dx, get=get: get(1, i, dx),
             lambda i, dx, dy, row=row: row(1, i, dx, dy),
             mask,
             lambda dx, dy, row=row: row(2, 0, dx, dy),
@@ -730,8 +706,8 @@
 
 
 def outer_call(
-    post, adj, fluid, bcell, first, second, fromleft, fromright, cornerleft, cornerright, profile,
-    magnet, partial, newf, newg, outf, outg, scale,
+    post, adjf, adjg, fluid, bcell, first, second, fromleft, fromright, cornerleft, cornerright,
+    profile, magnet, partial, newf, newg, outf, outg, scale,
 ):
     sx, sy, sz = profile.shape
     count = partial.shape[0]
@@ -739,7 +715,7 @@
     field = jax.ShapeDtypeStruct(newg.shape, jnp.float32)
     return pl.pallas_call(
         functools.partial(outer_kernel, scale),
-        in_specs=[VMEM] * 13 + [ANY] * 4,
+        in_specs=[VMEM] * 14 + [ANY] * 4,
         out_specs=[ANY] * 4 + [VMEM],
         out_shape=[
             flow,
@@ -748,7 +724,7 @@
             field,
             jax.ShapeDtypeStruct((lax.axis_size(("gx", "gy")), count), jnp.float32),
         ],
-        input_output_aliases={13: 0, 14: 1, 15: 2, 16: 3},
+        input_output_aliases={14: 0, 15: 1, 16: 2, 17: 3},
         scratch_shapes=[
             pltpu.VMEM((NP, 2, sy, sz), jnp.float32),
             pltpu.VMEM((NP, 2, sy, sz), jnp.float32),
@@ -760,7 +736,7 @@
         compiler_params=pltpu.CompilerParams(vmem_limit_bytes=OUTER_VMEM),
         name="outer",
     )(
-        post, adj, fluid, bcell, first, second, fromleft, fromright, cornerleft, cornerright,
+        post, adjf, adjg, fluid, bcell, first, second, fromleft, fromright, cornerleft, cornerright,
         profile, magnet, partial, newf, newg, outf, outg,
     )
 
@@ -781,16 +757,16 @@
     first = lax.ppermute(mine1, "gy", inside)
     fromleft = lax.ppermute(right, "gx", ring(around, 1))
     fromright = lax.ppermute(left, "gx", ring(around, -1))
-    post, adj, fluid, bcell, profile, magnet = collide_call(*arrays)
+    post, fluid, bcell = collide_call(flow, field, profile, table, wall, magnet)
     corner_r, corner_l = corner_call(first, second, bcell)
     cornerleft = lax.ppermute(corner_r, "gx", ring(around, 1))
     cornerright = lax.ppermute(corner_l, "gx", ring(around, -1))
     newf, newg, outf, outg, partial = inner_call(
-        post, adj, fluid, bcell, first, second, profile, magnet, count
+        post, adj_flow_in, adj_field_in, fluid, bcell, first, second, profile, magnet, count
     )
     cells = flow.shape[1] * around * flow.shape[2] * across * flow.shape[3]
     newf, newg, outf, outg, share = outer_call(
-        post, adj, fluid, bcell, first, second, fromleft, fromright, cornerleft, cornerright,
+        post, adj_flow_in, adj_field_in, fluid, bcell, first, second, fromleft, fromright, cornerleft, cornerright,
         profile, magnet, partial, newf, newg, outf, outg, 1.0 / math.sqrt(cells / count),
     )
     totals = jnp.sum(lax.all_to_all(share, ("gx", "gy"), 0, 0, tiled=True), axis=0)

time: 35 us -> 34.1 us (0.974)
  Pallas kernels: 12.6 us -> 10 us
  blocking collectives: 9.03 us -> 10.1 us
  waiting for transfers between devices: 0.02 us -> 0.49 us
    pallas_call x2, Pallas kernels: 7.95 us -> 4.97 us  [the longest x1 3.78 us: inner_call(): pl.pallas_call(inner_kernel, in_specs=[VMEM] * 9, out_specs=[ANY, ANY, AN...]
    ppermute x1, starting transfers between devices: 0.06 us -> 1.89 us  [on_device(): cornerleft = lax.ppermute(corner_r, 'gx', ring(around, 1))]
    ppermute x1, starting transfers between devices: 3.81 us -> 2.09 us  [on_device(): cornerright = lax.ppermute(corner_l, 'gx', ring(around, -1))]
    all_to_all x1, blocking collectives: 9.03 us -> 10.1 us  [on_device(): lax.all_to_all(share, ('gx', 'gy'), 0, 0, tiled=True)]
    ppermute x1, waiting for transfers between devices: 0.01 us -> 0.48 us  [on_device(): cornerleft = lax.ppermute(corner_r, 'gx', ring(around, 1))]
    pallas_call x1, Pallas kernels: 2.76 us -> 3.22 us  [rim_call(): pl.pallas_call(rim_kernel, in_specs=[ANY, ANY, ANY, ANY, ANY, VMEM, ANY,...]
  transfers between devices with their start and end apart: 6 -> 6, of which waited for: 0 -> 1; matrix products, arithmetic and copies ran while one was open for 0% -> 0% of each run, Pallas kernels for 23% -> 15%
where the time goes in v6:
time: 34.1 us; the launch traced here: 33.9 us
  starting transfers between devices  11.9 us (35%)
  blocking collectives  10.1 us (30%)
  Pallas kernels  10 us (29%)
  between operations  0.79 us (2%)
  other arithmetic  0.56 us (2%)
  waiting for transfers between devices  0.49 us (1%)
    all_to_all x1, blocking collectives, on_device(): lax.all_to_all(share, ('gx', 'gy'), 0, 0, tiled=True)  10.1 us
    pallas_call x1, Pallas kernels, inner_call(): pl.pallas_call(inner_kernel, in_specs=[VMEM] * 9, out_specs=[ANY, ANY, AN...  3.78 us
    ppermute x1, starting transfers between devices, on_device(): second = lax.ppermute(mine2, 'gy', between)  3.56 us
    pallas_call x1, Pallas kernels, rim_call(): pl.pallas_call(rim_kernel, in_specs=[ANY, ANY, ANY, ANY, ANY, VMEM, ANY,...  3.22 us
    ppermute x1, starting transfers between devices, on_device(): fromright = lax.ppermute(left, 'gx', ring(around, -1))  2.25 us
    ppermute x1, starting transfers between devices, on_device(): cornerright = lax.ppermute(corner_l, 'gx', ring(around, -1))  2.09 us
    ppermute x1, starting transfers between devices, on_device(): cornerleft = lax.ppermute(corner_r, 'gx', ring(around, 1))  1.89 us
    pallas_call x1, Pallas kernels, outer_call(): pl.pallas_call(functools.partial(outer_kernel, scale), in_specs=[VMEM] *...  1.84 us
  transfers between devices with their start and end apart: 6, of which 1 were waited for; matrix products, arithmetic and copies ran while one was open for 0% of the time, Pallas kernels for 15%

profile of v6, /device:TPU:0, one launch (start us, length us, event | category | flops | bytes accessed | tf_op | source)
XLA Modules:
  0.0 33.9 jit_solution(16539678239759781101)
XLA Ops:
  0.7 3.2 %rims.1 = (f32[13,8,512]{2,1,0:T(8,128)S(1)}, f32[13,8,512]{2,1,0:T(8,128)S(1)}, f32[13,8,512]{2,1,0:T(8,128)S(1)}, f32[13,8,512]{2,1,0:T(8,128)S(1)}) custom-call(f32[19,8,8,512]{3,2,1,0:T(8,128)} %flow_ref.3, f32[7,8,8,512]{3,2,1,0:T(8,128)} %field_ref.3, f32[19,8,8,512]{3,2,1,0:T(8,128)} %adjf_ref.5, f32[7,8,8,512]{3,2,1,0:T(8,128)} %adjg_ref.5, ...), custom_call_target="tpu_custom_call" | custom-call | tf_op jit(solution)/shard_map/rims/pallas_call | solution.py:249
  3.9 0.0 copy-start
  3.9 0.0 copy-start.2
  3.9 0.5 %collective-permute-start = (f32[13,8,512]{2,1,0:T(8,128)S(1)}, f32[13,8,512]{2,1,0:T(8,128)S(1)}, u32[]{:S(2)}, u32[]{:S(2)}) collective-permute-start(f32[13,8,512]{2,1,0:T(8,128)S(1)} %get-tuple-element.27), channel_id=1, source_target_pairs={{0,1},{1,0},{2,3},{3,2},{4,5},{5,4},{6,7},{7,6},{8,9},{9,8},{10,11... | collective-permute-start | bytes 638984 | tf_op jit(solution)/shard_map/ppermute | solution.py:757
  4.5 3.6 %collective-permute-start.1 = (f32[13,8,512]{2,1,0:T(8,128)S(1)}, f32[13,8,512]{2,1,0:T(8,128)S(1)}, u32[]{:S(2)}, u32[]{:S(2)}) collective-permute-start(f32[13,8,512]{2,1,0:T(8,128)S(1)} %get-tuple-element.28), channel_id=1, source_target_pairs={{0,7},{1,2},{2,1},{3,4},{4,3},{5,6},{6,5},{7,0},{8,15},{9,10},{10,... | collective-permute-start | bytes 638984 | tf_op jit(solution)/shard_map/ppermute | solution.py:756
  8.0 1.6 %collective-permute-start.2 = (f32[13,8,512]{2,1,0:T(8,128)S(1)}, f32[13,8,512]{2,1,0:T(8,128)S(1)}, u32[]{:S(2)}, u32[]{:S(2)}) collective-permute-start(f32[13,8,512]{2,1,0:T(8,128)S(1)} %get-tuple-element.29), channel_id=1, source_target_pairs={{0,8},{8,16},{16,24},{24,0},{1,9},{9,17},{17,25},{25,1},{2,10},{10... | collective-permute-start | bytes 638984 | tf_op jit(solution)/shard_map/ppermute | solution.py:758
  9.6 2.2 %collective-permute-start.3 = (f32[13,8,512]{2,1,0:T(8,128)S(1)}, f32[13,8,512]{2,1,0:T(8,128)S(1)}, u32[]{:S(2)}, u32[]{:S(2)}) collective-permute-start(f32[13,8,512]{2,1,0:T(8,128)S(1)} %get-tuple-element.30), channel_id=1, source_target_pairs={{0,24},{8,0},{16,8},{24,16},{1,25},{9,1},{17,9},{25,17},{2,26},{10... | collective-permute-start | bytes 638984 | tf_op jit(solution)/shard_map/ppermute | solution.py:759
  11.8 0.0 copy-done.5
  11.9 0.0 copy-done.6
  11.9 0.0 copy-done.7
  11.9 1.2 %collide.1 = (f32[26,8,8,512]{3,2,1,0:T(8,128)S(1)}, f32[8,8,512]{2,1,0:T(8,128)S(1)}, f32[8,8,512]{2,1,0:T(8,128)S(1)}) custom-call(f32[19,8,8,512]{3,2,1,0:T(8,128)S(1)} %copy-done.1, f32[7,8,8,512]{3,2,1,0:T(8,128)S(1)} %copy-done.3, f32[8,8,512]{2,1,0:T(8,128)S(1)} %copy-done.4, f32[1,32]{1,0:T(1,128)S(1)} %bitcast.6, s32[8,8,512]{2,1,0:T(8,128)S(1)} %copy-done.6, ...), custom_call_target="tpu_custom_call" | custom-call | flops 9830400 | bytes 10223616 | tf_op jit(solution)/shard_map/collide/pallas_call | solution.py:295
  13.1 0.0 collective-permute-done.first_ref
  13.1 0.0 collective-permute-done.1.second_ref
  13.1 1.9 %collective-permute-start.4 = (f32[8,512]{1,0:T(8,128)S(1)}, f32[8,512]{1,0:T(8,128)S(1)}, u32[]{:S(2)}, u32[]{:S(2)}) collective-permute-start(f32[8,512]{1,0:T(8,128)S(1)} %get-tuple-element.31), channel_id=1, source_target_pairs={{0,8},{8,16},{16,24},{24,0},{1,9},{9,17},{17,25},{25,1},{2,10},{10... | collective-permute-start | bytes 49160 | tf_op jit(solution)/shard_map/ppermute | solution.py:762
  15.0 2.1 %collective-permute-start.5 = (f32[8,512]{1,0:T(8,128)S(1)}, f32[8,512]{1,0:T(8,128)S(1)}, u32[]{:S(2)}, u32[]{:S(2)}) collective-permute-start(f32[8,512]{1,0:T(8,128)S(1)} %get-tuple-element.32), channel_id=1, source_target_pairs={{0,24},{8,0},{16,8},{24,16},{1,25},{9,1},{17,9},{25,17},{2,26},{10... | collective-permute-start | bytes 49160 | tf_op jit(solution)/shard_map/ppermute | solution.py:763
  17.1 0.0 copy-done.2
  17.1 3.8 %inner.1 = (f32[19,8,8,512]{3,2,1,0:T(8,128)}, f32[7,8,8,512]{3,2,1,0:T(8,128)}, f32[19,8,8,512]{3,2,1,0:T(8,128)}, f32[7,8,8,512]{3,2,1,0:T(8,128)}, f32[32,8,128]{2,1,0:T(8,128)S(1)}) custom-call(f32[26,8,8,512]{3,2,1,0:T(8,128)S(1)} %get-tuple-element.24.post_ref, f32[19,8,8,512]{3,2,1,0:T(8,128)S(1)} %copy-done, f32[7,8,8,512]{3,2,1,0:T(8,128)S(1)} %copy-done.2, ...), custom_call_target="tpu_custom_call" | custom-call | flops 22937600 | bytes 13631488 | tf_op jit(solution)/shard_map/inner/pallas_call | solution.py:614
  20.9 0.0 collective-permute-done.2.fromleft_ref
  20.9 0.0 collective-permute-done.3.fromright_ref
  20.9 0.5 %collective-permute-done.4.cornerleft_ref = f32[8,512]{1,0:T(8,128)S(1)} collective-permute-done((f32[8,512]{1,0:T(8,128)S(1)}, f32[8,512]{1,0:T(8,128)S(1)}, u32[]{:S(2)}, u32[]{:S(2)}) %collective-permute-start.4) | collective-permute-done | bytes 16416 | tf_op jit(solution)/shard_map/ppermute | solution.py:762
  21.4 0.0 collective-permute-done.5.cornerright_ref
  21.4 1.8 %outer.1 = (f32[19,8,8,512]{3,2,1,0:T(8,128)}, f32[7,8,8,512]{3,2,1,0:T(8,128)}, f32[19,8,8,512]{3,2,1,0:T(8,128)}, f32[7,8,8,512]{3,2,1,0:T(8,128)}, f32[32,32]{1,0:T(8,128)S(1)}) custom-call(f32[26,8,8,512]{3,2,1,0:T(8,128)S(1)} %get-tuple-element.24.post_ref, ...), custom_call_target="tpu_custom_call", output_to_operand_aliasing={{0}: (14, {}), {1}: (15, {}), {2}: (16, {}), {3}: (17, {})} | custom-call | tf_op jit(solution)/shard_map/outer/pallas_call | solution.py:716
  23.2 10.1 %all_to_all.9 = f32[32,1,32]{2,1,0:T(1,128)S(1)} all-to-all(f32[32,1,32]{2,1,0:T(1,128)S(1)} %bitcast.4), channel_id=1, replica_groups=mesh['gx'=4,'gy'=8] {'gx','gy'}, dimensions={0} | all-to-all | bytes 8192 | tf_op jit(solution)/shard_map/all_to_all | solution.py:772
  33.3 0.6 %reduce_sum.9 = f32[32]{0:T(128)} reduce(f32[32,1,32]{2,1,0:T(1,128)S(1)} %all_to_all.9, f32[]{:T(128)} %constant.0.clone.1), dimensions={0,1}, to_apply=%region_0.0 | reduce | flops 992 | bytes 4228 | tf_op jit(solution)/shard_map/reduce_sum | solution.py:772
  (11 shorter events, 0.0 us)
Async XLA Ops:
  0.6 11.2 %copy-start.1 = (f32[19,8,8,512]{3,2,1,0:T(8,128)S(1)}, f32[19,8,8,512]{3,2,1,0:T(8,128)}, u32[]{:S(2)}) copy-start(f32[19,8,8,512]{3,2,1,0:T(8,128)} %flow_ref.3) | copy-start | bytes 7471108
  0.6 11.2 %copy-start.3 = (f32[7,8,8,512]{3,2,1,0:T(8,128)S(1)}, f32[7,8,8,512]{3,2,1,0:T(8,128)}, u32[]{:S(2)}) copy-start(f32[7,8,8,512]{3,2,1,0:T(8,128)} %field_ref.3) | copy-start | bytes 2752516
  0.7 11.2 %copy-start.4 = (f32[8,8,512]{2,1,0:T(8,128)S(1)}, f32[8,8,512]{2,1,0:T(8,128)}, u32[]{:S(2)}) copy-start(f32[8,8,512]{2,1,0:T(8,128)} %profile_ref.7) | copy-start | bytes 393220
  0.7 11.2 %copy-start.5 = (s32[8,8,512]{2,1,0:T(8,128)S(1)}, s32[8,8,512]{2,1,0:T(8,128)}, u32[]{:S(2)}) copy-start(s32[8,8,512]{2,1,0:T(8,128)} %magnet_ref.7) | copy-start | bytes 393220
  0.7 11.2 %copy-start.6 = (s32[8,8,512]{2,1,0:T(8,128)S(1)}, s32[8,8,512]{2,1,0:T(8,128)}, u32[]{:S(2)}) copy-start(s32[8,8,512]{2,1,0:T(8,128)} %wall_ref.3) | copy-start | bytes 393220
  0.7 11.2 %copy-start.7 = (f32[32]{0:T(128)S(1)}, f32[32]{0:T(128)}, u32[]{:S(2)}) copy-start(f32[32]{0:T(128)} %param.13) | copy-start | bytes 388
  3.9 13.2 %copy-start = (f32[19,8,8,512]{3,2,1,0:T(8,128)S(1)}, f32[19,8,8,512]{3,2,1,0:T(8,128)}, u32[]{:S(2)}) copy-start(f32[19,8,8,512]{3,2,1,0:T(8,128)} %adjf_ref.5) | copy-start | bytes 7471108
  3.9 13.2 %copy-start.2 = (f32[7,8,8,512]{3,2,1,0:T(8,128)S(1)}, f32[7,8,8,512]{3,2,1,0:T(8,128)}, u32[]{:S(2)}) copy-start(f32[7,8,8,512]{3,2,1,0:T(8,128)} %adjg_ref.5) | copy-start | bytes 2752516
  3.9 9.1 %collective-permute-start = (f32[13,8,512]{2,1,0:T(8,128)S(1)}, f32[13,8,512]{2,1,0:T(8,128)S(1)}, u32[]{:S(2)}, u32[]{:S(2)}) collective-permute-start(f32[13,8,512]{2,1,0:T(8,128)S(1)} %get-tuple-element.27), channel_id=1, source_target_pairs={{0,1},{1,0},{2,3},{3,2},{4,5},{5,4},{6,7},{7,6},{8,9},{9,8},{10,11... | collective-permute-start | bytes 638984 | tf_op jit(solution)/shard_map/ppermute | solution.py:757
  4.5 8.6 %collective-permute-start.1 = (f32[13,8,512]{2,1,0:T(8,128)S(1)}, f32[13,8,512]{2,1,0:T(8,128)S(1)}, u32[]{:S(2)}, u32[]{:S(2)}) collective-permute-start(f32[13,8,512]{2,1,0:T(8,128)S(1)} %get-tuple-element.28), channel_id=1, source_target_pairs={{0,7},{1,2},{2,1},{3,4},{4,3},{5,6},{6,5},{7,0},{8,15},{9,10},{10,... | collective-permute-start | bytes 638984 | tf_op jit(solution)/shard_map/ppermute | solution.py:756
  8.0 12.9 %collective-permute-start.2 = (f32[13,8,512]{2,1,0:T(8,128)S(1)}, f32[13,8,512]{2,1,0:T(8,128)S(1)}, u32[]{:S(2)}, u32[]{:S(2)}) collective-permute-start(f32[13,8,512]{2,1,0:T(8,128)S(1)} %get-tuple-element.29), channel_id=1, source_target_pairs={{0,8},{8,16},{16,24},{24,0},{1,9},{9,17},{17,25},{25,1},{2,10},{10... | collective-permute-start | bytes 638984 | tf_op jit(solution)/shard_map/ppermute | solution.py:758
  9.6 11.3 %collective-permute-start.3 = (f32[13,8,512]{2,1,0:T(8,128)S(1)}, f32[13,8,512]{2,1,0:T(8,128)S(1)}, u32[]{:S(2)}, u32[]{:S(2)}) collective-permute-start(f32[13,8,512]{2,1,0:T(8,128)S(1)} %get-tuple-element.30), channel_id=1, source_target_pairs={{0,24},{8,0},{16,8},{24,16},{1,25},{9,1},{17,9},{25,17},{2,26},{10... | collective-permute-start | bytes 638984 | tf_op jit(solution)/shard_map/ppermute | solution.py:759
  13.1 8.3 %collective-permute-start.4 = (f32[8,512]{1,0:T(8,128)S(1)}, f32[8,512]{1,0:T(8,128)S(1)}, u32[]{:S(2)}, u32[]{:S(2)}) collective-permute-start(f32[8,512]{1,0:T(8,128)S(1)} %get-tuple-element.31), channel_id=1, source_target_pairs={{0,8},{8,16},{16,24},{24,0},{1,9},{9,17},{17,25},{25,1},{2,10},{10... | collective-permute-start | bytes 49160 | tf_op jit(solution)/shard_map/ppermute | solution.py:762
  15.0 6.4 %collective-permute-start.5 = (f32[8,512]{1,0:T(8,128)S(1)}, f32[8,512]{1,0:T(8,128)S(1)}, u32[]{:S(2)}, u32[]{:S(2)}) collective-permute-start(f32[8,512]{1,0:T(8,128)S(1)} %get-tuple-element.32), channel_id=1, source_target_pairs={{0,24},{8,0},{16,8},{24,16},{1,25},{9,1},{17,9},{25,17},{2,26},{10... | collective-permute-start | bytes 49160 | tf_op jit(solution)/shard_map/ppermute | solution.py:763

commit v7 on v6

--- a/solution.py
+++ b/solution.py
@@ -47,8 +47,8 @@
 SLOTS = 13
 MASK = 12
 
-RIM_VMEM = 58 << 20
-COLLIDE_VMEM = 4 << 20
+RIM_VMEM = 63 << 20
+COLLIDE_VMEM = 54 << 20
 INNER_VMEM = 12 << 20
 OUTER_VMEM = 8 << 20
 
@@ -65,8 +65,8 @@
     return jnp.concatenate(parts, axis=1)
 
 
-def lane_table(strengths_ref):
-    row = strengths_ref[...]
+def lane_table(strengths_v):
+    row = strengths_v[...]
     rest = 128 - row.shape[1]
     if rest:
         row = jnp.concatenate([row, jnp.zeros((1, rest), jnp.float32)], axis=1)
@@ -146,7 +146,8 @@
 def rim_kernel(
     flow_ref, field_ref, adjf_ref, adjg_ref, profile_ref, strengths_ref, wall_ref, magnet_ref,
     first_ref, second_ref, right_ref, left_ref,
-    rows_v, faces_v, profile_v, wall_v, magnet_v, message_v, cell_sem, rows_sem, faces_sem, adj_sem,
+    rows_v, faces_v, profile_v, wall_v, magnet_v, strengths_v, message_v, cell_sem, rows_sem,
+    faces_sem, adj_sem,
 ):
     sx, sy = profile_v.shape[:2]
     odd = lax.rem(lax.axis_index("gy"), 2)
@@ -169,7 +170,12 @@
     cells = [
         pltpu.make_async_copy(a, b, cell_sem.at[n])
         for n, (a, b) in enumerate(
-            ((wall_ref, wall_v), (magnet_ref, magnet_v), (profile_ref, profile_v))
+            (
+                (wall_ref, wall_v),
+                (magnet_ref, magnet_v),
+                (strengths_ref, strengths_v),
+                (profile_ref, profile_v),
+            )
         )
     ]
     faces = []
@@ -198,8 +204,8 @@
     start_all(rows[2:])
     start_all(faces)
     start_all(adjs)
-    table = lane_table(strengths_ref)
     wait_all(cells)
+    table = lane_table(strengths_v)
     for n, (y, wanted) in enumerate(zip(ends, (UP, DOWN))):
         wait_all(rows[2 * n : 2 * n + 2])
         fluid = 1.0 - wall_v[:, y, :].astype(jnp.float32)
@@ -248,7 +254,7 @@
     dma = pltpu.SemaphoreType.DMA
     return pl.pallas_call(
         rim_kernel,
-        in_specs=[ANY, ANY, ANY, ANY, ANY, VMEM, ANY, ANY],
+        in_specs=[ANY] * 8,
         out_specs=[VMEM] * 4,
         out_shape=[rows, rows, faces, faces],
         scratch_shapes=[
@@ -257,8 +263,9 @@
             cells,
             names,
             names,
+            pltpu.VMEM(strengths.shape, jnp.float32),
             pltpu.VMEM((2, SLOTS, sx, sz), jnp.float32),
-            dma((3,)),
+            dma((4,)),
             dma((2, 2)),
             dma((2, 2)),
             dma((4, 6)),
@@ -270,33 +277,66 @@
 
 def collide_kernel(
     flow_ref, field_ref, profile_ref, strengths_ref, wall_ref, magnet_ref,
-    post_ref, fluid_ref, bcell_ref,
+    post_ref, fluid_ref, bcell_ref, profile_v, magnet_v,
+    flow_v, field_v, wall_v, strengths_v, plane_sem, table_sem,
 ):
-    table = lane_table(strengths_ref)
+    sx = fluid_ref.shape[0]
+
+    def loads(x):
+        pairs = (
+            (wall_ref.at[x], wall_v.at[x]),
+            (magnet_ref.at[x], magnet_v.at[x]),
+            (profile_ref.at[x], profile_v.at[x]),
+            (flow_ref.at[:, x], flow_v.at[:, x]),
+            (field_ref.at[:, x], field_v.at[:, x]),
+        )
+        return [pltpu.make_async_copy(a, b, plane_sem.at[n, x]) for n, (a, b) in enumerate(pairs)]
+
+    table_load = pltpu.make_async_copy(strengths_ref, strengths_v, table_sem.at[0])
+    table_load.start()
+    for x in range(sx):
+        start_all(loads(x))
+    table_load.wait()
+    table = lane_table(strengths_v)
 
     def body(x, carry):
-        fluid = 1.0 - wall_ref[x].astype(jnp.float32)
-        bcell = gather_strength(table, magnet_ref[x]) * profile_ref[x]
+        wait_all(loads(x))
+        fluid = 1.0 - wall_v[x].astype(jnp.float32)
+        bcell = gather_strength(table, magnet_v[x]) * profile_v[x]
         fluid_ref[x] = fluid
         bcell_ref[x] = bcell
-        f = [flow_ref[i, x] for i in range(NF)]
-        g = [field_ref[k, x] for k in range(NG)]
+        f = [flow_v[i, x] for i in range(NF)]
+        g = [field_v[k, x] for k in range(NG)]
         for i, value in collide(f, g, fluid, bcell, range(NP)).items():
             post_ref[i, x] = value
         return carry
 
-    lax.fori_loop(0, fluid_ref.shape[0], body, 0)
+    lax.fori_loop(0, sx, body, 0)
 
 
 def collide_call(flow, field, profile, strengths, wall, magnet):
     sx, sy, sz = profile.shape
-    full = pltpu.VMEM((NP, sx, sy, sz), jnp.float32)
     cells = pltpu.VMEM((sx, sy, sz), jnp.float32)
+    names = pltpu.VMEM((sx, sy, sz), jnp.int32)
     return pl.pallas_call(
         collide_kernel,
-        in_specs=[VMEM] * 6,
-        out_specs=[VMEM] * 3,
-        out_shape=[full, cells, cells],
+        in_specs=[ANY] * 6,
+        out_specs=[VMEM] * 5,
+        out_shape=[
+            pltpu.VMEM((NP, sx, sy, sz), jnp.float32),
+            cells,
+            cells,
+            cells,
+            names,
+        ],
+        scratch_shapes=[
+            pltpu.VMEM(flow.shape, jnp.float32),
+            pltpu.VMEM(field.shape, jnp.float32),
+            names,
+            pltpu.VMEM(strengths.shape, jnp.float32),
+            pltpu.SemaphoreType.DMA((5, sx)),
+            pltpu.SemaphoreType.DMA((1,)),
+        ],
         compiler_params=pltpu.CompilerParams(vmem_limit_bytes=COLLIDE_VMEM),
         cost_estimate=pl.CostEstimate(
             flops=300 * sx * sy * sz, bytes_accessed=12 * NP * sx * sy * sz, transcendentals=0
@@ -345,7 +385,7 @@
 
 def plane_step(
     x_index, post, post_row, adj, adj_row, mask, mask_row, fluid, bcell, profile, magnet,
-    near_ref, new_ref, out_ref, sums_ref, count,
+    near_ref, new_ref, out_ref, sums_ref, count, new_done, out_done,
 ):
     sy, sz = fluid.shape
     yi = lax.broadcasted_iota(jnp.int32, (sy, sz), 0)
@@ -418,6 +458,7 @@
         bval = bval + (a + b)
         if k == 3:
             gy = a - b
+    new_done()
     inv = 1.0 / rho
     ux, uy, uz = momx * inv, momy * inv, momz * inv
     current = gy - bval * uy
@@ -514,6 +555,8 @@
             value = bbar - currentbar
         out_ref[NF + k, x_index] = value
 
+    out_done()
+
     share = dcell * profile
     for m in range(count):
         hit = jnp.where(magnet == m, share, 0.0)
@@ -597,8 +640,9 @@
             out_v,
             sums_ref,
             count,
+            lambda: start_all(stores(x)[:2]),
+            lambda: start_all(stores(x)[2:]),
         )
-        start_all(stores(x))
         return carry
 
     lax.fori_loop(1, sx - 1, body, 0)
@@ -645,6 +689,10 @@
     keep_low, keep_high = load_halo(first_ref, second_ref, halo_v)
     stores = []
     for n, (x, away) in enumerate(((0, -1), (sx - 1, 1))):
+        these = plane_stores(
+            n, x, new_v, out_v, newf_ref, newg_ref, outf_ref, outg_ref, store_sem
+        )
+        stores += these
         face_ref, corner_ref = (
             (fromleft_ref, cornerleft_ref) if away == -1 else (fromright_ref, cornerright_ref)
         )
@@ -686,12 +734,9 @@
             out_v,
             sums_v,
             count,
+            lambda these=these: start_all(these[:2]),
+            lambda these=these: start_all(these[2:]),
         )
-        these = plane_stores(
-            n, x, new_v, out_v, newf_ref, newg_ref, outf_ref, outg_ref, store_sem
-        )
-        start_all(these)
-        stores += these
     rows = jnp.concatenate(
         [jnp.sum(sums_v[m], axis=0, keepdims=True) for m in range(count)], axis=0
     )
@@ -757,7 +802,7 @@
     first = lax.ppermute(mine1, "gy", inside)
     fromleft = lax.ppermute(right, "gx", ring(around, 1))
     fromright = lax.ppermute(left, "gx", ring(around, -1))
-    post, fluid, bcell = collide_call(flow, field, profile, table, wall, magnet)
+    post, fluid, bcell, profile, magnet = collide_call(flow, field, profile, table, wall, magnet)
     corner_r, corner_l = corner_call(first, second, bcell)
     cornerleft = lax.ppermute(corner_r, "gx", ring(around, 1))
     cornerright = lax.ppermute(corner_l, "gx", ring(around, -1))

time: 34.1 us -> 33.6 us (0.985)
  Pallas kernels: 10 us -> 11.3 us
  blocking collectives: 10.1 us -> 9.02 us
  waiting for transfers between devices: 0.49 us -> 0.02 us
    ppermute x1, starting transfers between devices: 1.89 us -> 0.06 us  [on_device(): cornerleft = lax.ppermute(corner_r, 'gx', ring(around, 1))]
    ppermute x1, starting transfers between devices: 2.09 us -> 3.81 us  [on_device(): cornerright = lax.ppermute(corner_l, 'gx', ring(around, -1))]
    pallas_call x2, Pallas kernels: 4.41 us -> 5.65 us  [the longest x1 3.5 us: collide_call(): pl.pallas_call(collide_kernel, in_specs=[ANY] * 6, out_specs=[VMEM] * 5,...]
    all_to_all x1, blocking collectives: 10.1 us -> 9.02 us  [on_device(): lax.all_to_all(share, ('gx', 'gy'), 0, 0, tiled=True)]
    ppermute x1, waiting for transfers between devices: 0.48 us -> 0.01 us  [on_device(): cornerleft = lax.ppermute(corner_r, 'gx', ring(around, 1))]
  transfers between devices with their start and end apart: 6 -> 6, of which waited for: 1 -> 0; matrix products, arithmetic and copies ran while one was open for 0% -> 0% of each run, Pallas kernels for 15% -> 22%
where the time goes in v7:
time: 33.6 us; the launch traced here: 33.4 us
  starting transfers between devices  11.8 us (35%)
  Pallas kernels  11.3 us (34%)
  blocking collectives  9.02 us (27%)
  between operations  0.75 us (2%)
  other arithmetic  0.56 us (2%)
    all_to_all x1, blocking collectives, on_device(): lax.all_to_all(share, ('gx', 'gy'), 0, 0, tiled=True)  9.02 us
    ppermute x1, starting transfers between devices, on_device(): cornerright = lax.ppermute(corner_l, 'gx', ring(around, -1))  3.81 us
    pallas_call x1, Pallas kernels, inner_call(): pl.pallas_call(inner_kernel, in_specs=[VMEM] * 9, out_specs=[ANY, ANY, AN...  3.78 us
    ppermute x1, starting transfers between devices, on_device(): second = lax.ppermute(mine2, 'gy', between)  3.56 us
    pallas_call x1, Pallas kernels, collide_call(): pl.pallas_call(collide_kernel, in_specs=[ANY] * 6, out_specs=[VMEM] * 5,...  3.5 us
    ppermute x1, starting transfers between devices, on_device(): fromright = lax.ppermute(left, 'gx', ring(around, -1))  2.25 us
    pallas_call x1, Pallas kernels, rim_call(): pl.pallas_call(rim_kernel, in_specs=[ANY] * 8, out_specs=[VMEM] * 4, out_...  2.14 us
    pallas_call x1, Pallas kernels, outer_call(): pl.pallas_call(functools.partial(outer_kernel, scale), in_specs=[VMEM] *...  1.85 us
  transfers between devices with their start and end apart: 6, of which 0 were waited for; matrix products, arithmetic and copies ran while one was open for 0% of the time, Pallas kernels for 22%

profile of v7, /device:TPU:0, one launch (start us, length us, event | category | flops | bytes accessed | tf_op | source)
XLA Modules:
  0.0 33.4 jit_solution(14035287655068640844)
XLA Ops:
  0.6 2.1 %rims.1 = (f32[13,8,512]{2,1,0:T(8,128)S(1)}, f32[13,8,512]{2,1,0:T(8,128)S(1)}, f32[13,8,512]{2,1,0:T(8,128)S(1)}, f32[13,8,512]{2,1,0:T(8,128)S(1)}) custom-call(f32[19,8,8,512]{3,2,1,0:T(8,128)} %flow_ref.3, f32[7,8,8,512]{3,2,1,0:T(8,128)} %field_ref.3, f32[19,8,8,512]{3,2,1,0:T(8,128)} %adjf_ref.5, f32[7,8,8,512]{3,2,1,0:T(8,128)} %adjg_ref.5, ...), custom_call_target="tpu_custom_call" | custom-call | tf_op jit(solution)/shard_map/rims/pallas_call | solution.py:255
  2.8 0.0 copy-start
  2.8 0.0 copy-start.1
  2.8 0.5 %collective-permute-start = (f32[13,8,512]{2,1,0:T(8,128)S(1)}, f32[13,8,512]{2,1,0:T(8,128)S(1)}, u32[]{:S(2)}, u32[]{:S(2)}) collective-permute-start(f32[13,8,512]{2,1,0:T(8,128)S(1)} %get-tuple-element.29), channel_id=1, source_target_pairs={{0,1},{1,0},{2,3},{3,2},{4,5},{5,4},{6,7},{7,6},{8,9},{9,8},{10,11... | collective-permute-start | bytes 638984 | tf_op jit(solution)/shard_map/ppermute | solution.py:802
  3.3 3.6 %collective-permute-start.1 = (f32[13,8,512]{2,1,0:T(8,128)S(1)}, f32[13,8,512]{2,1,0:T(8,128)S(1)}, u32[]{:S(2)}, u32[]{:S(2)}) collective-permute-start(f32[13,8,512]{2,1,0:T(8,128)S(1)} %get-tuple-element.30), channel_id=1, source_target_pairs={{0,7},{1,2},{2,1},{3,4},{4,3},{5,6},{6,5},{7,0},{8,15},{9,10},{10,... | collective-permute-start | bytes 638984 | tf_op jit(solution)/shard_map/ppermute | solution.py:801
  6.9 1.6 %collective-permute-start.2 = (f32[13,8,512]{2,1,0:T(8,128)S(1)}, f32[13,8,512]{2,1,0:T(8,128)S(1)}, u32[]{:S(2)}, u32[]{:S(2)}) collective-permute-start(f32[13,8,512]{2,1,0:T(8,128)S(1)} %get-tuple-element.31), channel_id=1, source_target_pairs={{0,8},{8,16},{16,24},{24,0},{1,9},{9,17},{17,25},{25,1},{2,10},{10... | collective-permute-start | bytes 638984 | tf_op jit(solution)/shard_map/ppermute | solution.py:803
  8.5 2.2 %collective-permute-start.3 = (f32[13,8,512]{2,1,0:T(8,128)S(1)}, f32[13,8,512]{2,1,0:T(8,128)S(1)}, u32[]{:S(2)}, u32[]{:S(2)}) collective-permute-start(f32[13,8,512]{2,1,0:T(8,128)S(1)} %get-tuple-element.32), channel_id=1, source_target_pairs={{0,24},{8,0},{16,8},{24,16},{1,25},{9,1},{17,9},{25,17},{2,26},{10... | collective-permute-start | bytes 638984 | tf_op jit(solution)/shard_map/ppermute | solution.py:804
  10.7 3.5 %collide.1 = (f32[26,8,8,512]{3,2,1,0:T(8,128)S(1)}, f32[8,8,512]{2,1,0:T(8,128)S(1)}, f32[8,8,512]{2,1,0:T(8,128)S(1)}, f32[8,8,512]{2,1,0:T(8,128)S(1)}, s32[8,8,512]{2,1,0:T(8,128)S(1)}) custom-call(f32[19,8,8,512]{3,2,1,0:T(8,128)} %flow_ref.3, f32[7,8,8,512]{3,2,1,0:T(8,128)} %field_ref.3, f32[8,8,512]{2,1,0:T(8,128)} %profile_ref.3, f32[1,32]{1,0:T(1,128)} %bitcast.6, ...), custom_call_target="tpu_custom_call" | custom-call | flops 9830400 | bytes 10223616 | tf_op jit(solution)/shard_map/collide/pallas_call | solution.py:321
  14.2 0.0 collective-permute-done.first_ref
  14.2 0.0 collective-permute-done.1.second_ref
  14.3 0.1 collective-permute-start.4
  14.3 3.8 %collective-permute-start.5 = (f32[8,512]{1,0:T(8,128)S(1)}, f32[8,512]{1,0:T(8,128)S(1)}, u32[]{:S(2)}, u32[]{:S(2)}) collective-permute-start(f32[8,512]{1,0:T(8,128)S(1)} %get-tuple-element.34), channel_id=1, source_target_pairs={{0,24},{8,0},{16,8},{24,16},{1,25},{9,1},{17,9},{25,17},{2,26},{10... | collective-permute-start | bytes 49160 | tf_op jit(solution)/shard_map/ppermute | solution.py:808
  18.1 0.0 copy-done
  18.1 0.0 copy-done.1
  18.1 3.8 %inner.1 = (f32[19,8,8,512]{3,2,1,0:T(8,128)}, f32[7,8,8,512]{3,2,1,0:T(8,128)}, f32[19,8,8,512]{3,2,1,0:T(8,128)}, f32[7,8,8,512]{3,2,1,0:T(8,128)}, f32[32,8,128]{2,1,0:T(8,128)S(1)}) custom-call(f32[26,8,8,512]{3,2,1,0:T(8,128)S(1)} %get-tuple-element.26.post_ref, f32[19,8,8,512]{3,2,1,0:T(8,128)S(1)} %copy-done, f32[7,8,8,512]{3,2,1,0:T(8,128)S(1)} %copy-done.1, ...), custom_call_target="tpu_custom_call" | custom-call | flops 22937600 | bytes 13631488 | tf_op jit(solution)/shard_map/inner/pallas_call | solution.py:658
  21.9 0.0 collective-permute-done.2.fromleft_ref
  21.9 0.0 collective-permute-done.3.fromright_ref
  22.0 0.0 collective-permute-done.4.cornerleft_ref
  22.0 0.0 collective-permute-done.5.cornerright_ref
  22.0 1.9 %outer.1 = (f32[19,8,8,512]{3,2,1,0:T(8,128)}, f32[7,8,8,512]{3,2,1,0:T(8,128)}, f32[19,8,8,512]{3,2,1,0:T(8,128)}, f32[7,8,8,512]{3,2,1,0:T(8,128)}, f32[32,32]{1,0:T(8,128)S(1)}) custom-call(f32[26,8,8,512]{3,2,1,0:T(8,128)S(1)} %get-tuple-element.26.post_ref, ...), custom_call_target="tpu_custom_call", output_to_operand_aliasing={{0}: (14, {}), {1}: (15, {}), {2}: (16, {}), {3}: (17, {})} | custom-call | tf_op jit(solution)/shard_map/outer/pallas_call | solution.py:761
  23.8 9.0 %all_to_all.9 = f32[32,1,32]{2,1,0:T(1,128)S(1)} all-to-all(f32[32,1,32]{2,1,0:T(1,128)S(1)} %bitcast.4), channel_id=1, replica_groups=mesh['gx'=4,'gy'=8] {'gx','gy'}, dimensions={0} | all-to-all | bytes 8192 | tf_op jit(solution)/shard_map/all_to_all | solution.py:817
  32.8 0.6 %reduce_sum.9 = f32[32]{0:T(128)} reduce(f32[32,1,32]{2,1,0:T(1,128)S(1)} %all_to_all.9, f32[]{:T(128)} %constant.0.clone.1), dimensions={0,1}, to_apply=%region_0.0 | reduce | flops 992 | bytes 4228 | tf_op jit(solution)/shard_map/reduce_sum | solution.py:817
  (1 shorter events, 0.0 us)
Async XLA Ops:
  2.8 15.4 %copy-start = (f32[19,8,8,512]{3,2,1,0:T(8,128)S(1)}, f32[19,8,8,512]{3,2,1,0:T(8,128)}, u32[]{:S(2)}) copy-start(f32[19,8,8,512]{3,2,1,0:T(8,128)} %adjf_ref.5) | copy-start | bytes 7471108
  2.8 15.3 %copy-start.1 = (f32[7,8,8,512]{3,2,1,0:T(8,128)S(1)}, f32[7,8,8,512]{3,2,1,0:T(8,128)}, u32[]{:S(2)}) copy-start(f32[7,8,8,512]{3,2,1,0:T(8,128)} %adjg_ref.5) | copy-start | bytes 2752516
  2.8 11.4 %collective-permute-start = (f32[13,8,512]{2,1,0:T(8,128)S(1)}, f32[13,8,512]{2,1,0:T(8,128)S(1)}, u32[]{:S(2)}, u32[]{:S(2)}) collective-permute-start(f32[13,8,512]{2,1,0:T(8,128)S(1)} %get-tuple-element.29), channel_id=1, source_target_pairs={{0,1},{1,0},{2,3},{3,2},{4,5},{5,4},{6,7},{7,6},{8,9},{9,8},{10,11... | collective-permute-start | bytes 638984 | tf_op jit(solution)/shard_map/ppermute | solution.py:802
  3.3 10.9 %collective-permute-start.1 = (f32[13,8,512]{2,1,0:T(8,128)S(1)}, f32[13,8,512]{2,1,0:T(8,128)S(1)}, u32[]{:S(2)}, u32[]{:S(2)}) collective-permute-start(f32[13,8,512]{2,1,0:T(8,128)S(1)} %get-tuple-element.30), channel_id=1, source_target_pairs={{0,7},{1,2},{2,1},{3,4},{4,3},{5,6},{6,5},{7,0},{8,15},{9,10},{10,... | collective-permute-start | bytes 638984 | tf_op jit(solution)/shard_map/ppermute | solution.py:801
  6.9 15.1 %collective-permute-start.2 = (f32[13,8,512]{2,1,0:T(8,128)S(1)}, f32[13,8,512]{2,1,0:T(8,128)S(1)}, u32[]{:S(2)}, u32[]{:S(2)}) collective-permute-start(f32[13,8,512]{2,1,0:T(8,128)S(1)} %get-tuple-element.31), channel_id=1, source_target_pairs={{0,8},{8,16},{16,24},{24,0},{1,9},{9,17},{17,25},{25,1},{2,10},{10... | collective-permute-start | bytes 638984 | tf_op jit(solution)/shard_map/ppermute | solution.py:803
  8.5 13.5 %collective-permute-start.3 = (f32[13,8,512]{2,1,0:T(8,128)S(1)}, f32[13,8,512]{2,1,0:T(8,128)S(1)}, u32[]{:S(2)}, u32[]{:S(2)}) collective-permute-start(f32[13,8,512]{2,1,0:T(8,128)S(1)} %get-tuple-element.32), channel_id=1, source_target_pairs={{0,24},{8,0},{16,8},{24,16},{1,25},{9,1},{17,9},{25,17},{2,26},{10... | collective-permute-start | bytes 638984 | tf_op jit(solution)/shard_map/ppermute | solution.py:804
  14.3 7.7 %collective-permute-start.4 = (f32[8,512]{1,0:T(8,128)S(1)}, f32[8,512]{1,0:T(8,128)S(1)}, u32[]{:S(2)}, u32[]{:S(2)}) collective-permute-start(f32[8,512]{1,0:T(8,128)S(1)} %get-tuple-element.33), channel_id=1, source_target_pairs={{0,8},{8,16},{16,24},{24,0},{1,9},{9,17},{17,25},{25,1},{2,10},{10... | collective-permute-start | bytes 49160 | tf_op jit(solution)/shard_map/ppermute | solution.py:807
  14.3 7.6 %collective-permute-start.5 = (f32[8,512]{1,0:T(8,128)S(1)}, f32[8,512]{1,0:T(8,128)S(1)}, u32[]{:S(2)}, u32[]{:S(2)}) collective-permute-start(f32[8,512]{1,0:T(8,128)S(1)} %get-tuple-element.34), channel_id=1, source_target_pairs={{0,24},{8,0},{16,8},{24,16},{1,25},{9,1},{17,9},{25,17},{2,26},{10... | collective-permute-start | bytes 49160 | tf_op jit(solution)/shard_map/ppermute | solution.py:808

commit v8 on v6

--- a/solution.py
+++ b/solution.py
@@ -146,7 +146,8 @@
 def rim_kernel(
     flow_ref, field_ref, adjf_ref, adjg_ref, profile_ref, strengths_ref, wall_ref, magnet_ref,
     first_ref, second_ref, right_ref, left_ref,
-    rows_v, faces_v, profile_v, wall_v, magnet_v, message_v, cell_sem, rows_sem, faces_sem, adj_sem,
+    rows_v, faces_v, profile_v, wall_v, magnet_v, strengths_v, message_v, cell_sem, rows_sem,
+    faces_sem, adj_sem,
 ):
     sx, sy = profile_v.shape[:2]
     odd = lax.rem(lax.axis_index("gy"), 2)
@@ -169,7 +170,12 @@
     cells = [
         pltpu.make_async_copy(a, b, cell_sem.at[n])
         for n, (a, b) in enumerate(
-            ((wall_ref, wall_v), (magnet_ref, magnet_v), (profile_ref, profile_v))
+            (
+                (wall_ref, wall_v),
+                (magnet_ref, magnet_v),
+                (strengths_ref, strengths_v),
+                (profile_ref, profile_v),
+            )
         )
     ]
     faces = []
@@ -198,8 +204,8 @@
     start_all(rows[2:])
     start_all(faces)
     start_all(adjs)
-    table = lane_table(strengths_ref)
     wait_all(cells)
+    table = lane_table(strengths_v)
     for n, (y, wanted) in enumerate(zip(ends, (UP, DOWN))):
         wait_all(rows[2 * n : 2 * n + 2])
         fluid = 1.0 - wall_v[:, y, :].astype(jnp.float32)
@@ -248,7 +254,7 @@
     dma = pltpu.SemaphoreType.DMA
     return pl.pallas_call(
         rim_kernel,
-        in_specs=[ANY, ANY, ANY, ANY, ANY, VMEM, ANY, ANY],
+        in_specs=[ANY] * 8,
         out_specs=[VMEM] * 4,
         out_shape=[rows, rows, faces, faces],
         scratch_shapes=[
@@ -257,8 +263,9 @@
             cells,
             names,
             names,
+            pltpu.VMEM(strengths.shape, jnp.float32),
             pltpu.VMEM((2, SLOTS, sx, sz), jnp.float32),
-            dma((3,)),
+            dma((4,)),
             dma((2, 2)),
             dma((2, 2)),
             dma((4, 6)),
@@ -632,7 +639,8 @@
 
 
 def outer_kernel(
-    scale, post_ref, adjf_ref, adjg_ref, fluid_ref, bcell_ref, first_ref, second_ref, fromleft_ref, fromright_ref,
+    scale, second_ref, fromleft_ref, fromright_ref, first_ref, post_ref, adjf_ref, adjg_ref,
+    fluid_ref, bcell_ref,
     cornerleft_ref, cornerright_ref, profile_ref, magnet_ref,
     partial_ref, newf_in, newg_in, outf_in, outg_in,
     newf_ref, newg_ref, outf_ref, outg_ref, share_ref,
@@ -736,8 +744,8 @@
         compiler_params=pltpu.CompilerParams(vmem_limit_bytes=OUTER_VMEM),
         name="outer",
     )(
-        post, adjf, adjg, fluid, bcell, first, second, fromleft, fromright, cornerleft, cornerright,
-        profile, magnet, partial, newf, newg, outf, outg,
+        second, fromleft, fromright, first, post, adjf, adjg, fluid, bcell, cornerleft,
+        cornerright, profile, magnet, partial, newf, newg, outf, outg,
     )
 
 

time: 34.1 us -> 33.4 us (0.979)
  Pallas kernels: 10 us -> 9.12 us
  blocking collectives: 10.1 us -> 9.61 us
  starting transfers between devices: 11.9 us -> 12.3 us
    ppermute x1, starting transfers between devices: 1.89 us -> 3.01 us  [on_device(): cornerleft = lax.ppermute(corner_r, 'gx', ring(around, 1))]
    pallas_call x1, Pallas kernels: 3.22 us -> 2.28 us  [rim_call(): pl.pallas_call(rim_kernel, in_specs=[ANY] * 8, out_specs=[VMEM] * 4, out_...]
    ppermute x1, starting transfers between devices: 0.52 us -> 0.01 us  [on_device(): first = lax.ppermute(mine1, 'gy', inside)]
    all_to_all x1, blocking collectives: 10.1 us -> 9.61 us  [on_device(): lax.all_to_all(share, ('gx', 'gy'), 0, 0, tiled=True)]
where the time goes in v8:
time: 33.4 us; the launch traced here: 33.2 us
  starting transfers between devices  12.3 us (37%)
  blocking collectives  9.61 us (29%)
  Pallas kernels  9.12 us (27%)
  between operations  0.79 us (2%)
  waiting for transfers between devices  0.76 us (2%)
  other arithmetic  0.56 us (2%)
    all_to_all x1, blocking collectives, on_device(): lax.all_to_all(share, ('gx', 'gy'), 0, 0, tiled=True)  9.61 us
    pallas_call x1, Pallas kernels, inner_call(): pl.pallas_call(inner_kernel, in_specs=[VMEM] * 9, out_specs=[ANY, ANY, AN...  3.78 us
    ppermute x1, starting transfers between devices, on_device(): second = lax.ppermute(mine2, 'gy', between)  3.4 us
    ppermute x1, starting transfers between devices, on_device(): cornerleft = lax.ppermute(corner_r, 'gx', ring(around, 1))  3.01 us
    pallas_call x1, Pallas kernels, rim_call(): pl.pallas_call(rim_kernel, in_specs=[ANY] * 8, out_specs=[VMEM] * 4, out_...  2.28 us
    ppermute x1, starting transfers between devices, on_device(): fromright = lax.ppermute(left, 'gx', ring(around, -1))  2.25 us
    ppermute x1, starting transfers between devices, on_device(): cornerright = lax.ppermute(corner_l, 'gx', ring(around, -1))  2.09 us
    pallas_call x1, Pallas kernels, outer_call(): pl.pallas_call(functools.partial(outer_kernel, scale), in_specs=[VMEM] *...  1.85 us
  transfers between devices with their start and end apart: 6, of which 1 were waited for; matrix products, arithmetic and copies ran while one was open for 0% of the time, Pallas kernels for 15%

profile of v8, /device:TPU:0, one launch (start us, length us, event | category | flops | bytes accessed | tf_op | source)
XLA Modules:
  0.0 33.2 jit_solution(5175320373467072907)
XLA Ops:
  0.6 0.0 copy-start.1
  0.6 0.0 copy-start.3
  0.7 0.0 copy-start.4
  0.7 2.3 %rims.1 = (f32[13,8,512]{2,1,0:T(8,128)S(1)}, f32[13,8,512]{2,1,0:T(8,128)S(1)}, f32[13,8,512]{2,1,0:T(8,128)S(1)}, f32[13,8,512]{2,1,0:T(8,128)S(1)}) custom-call(f32[19,8,8,512]{3,2,1,0:T(8,128)} %flow_ref.3, f32[7,8,8,512]{3,2,1,0:T(8,128)} %field_ref.3, f32[19,8,8,512]{3,2,1,0:T(8,128)} %adjf_ref.5, f32[7,8,8,512]{3,2,1,0:T(8,128)} %adjg_ref.5, ...), custom_call_target="tpu_custom_call" | custom-call | tf_op jit(solution)/shard_map/rims/pallas_call | solution.py:255
  3.0 0.0 copy-start
  3.0 0.0 copy-start.2
  3.0 3.4 %collective-permute-start = (f32[13,8,512]{2,1,0:T(8,128)S(1)}, f32[13,8,512]{2,1,0:T(8,128)S(1)}, u32[]{:S(2)}, u32[]{:S(2)}) collective-permute-start(f32[13,8,512]{2,1,0:T(8,128)S(1)} %get-tuple-element.24), channel_id=1, source_target_pairs={{0,7},{1,2},{2,1},{3,4},{4,3},{5,6},{6,5},{7,0},{8,15},{9,10},{10,... | collective-permute-start | bytes 638984 | tf_op jit(solution)/shard_map/ppermute | solution.py:764
  6.4 0.0 collective-permute-start.3
  6.4 1.6 %collective-permute-start.1 = (f32[13,8,512]{2,1,0:T(8,128)S(1)}, f32[13,8,512]{2,1,0:T(8,128)S(1)}, u32[]{:S(2)}, u32[]{:S(2)}) collective-permute-start(f32[13,8,512]{2,1,0:T(8,128)S(1)} %get-tuple-element.25), channel_id=1, source_target_pairs={{0,8},{8,16},{16,24},{24,0},{1,9},{9,17},{17,25},{25,1},{2,10},{10... | collective-permute-start | bytes 638984 | tf_op jit(solution)/shard_map/ppermute | solution.py:766
  8.0 2.2 %collective-permute-start.2 = (f32[13,8,512]{2,1,0:T(8,128)S(1)}, f32[13,8,512]{2,1,0:T(8,128)S(1)}, u32[]{:S(2)}, u32[]{:S(2)}) collective-permute-start(f32[13,8,512]{2,1,0:T(8,128)S(1)} %get-tuple-element.26), channel_id=1, source_target_pairs={{0,24},{8,0},{16,8},{24,16},{1,25},{9,1},{17,9},{25,17},{2,26},{10... | collective-permute-start | bytes 638984 | tf_op jit(solution)/shard_map/ppermute | solution.py:767
  10.3 1.2 %collide.1 = (f32[26,8,8,512]{3,2,1,0:T(8,128)S(1)}, f32[8,8,512]{2,1,0:T(8,128)S(1)}, f32[8,8,512]{2,1,0:T(8,128)S(1)}) custom-call(f32[19,8,8,512]{3,2,1,0:T(8,128)S(1)} %copy-done.1, f32[7,8,8,512]{3,2,1,0:T(8,128)S(1)} %copy-done.3, f32[8,8,512]{2,1,0:T(8,128)S(1)} %copy-done.4, f32[1,32]{1,0:T(1,128)S(1)} %bitcast.6, s32[8,8,512]{2,1,0:T(8,128)S(1)} %copy-done.6, ...), custom_call_target="tpu_custom_call" | custom-call | flops 9830400 | bytes 10223616 | tf_op jit(solution)/shard_map/collide/pallas_call | solution.py:302
  11.5 0.0 collective-permute-done.second_ref
  11.5 0.0 collective-permute-done.3.first_ref
  11.5 3.0 %collective-permute-start.4 = (f32[8,512]{1,0:T(8,128)S(1)}, f32[8,512]{1,0:T(8,128)S(1)}, u32[]{:S(2)}, u32[]{:S(2)}) collective-permute-start(f32[8,512]{1,0:T(8,128)S(1)} %get-tuple-element.31), channel_id=1, source_target_pairs={{0,8},{8,16},{16,24},{24,0},{1,9},{9,17},{17,25},{25,1},{2,10},{10... | collective-permute-start | bytes 49160 | tf_op jit(solution)/shard_map/ppermute | solution.py:770
  14.5 2.1 %collective-permute-start.5 = (f32[8,512]{1,0:T(8,128)S(1)}, f32[8,512]{1,0:T(8,128)S(1)}, u32[]{:S(2)}, u32[]{:S(2)}) collective-permute-start(f32[8,512]{1,0:T(8,128)S(1)} %get-tuple-element.32), channel_id=1, source_target_pairs={{0,24},{8,0},{16,8},{24,16},{1,25},{9,1},{17,9},{25,17},{2,26},{10... | collective-permute-start | bytes 49160 | tf_op jit(solution)/shard_map/ppermute | solution.py:771
  16.6 0.0 copy-done
  16.6 3.8 %inner.1 = (f32[19,8,8,512]{3,2,1,0:T(8,128)}, f32[7,8,8,512]{3,2,1,0:T(8,128)}, f32[19,8,8,512]{3,2,1,0:T(8,128)}, f32[7,8,8,512]{3,2,1,0:T(8,128)}, f32[32,8,128]{2,1,0:T(8,128)S(1)}) custom-call(f32[26,8,8,512]{3,2,1,0:T(8,128)S(1)} %get-tuple-element.28.post_ref, f32[19,8,8,512]{3,2,1,0:T(8,128)S(1)} %copy-done, f32[7,8,8,512]{3,2,1,0:T(8,128)S(1)} %copy-done.2, ...), custom_call_target="tpu_custom_call" | custom-call | flops 22937600 | bytes 13631488 | tf_op jit(solution)/shard_map/inner/pallas_call | solution.py:621
  20.4 0.0 collective-permute-done.1.fromleft_ref
  20.4 0.0 collective-permute-done.2.fromright_ref
  20.4 0.7 %collective-permute-done.4.cornerleft_ref = f32[8,512]{1,0:T(8,128)S(1)} collective-permute-done((f32[8,512]{1,0:T(8,128)S(1)}, f32[8,512]{1,0:T(8,128)S(1)}, u32[]{:S(2)}, u32[]{:S(2)}) %collective-permute-start.4) | collective-permute-done | bytes 16416 | tf_op jit(solution)/shard_map/ppermute | solution.py:770
  21.2 0.0 collective-permute-done.5.cornerright_ref
  21.2 1.9 %outer.1 = (f32[19,8,8,512]{3,2,1,0:T(8,128)}, f32[7,8,8,512]{3,2,1,0:T(8,128)}, f32[19,8,8,512]{3,2,1,0:T(8,128)}, f32[7,8,8,512]{3,2,1,0:T(8,128)}, f32[32,32]{1,0:T(8,128)S(1)}) custom-call(f32[13,8,512]{2,1,0:T(8,128)S(1)} %collective-permute-done.second_ref, ...), custom_call_target="tpu_custom_call", output_to_operand_aliasing={{0}: (14, {}), {1}: (15, {}), {2}: (16, {}), {3}: (17, {})} | custom-call | tf_op jit(solution)/shard_map/outer/pallas_call | solution.py:724
  23.0 9.6 %all_to_all.9 = f32[32,1,32]{2,1,0:T(1,128)S(1)} all-to-all(f32[32,1,32]{2,1,0:T(1,128)S(1)} %bitcast.4), channel_id=1, replica_groups=mesh['gx'=4,'gy'=8] {'gx','gy'}, dimensions={0} | all-to-all | bytes 8192 | tf_op jit(solution)/shard_map/all_to_all | solution.py:780
  32.6 0.6 %reduce_sum.9 = f32[32]{0:T(128)} reduce(f32[32,1,32]{2,1,0:T(1,128)S(1)} %all_to_all.9, f32[]{:T(128)} %constant.0.clone.1), dimensions={0,1}, to_apply=%region_0.0 | reduce | flops 992 | bytes 4228 | tf_op jit(solution)/shard_map/reduce_sum | solution.py:780
  (11 shorter events, 0.0 us)
Async XLA Ops:
  0.6 9.6 %copy-start.1 = (f32[19,8,8,512]{3,2,1,0:T(8,128)S(1)}, f32[19,8,8,512]{3,2,1,0:T(8,128)}, u32[]{:S(2)}) copy-start(f32[19,8,8,512]{3,2,1,0:T(8,128)} %flow_ref.3) | copy-start | bytes 7471108
  0.6 9.6 %copy-start.3 = (f32[7,8,8,512]{3,2,1,0:T(8,128)S(1)}, f32[7,8,8,512]{3,2,1,0:T(8,128)}, u32[]{:S(2)}) copy-start(f32[7,8,8,512]{3,2,1,0:T(8,128)} %field_ref.3) | copy-start | bytes 2752516
  0.7 9.6 %copy-start.4 = (f32[8,8,512]{2,1,0:T(8,128)S(1)}, f32[8,8,512]{2,1,0:T(8,128)}, u32[]{:S(2)}) copy-start(f32[8,8,512]{2,1,0:T(8,128)} %profile_ref.7) | copy-start | bytes 393220
  0.7 9.6 %copy-start.5 = (s32[8,8,512]{2,1,0:T(8,128)S(1)}, s32[8,8,512]{2,1,0:T(8,128)}, u32[]{:S(2)}) copy-start(s32[8,8,512]{2,1,0:T(8,128)} %magnet_ref.7) | copy-start | bytes 393220
  0.7 9.6 %copy-start.6 = (s32[8,8,512]{2,1,0:T(8,128)S(1)}, s32[8,8,512]{2,1,0:T(8,128)}, u32[]{:S(2)}) copy-start(s32[8,8,512]{2,1,0:T(8,128)} %wall_ref.3) | copy-start | bytes 393220
  0.7 9.6 %copy-start.7 = (f32[32]{0:T(128)S(1)}, f32[32]{0:T(128)}, u32[]{:S(2)}) copy-start(f32[32]{0:T(128)} %param.13) | copy-start | bytes 388
  3.0 13.6 %copy-start = (f32[19,8,8,512]{3,2,1,0:T(8,128)S(1)}, f32[19,8,8,512]{3,2,1,0:T(8,128)}, u32[]{:S(2)}) copy-start(f32[19,8,8,512]{3,2,1,0:T(8,128)} %adjf_ref.5) | copy-start | bytes 7471108
  3.0 13.6 %copy-start.2 = (f32[7,8,8,512]{3,2,1,0:T(8,128)S(1)}, f32[7,8,8,512]{3,2,1,0:T(8,128)}, u32[]{:S(2)}) copy-start(f32[7,8,8,512]{3,2,1,0:T(8,128)} %adjg_ref.5) | copy-start | bytes 2752516
  3.0 8.5 %collective-permute-start = (f32[13,8,512]{2,1,0:T(8,128)S(1)}, f32[13,8,512]{2,1,0:T(8,128)S(1)}, u32[]{:S(2)}, u32[]{:S(2)}) collective-permute-start(f32[13,8,512]{2,1,0:T(8,128)S(1)} %get-tuple-element.24), channel_id=1, source_target_pairs={{0,7},{1,2},{2,1},{3,4},{4,3},{5,6},{6,5},{7,0},{8,15},{9,10},{10,... | collective-permute-start | bytes 638984 | tf_op jit(solution)/shard_map/ppermute | solution.py:764
  6.4 5.1 %collective-permute-start.3 = (f32[13,8,512]{2,1,0:T(8,128)S(1)}, f32[13,8,512]{2,1,0:T(8,128)S(1)}, u32[]{:S(2)}, u32[]{:S(2)}) collective-permute-start(f32[13,8,512]{2,1,0:T(8,128)S(1)} %get-tuple-element.27), channel_id=1, source_target_pairs={{0,1},{1,0},{2,3},{3,2},{4,5},{5,4},{6,7},{7,6},{8,9},{9,8},{10,11... | collective-permute-start | bytes 638984 | tf_op jit(solution)/shard_map/ppermute | solution.py:765
  6.4 14.0 %collective-permute-start.1 = (f32[13,8,512]{2,1,0:T(8,128)S(1)}, f32[13,8,512]{2,1,0:T(8,128)S(1)}, u32[]{:S(2)}, u32[]{:S(2)}) collective-permute-start(f32[13,8,512]{2,1,0:T(8,128)S(1)} %get-tuple-element.25), channel_id=1, source_target_pairs={{0,8},{8,16},{16,24},{24,0},{1,9},{9,17},{17,25},{25,1},{2,10},{10... | collective-permute-start | bytes 638984 | tf_op jit(solution)/shard_map/ppermute | solution.py:766
  8.0 12.4 %collective-permute-start.2 = (f32[13,8,512]{2,1,0:T(8,128)S(1)}, f32[13,8,512]{2,1,0:T(8,128)S(1)}, u32[]{:S(2)}, u32[]{:S(2)}) collective-permute-start(f32[13,8,512]{2,1,0:T(8,128)S(1)} %get-tuple-element.26), channel_id=1, source_target_pairs={{0,24},{8,0},{16,8},{24,16},{1,25},{9,1},{17,9},{25,17},{2,26},{10... | collective-permute-start | bytes 638984 | tf_op jit(solution)/shard_map/ppermute | solution.py:767
  11.5 9.7 %collective-permute-start.4 = (f32[8,512]{1,0:T(8,128)S(1)}, f32[8,512]{1,0:T(8,128)S(1)}, u32[]{:S(2)}, u32[]{:S(2)}) collective-permute-start(f32[8,512]{1,0:T(8,128)S(1)} %get-tuple-element.31), channel_id=1, source_target_pairs={{0,8},{8,16},{16,24},{24,0},{1,9},{9,17},{17,25},{25,1},{2,10},{10... | collective-permute-start | bytes 49160 | tf_op jit(solution)/shard_map/ppermute | solution.py:770
  14.5 6.7 %collective-permute-start.5 = (f32[8,512]{1,0:T(8,128)S(1)}, f32[8,512]{1,0:T(8,128)S(1)}, u32[]{:S(2)}, u32[]{:S(2)}) collective-permute-start(f32[8,512]{1,0:T(8,128)S(1)} %get-tuple-element.32), channel_id=1, source_target_pairs={{0,24},{8,0},{16,8},{24,16},{1,25},{9,1},{17,9},{25,17},{2,26},{10... | collective-permute-start | bytes 49160 | tf_op jit(solution)/shard_map/ppermute | solution.py:771

commit v9 on v8

--- a/solution.py
+++ b/solution.py
@@ -321,30 +321,26 @@
     return posts.index(post), 6 + adjs.index(adj), MASK
 
 
-def corner_kernel(first_ref, second_ref, after_ref, right_ref, left_ref):
+def corner_kernel(table, x, first_ref, second_ref, after_ref, out_ref):
     del after_ref
     odd = lax.rem(lax.axis_index("gy"), 2) == 1
-    sx = first_ref.shape[1]
-
-    def row(side, slot, x):
+
+    def row(side, slot):
         a, b = first_ref[slot, x : x + 1, :], second_ref[slot, x : x + 1, :]
         return jnp.where(odd, a, b) if side == 0 else jnp.where(odd, b, a)
 
-    for out, table, x in ((right_ref, CORNER_RIGHT, sx - 1), (left_ref, CORNER_LEFT, 0)):
-        out[...] = jnp.zeros_like(out)
-        for side, post, _, adj in table:
-            for n, slot in enumerate(corner_slots(side, post, adj)):
-                out[2 * n + side : 2 * n + side + 1, :] = row(side, slot, x)
-
-
-def corner_call(first, second, after):
-    sz = first.shape[2]
-    out = pltpu.VMEM((8, sz), jnp.float32)
+    out_ref[...] = jnp.zeros_like(out_ref)
+    for side, post, _, adj in table:
+        for n, slot in enumerate(corner_slots(side, post, adj)):
+            out_ref[2 * n + side : 2 * n + side + 1, :] = row(side, slot)
+
+
+def corner_call(table, x, first, second, after):
     return pl.pallas_call(
-        corner_kernel,
+        functools.partial(corner_kernel, table, x),
         in_specs=[VMEM, VMEM, ANY],
-        out_specs=[VMEM, VMEM],
-        out_shape=[out, out],
+        out_specs=VMEM,
+        out_shape=pltpu.VMEM((8, first.shape[2]), jnp.float32),
         compiler_params=pltpu.CompilerParams(vmem_limit_bytes=2 << 20),
         name="corners",
     )(first, second, after)
@@ -566,29 +562,16 @@
     return [pltpu.make_async_copy(a, b, sem.at[k, n]) for k, (a, b) in enumerate(pairs)]
 
 
-def inner_kernel(
-    post_ref, adjf_ref, adjg_ref, fluid_ref, bcell_ref, first_ref, second_ref, profile_ref,
-    magnet_ref,
-    newf_ref, newg_ref, outf_ref, outg_ref, sums_ref,
-    new_v, out_v, halo_v, near_v, store_sem,
+def inner_planes(
+    start, stop, base, done, post_ref, adjf_ref, adjg_ref, fluid_ref, bcell_ref, profile_ref,
+    magnet_ref, new_v, out_v, halo_v, near_v, sums_ref,
 ):
-    sx = fluid_ref.shape[0]
-    count = sums_ref.shape[0]
-
-    def stores(x):
-        return plane_stores(
-            x, x, new_v, out_v, newf_ref, newg_ref, outf_ref, outg_ref, store_sem
-        )
-
-    sums_ref[...] = jnp.zeros_like(sums_ref)
-    load_halo(first_ref, second_ref, halo_v)
-
     def body(x, carry):
         def row_of(slot, dx, dy):
             return halo_v[0 if dy == -1 else 1, slot, pl.ds(x + dx, 1), :]
 
         plane_step(
-            x,
+            x - base,
             lambda i, dx: post_ref[i, x + dx],
             lambda i, dx, dy: row_of(halo_slot(0, i, dy), dx, dy),
             lambda i, dx: adj_plane(adjf_ref, adjg_ref, i, x + dx),
@@ -603,39 +586,113 @@
             new_v,
             out_v,
             sums_ref,
-            count,
+            sums_ref.shape[0],
         )
-        start_all(stores(x))
+        done(x)
         return carry
 
-    lax.fori_loop(1, sx - 1, body, 0)
-    for x in range(1, sx - 1):
-        wait_all(stores(x))
+    lax.fori_loop(start, stop, body, 0)
+
+
+def inner_kernel(
+    post_ref, adjf_ref, adjg_ref, fluid_ref, bcell_ref, first_ref, second_ref, profile_ref,
+    magnet_ref,
+    new_ref, out_ref, sums_ref, halo_ref,
+    near_v,
+):
+    sums_ref[...] = jnp.zeros_like(sums_ref)
+    load_halo(first_ref, second_ref, halo_ref)
+    inner_planes(
+        1, 1 + new_ref.shape[1], 1, lambda x: None, post_ref, adjf_ref, adjg_ref, fluid_ref,
+        bcell_ref, profile_ref, magnet_ref, new_ref, out_ref, halo_ref, near_v, sums_ref,
+    )
 
 
 def inner_call(post, adjf, adjg, fluid, bcell, first, second, profile, magnet, count):
     sx, sy, sz = profile.shape
-    full = pltpu.VMEM((NP, sx, sy, sz), jnp.float32)
+    part = pltpu.VMEM((NP, (sx - 2) // 2, sy, sz), jnp.float32)
+    return pl.pallas_call(
+        inner_kernel,
+        in_specs=[VMEM] * 9,
+        out_specs=[VMEM] * 4,
+        out_shape=[
+            part,
+            part,
+            pltpu.VMEM((count, 8, 128), jnp.float32),
+            pltpu.VMEM((2, SLOTS, sx, sz), jnp.float32),
+        ],
+        scratch_shapes=[pltpu.VMEM((18, sy, sz), jnp.float32)],
+        compiler_params=pltpu.CompilerParams(vmem_limit_bytes=OUTER_VMEM),
+        cost_estimate=pl.CostEstimate(
+            flops=350 * sx * sy * sz, bytes_accessed=8 * NP * sx * sy * sz, transcendentals=0
+        ),
+        name="inner",
+    )(post, adjf, adjg, fluid, bcell, first, second, profile, magnet)
+
+
+def rest_kernel(
+    post_ref, adjf_ref, adjg_ref, fluid_ref, bcell_ref, halo_ref, profile_ref, magnet_ref,
+    new_ref, out_ref, partial_ref, after_ref,
+    newf_ref, newg_ref, outf_ref, outg_ref, sums_ref,
+    new_v, out_v, near_v, store_sem,
+):
+    del after_ref
+    sx = fluid_ref.shape[0]
+    middle = 1 + new_ref.shape[1]
+
+    def stores(x):
+        pairs = (
+            (new_v.at[pl.ds(0, NF), x - middle], newf_ref.at[:, x]),
+            (new_v.at[pl.ds(NF, NG), x - middle], newg_ref.at[:, x]),
+            (out_v.at[pl.ds(0, NF), x - middle], outf_ref.at[:, x]),
+            (out_v.at[pl.ds(NF, NG), x - middle], outg_ref.at[:, x]),
+        )
+        return [pltpu.make_async_copy(a, b, store_sem.at[k, x]) for k, (a, b) in enumerate(pairs)]
+
+    early = []
+    for x in range(1, middle):
+        pairs = (
+            (new_ref.at[pl.ds(0, NF), x - 1], newf_ref.at[:, x]),
+            (new_ref.at[pl.ds(NF, NG), x - 1], newg_ref.at[:, x]),
+            (out_ref.at[pl.ds(0, NF), x - 1], outf_ref.at[:, x]),
+            (out_ref.at[pl.ds(NF, NG), x - 1], outg_ref.at[:, x]),
+        )
+        early += [pltpu.make_async_copy(a, b, store_sem.at[k, x]) for k, (a, b) in enumerate(pairs)]
+    start_all(early)
+    sums_ref[...] = partial_ref[...]
+    inner_planes(
+        middle, sx - 1, middle, lambda x: start_all(stores(x)), post_ref, adjf_ref, adjg_ref,
+        fluid_ref, bcell_ref, profile_ref, magnet_ref, new_v, out_v, halo_ref, near_v, sums_ref,
+    )
+    wait_all(early)
+    for x in range(middle, sx - 1):
+        wait_all(stores(x))
+
+
+def rest_call(
+    post, adjf, adjg, fluid, bcell, halo, profile, magnet, new, out, partial, after
+):
+    sx, sy, sz = profile.shape
+    part = pltpu.VMEM((NP, sx - 2 - new.shape[1], sy, sz), jnp.float32)
     flow = jax.ShapeDtypeStruct((NF, sx, sy, sz), jnp.float32)
     field = jax.ShapeDtypeStruct((NG, sx, sy, sz), jnp.float32)
     return pl.pallas_call(
-        inner_kernel,
-        in_specs=[VMEM] * 9,
+        rest_kernel,
+        in_specs=[VMEM] * 11 + [ANY],
         out_specs=[ANY, ANY, ANY, ANY, VMEM],
-        out_shape=[flow, field, flow, field, pltpu.VMEM((count, 8, 128), jnp.float32)],
+        out_shape=[flow, field, flow, field, pltpu.VMEM(partial.shape, jnp.float32)],
         scratch_shapes=[
-            full,
-            full,
-            pltpu.VMEM((2, SLOTS, sx, sz), jnp.float32),
+            part,
+            part,
             pltpu.VMEM((18, sy, sz), jnp.float32),
             pltpu.SemaphoreType.DMA((4, sx)),
         ],
-        compiler_params=pltpu.CompilerParams(vmem_limit_bytes=INNER_VMEM),
+        compiler_params=pltpu.CompilerParams(vmem_limit_bytes=OUTER_VMEM),
         cost_estimate=pl.CostEstimate(
-            flops=700 * sx * sy * sz, bytes_accessed=16 * NP * sx * sy * sz, transcendentals=0
+            flops=350 * sx * sy * sz, bytes_accessed=8 * NP * sx * sy * sz, transcendentals=0
         ),
-        name="inner",
-    )(post, adjf, adjg, fluid, bcell, first, second, profile, magnet)
+        name="rest",
+    )(post, adjf, adjg, fluid, bcell, halo, profile, magnet, new, out, partial, after)
 
 
 def outer_kernel(
@@ -766,11 +823,16 @@
     fromleft = lax.ppermute(right, "gx", ring(around, 1))
     fromright = lax.ppermute(left, "gx", ring(around, -1))
     post, fluid, bcell = collide_call(flow, field, profile, table, wall, magnet)
-    corner_r, corner_l = corner_call(first, second, bcell)
+    corner_r = corner_call(CORNER_RIGHT, flow.shape[1] - 1, first, second, bcell)
     cornerleft = lax.ppermute(corner_r, "gx", ring(around, 1))
+    new, out, partial, halo = inner_call(
+        post, adj_flow_in, adj_field_in, fluid, bcell, first, second, profile, magnet, count
+    )
+    corner_l = corner_call(CORNER_LEFT, 0, first, second, partial)
     cornerright = lax.ppermute(corner_l, "gx", ring(around, -1))
-    newf, newg, outf, outg, partial = inner_call(
-        post, adj_flow_in, adj_field_in, fluid, bcell, first, second, profile, magnet, count
+    newf, newg, outf, outg, partial = rest_call(
+        post, adj_flow_in, adj_field_in, fluid, bcell, halo, profile, magnet, new, out, partial,
+        corner_l,
     )
     cells = flow.shape[1] * around * flow.shape[2] * across * flow.shape[3]
     newf, newg, outf, outg, share = outer_call(

time: 33.4 us -> 34.7 us (1.039)
  blocking collectives: 9.61 us -> 11 us
    all_to_all x1, blocking collectives: 9.61 us -> 11 us  [on_device(): lax.all_to_all(share, ('gx', 'gy'), 0, 0, tiled=True)]
    pallas_call x2 -> x4, Pallas kernels: 3.8 us -> 3.96 us  [the longest x1 2.55 us: rest_call(): pl.pallas_call(rest_kernel, in_specs=[VMEM] * 11 + [ANY], out_specs=[ANY,...]
where the time goes in v9:
time: 34.7 us; the launch traced here: 34.6 us
  starting transfers between devices  12.3 us (35%)
  blocking collectives  11 us (32%)
  Pallas kernels  9.28 us (27%)
  between operations  0.81 us (2%)
  waiting for transfers between devices  0.56 us (2%)
  other arithmetic  0.56 us (2%)
    all_to_all x1, blocking collectives, on_device(): lax.all_to_all(share, ('gx', 'gy'), 0, 0, tiled=True)  11 us
    ppermute x1, starting transfers between devices, on_device(): second = lax.ppermute(mine2, 'gy', between)  3.4 us
    ppermute x1, starting transfers between devices, on_device(): cornerleft = lax.ppermute(corner_r, 'gx', ring(around, 1))  3.01 us
    pallas_call x1, Pallas kernels, rest_call(): pl.pallas_call(rest_kernel, in_specs=[VMEM] * 11 + [ANY], out_specs=[ANY,...  2.55 us
    pallas_call x1, Pallas kernels, rim_call(): pl.pallas_call(rim_kernel, in_specs=[ANY] * 8, out_specs=[VMEM] * 4, out_...  2.28 us
    ppermute x1, starting transfers between devices, on_device(): fromright = lax.ppermute(left, 'gx', ring(around, -1))  2.25 us
    ppermute x1, starting transfers between devices, on_device(): cornerright = lax.ppermute(corner_l, 'gx', ring(around, -1))  2.11 us
    pallas_call x1, Pallas kernels, outer_call(): pl.pallas_call(functools.partial(outer_kernel, scale), in_specs=[VMEM] *...  1.85 us
  transfers between devices with their start and end apart: 6, of which 1 were waited for; matrix products, arithmetic and copies ran while one was open for 0% of the time, Pallas kernels for 15%

profile of v9, /device:TPU:0, one launch (start us, length us, event | category | flops | bytes accessed | tf_op | source)
XLA Modules:
  0.0 34.6 jit_solution(16846247847942574701)
XLA Ops:
  0.6 0.0 copy-start.2
  0.6 0.0 copy-start.3
  0.7 0.0 copy-start.4
  0.7 2.3 %rims.1 = (f32[13,8,512]{2,1,0:T(8,128)S(1)}, f32[13,8,512]{2,1,0:T(8,128)S(1)}, f32[13,8,512]{2,1,0:T(8,128)S(1)}, f32[13,8,512]{2,1,0:T(8,128)S(1)}) custom-call(f32[19,8,8,512]{3,2,1,0:T(8,128)} %flow_ref.3, f32[7,8,8,512]{3,2,1,0:T(8,128)} %field_ref.3, f32[19,8,8,512]{3,2,1,0:T(8,128)} %adjf_ref.7, f32[7,8,8,512]{3,2,1,0:T(8,128)} %adjg_ref.7, ...), custom_call_target="tpu_custom_call" | custom-call | tf_op jit(solution)/shard_map/rims/pallas_call | solution.py:255
  3.0 0.0 copy-start
  3.0 0.0 copy-start.1
  3.0 3.4 %collective-permute-start = (f32[13,8,512]{2,1,0:T(8,128)S(1)}, f32[13,8,512]{2,1,0:T(8,128)S(1)}, u32[]{:S(2)}, u32[]{:S(2)}) collective-permute-start(f32[13,8,512]{2,1,0:T(8,128)S(1)} %get-tuple-element.26), channel_id=1, source_target_pairs={{0,7},{1,2},{2,1},{3,4},{4,3},{5,6},{6,5},{7,0},{8,15},{9,10},{10,... | collective-permute-start | bytes 638984 | tf_op jit(solution)/shard_map/ppermute | solution.py:821
  6.4 0.0 collective-permute-start.3
  6.4 1.6 %collective-permute-start.1 = (f32[13,8,512]{2,1,0:T(8,128)S(1)}, f32[13,8,512]{2,1,0:T(8,128)S(1)}, u32[]{:S(2)}, u32[]{:S(2)}) collective-permute-start(f32[13,8,512]{2,1,0:T(8,128)S(1)} %get-tuple-element.27), channel_id=1, source_target_pairs={{0,8},{8,16},{16,24},{24,0},{1,9},{9,17},{17,25},{25,1},{2,10},{10... | collective-permute-start | bytes 638984 | tf_op jit(solution)/shard_map/ppermute | solution.py:823
  8.0 2.2 %collective-permute-start.2 = (f32[13,8,512]{2,1,0:T(8,128)S(1)}, f32[13,8,512]{2,1,0:T(8,128)S(1)}, u32[]{:S(2)}, u32[]{:S(2)}) collective-permute-start(f32[13,8,512]{2,1,0:T(8,128)S(1)} %get-tuple-element.28), channel_id=1, source_target_pairs={{0,24},{8,0},{16,8},{24,16},{1,25},{9,1},{17,9},{25,17},{2,26},{10... | collective-permute-start | bytes 638984 | tf_op jit(solution)/shard_map/ppermute | solution.py:824
  10.3 1.2 %collide.1 = (f32[26,8,8,512]{3,2,1,0:T(8,128)S(1)}, f32[8,8,512]{2,1,0:T(8,128)S(1)}, f32[8,8,512]{2,1,0:T(8,128)S(1)}) custom-call(f32[19,8,8,512]{3,2,1,0:T(8,128)S(1)} %copy-done.2, f32[7,8,8,512]{3,2,1,0:T(8,128)S(1)} %copy-done.3, f32[8,8,512]{2,1,0:T(8,128)S(1)} %copy-done.4, f32[1,32]{1,0:T(1,128)S(1)} %bitcast.6, s32[8,8,512]{2,1,0:T(8,128)S(1)} %copy-done.6, ...), custom_call_target="tpu_custom_call" | custom-call | flops 9830400 | bytes 10223616 | tf_op jit(solution)/shard_map/collide/pallas_call | solution.py:302
  11.5 0.0 collective-permute-done.second_ref
  11.5 0.0 collective-permute-done.3.first_ref
  11.5 3.0 %collective-permute-start.4 = (f32[8,512]{1,0:T(8,128)S(1)}, f32[8,512]{1,0:T(8,128)S(1)}, u32[]{:S(2)}, u32[]{:S(2)}) collective-permute-start(f32[8,512]{1,0:T(8,128)S(1)} %corners.2), channel_id=1, source_target_pairs={{0,8},{8,16},{16,24},{24,0},{1,9},{9,17},{17,25},{25,1},{2,10},{10... | collective-permute-start | bytes 49160 | tf_op jit(solution)/shard_map/ppermute | solution.py:827
  14.5 1.4 %inner.1 = (f32[26,3,8,512]{3,2,1,0:T(8,128)S(1)}, f32[26,3,8,512]{3,2,1,0:T(8,128)S(1)}, f32[32,8,128]{2,1,0:T(8,128)S(1)}, f32[2,13,8,512]{3,2,1,0:T(8,128)S(1)}) custom-call(f32[26,8,8,512]{3,2,1,0:T(8,128)S(1)} %get-tuple-element.30.post_ref, f32[19,8,8,512]{3,2,1,0:T(8,128)S(1)} %copy-done, f32[7,8,8,512]{3,2,1,0:T(8,128)S(1)} %copy-done.1, ...), custom_call_target="tpu_custom_call" | custom-call | flops 11468800 | bytes 6815744 | tf_op jit(solution)/shard_map/inner/pallas_call | solution.py:614
  15.9 2.1 %collective-permute-start.5 = (f32[8,512]{1,0:T(8,128)S(1)}, f32[8,512]{1,0:T(8,128)S(1)}, u32[]{:S(2)}, u32[]{:S(2)}) collective-permute-start(f32[8,512]{1,0:T(8,128)S(1)} %corners.3.after_ref), channel_id=1, source_target_pairs={{0,24},{8,0},{16,8},{24,16},{1,25},{9,1},{17,9},{25,17},{2,26},{10... | collective-permute-start | bytes 49160 | tf_op jit(solution)/shard_map/ppermute | solution.py:832
  18.0 2.5 %rest.1 = (f32[19,8,8,512]{3,2,1,0:T(8,128)}, f32[7,8,8,512]{3,2,1,0:T(8,128)}, f32[19,8,8,512]{3,2,1,0:T(8,128)}, f32[7,8,8,512]{3,2,1,0:T(8,128)}, f32[32,8,128]{2,1,0:T(8,128)S(1)}) custom-call(f32[26,8,8,512]{3,2,1,0:T(8,128)S(1)} %get-tuple-element.30.post_ref, f32[19,8,8,512]{3,2,1,0:T(8,128)S(1)} %copy-done, f32[7,8,8,512]{3,2,1,0:T(8,128)S(1)} %copy-done.1, ...), custom_call_target="tpu_custom_call" | custom-call | flops 11468800 | bytes 6815744 | tf_op jit(solution)/shard_map/rest/pallas_call | solution.py:679
  20.6 0.0 collective-permute-done.1.fromleft_ref
  20.6 0.0 collective-permute-done.2.fromright_ref
  20.6 0.6 %collective-permute-done.4.cornerleft_ref = f32[8,512]{1,0:T(8,128)S(1)} collective-permute-done((f32[8,512]{1,0:T(8,128)S(1)}, f32[8,512]{1,0:T(8,128)S(1)}, u32[]{:S(2)}, u32[]{:S(2)}) %collective-permute-start.4) | collective-permute-done | bytes 16416 | tf_op jit(solution)/shard_map/ppermute | solution.py:827
  21.2 0.0 collective-permute-done.5.cornerright_ref
  21.2 1.9 %outer.1 = (f32[19,8,8,512]{3,2,1,0:T(8,128)}, f32[7,8,8,512]{3,2,1,0:T(8,128)}, f32[19,8,8,512]{3,2,1,0:T(8,128)}, f32[7,8,8,512]{3,2,1,0:T(8,128)}, f32[32,32]{1,0:T(8,128)S(1)}) custom-call(f32[13,8,512]{2,1,0:T(8,128)S(1)} %collective-permute-done.second_ref, ...), custom_call_target="tpu_custom_call", output_to_operand_aliasing={{0}: (14, {}), {1}: (15, {}), {2}: (16, {}), {3}: (17, {})} | custom-call | tf_op jit(solution)/shard_map/outer/pallas_call | solution.py:781
  23.0 11.0 %all_to_all.9 = f32[32,1,32]{2,1,0:T(1,128)S(1)} all-to-all(f32[32,1,32]{2,1,0:T(1,128)S(1)} %bitcast.4), channel_id=1, replica_groups=mesh['gx'=4,'gy'=8] {'gx','gy'}, dimensions={0} | all-to-all | bytes 8192 | tf_op jit(solution)/shard_map/all_to_all | solution.py:842
  34.0 0.6 %reduce_sum.9 = f32[32]{0:T(128)} reduce(f32[32,1,32]{2,1,0:T(1,128)S(1)} %all_to_all.9, f32[]{:T(128)} %constant.0.clone.1), dimensions={0,1}, to_apply=%region_0.0 | reduce | flops 992 | bytes 4228 | tf_op jit(solution)/shard_map/reduce_sum | solution.py:842
  (13 shorter events, 0.1 us)
Async XLA Ops:
  0.6 9.6 %copy-start.2 = (f32[19,8,8,512]{3,2,1,0:T(8,128)S(1)}, f32[19,8,8,512]{3,2,1,0:T(8,128)}, u32[]{:S(2)}) copy-start(f32[19,8,8,512]{3,2,1,0:T(8,128)} %flow_ref.3) | copy-start | bytes 7471108
  0.6 9.6 %copy-start.3 = (f32[7,8,8,512]{3,2,1,0:T(8,128)S(1)}, f32[7,8,8,512]{3,2,1,0:T(8,128)}, u32[]{:S(2)}) copy-start(f32[7,8,8,512]{3,2,1,0:T(8,128)} %field_ref.3) | copy-start | bytes 2752516
  0.7 9.6 %copy-start.4 = (f32[8,8,512]{2,1,0:T(8,128)S(1)}, f32[8,8,512]{2,1,0:T(8,128)}, u32[]{:S(2)}) copy-start(f32[8,8,512]{2,1,0:T(8,128)} %profile_ref.9) | copy-start | bytes 393220
  0.7 9.6 %copy-start.5 = (s32[8,8,512]{2,1,0:T(8,128)S(1)}, s32[8,8,512]{2,1,0:T(8,128)}, u32[]{:S(2)}) copy-start(s32[8,8,512]{2,1,0:T(8,128)} %magnet_ref.9) | copy-start | bytes 393220
  0.7 9.6 %copy-start.6 = (s32[8,8,512]{2,1,0:T(8,128)S(1)}, s32[8,8,512]{2,1,0:T(8,128)}, u32[]{:S(2)}) copy-start(s32[8,8,512]{2,1,0:T(8,128)} %wall_ref.3) | copy-start | bytes 393220
  0.7 9.6 %copy-start.7 = (f32[32]{0:T(128)S(1)}, f32[32]{0:T(128)}, u32[]{:S(2)}) copy-start(f32[32]{0:T(128)} %param.13) | copy-start | bytes 388
  3.0 11.5 %copy-start = (f32[19,8,8,512]{3,2,1,0:T(8,128)S(1)}, f32[19,8,8,512]{3,2,1,0:T(8,128)}, u32[]{:S(2)}) copy-start(f32[19,8,8,512]{3,2,1,0:T(8,128)} %adjf_ref.7) | copy-start | bytes 7471108
  3.0 11.5 %copy-start.1 = (f32[7,8,8,512]{3,2,1,0:T(8,128)S(1)}, f32[7,8,8,512]{3,2,1,0:T(8,128)}, u32[]{:S(2)}) copy-start(f32[7,8,8,512]{3,2,1,0:T(8,128)} %adjg_ref.7) | copy-start | bytes 2752516
  3.0 8.5 %collective-permute-start = (f32[13,8,512]{2,1,0:T(8,128)S(1)}, f32[13,8,512]{2,1,0:T(8,128)S(1)}, u32[]{:S(2)}, u32[]{:S(2)}) collective-permute-start(f32[13,8,512]{2,1,0:T(8,128)S(1)} %get-tuple-element.26), channel_id=1, source_target_pairs={{0,7},{1,2},{2,1},{3,4},{4,3},{5,6},{6,5},{7,0},{8,15},{9,10},{10,... | collective-permute-start | bytes 638984 | tf_op jit(solution)/shard_map/ppermute | solution.py:821
  6.4 5.1 %collective-permute-start.3 = (f32[13,8,512]{2,1,0:T(8,128)S(1)}, f32[13,8,512]{2,1,0:T(8,128)S(1)}, u32[]{:S(2)}, u32[]{:S(2)}) collective-permute-start(f32[13,8,512]{2,1,0:T(8,128)S(1)} %get-tuple-element.29), channel_id=1, source_target_pairs={{0,1},{1,0},{2,3},{3,2},{4,5},{5,4},{6,7},{7,6},{8,9},{9,8},{10,11... | collective-permute-start | bytes 638984 | tf_op jit(solution)/shard_map/ppermute | solution.py:822
  6.4 14.2 %collective-permute-start.1 = (f32[13,8,512]{2,1,0:T(8,128)S(1)}, f32[13,8,512]{2,1,0:T(8,128)S(1)}, u32[]{:S(2)}, u32[]{:S(2)}) collective-permute-start(f32[13,8,512]{2,1,0:T(8,128)S(1)} %get-tuple-element.27), channel_id=1, source_target_pairs={{0,8},{8,16},{16,24},{24,0},{1,9},{9,17},{17,25},{25,1},{2,10},{10... | collective-permute-start | bytes 638984 | tf_op jit(solution)/shard_map/ppermute | solution.py:823
  8.0 12.6 %collective-permute-start.2 = (f32[13,8,512]{2,1,0:T(8,128)S(1)}, f32[13,8,512]{2,1,0:T(8,128)S(1)}, u32[]{:S(2)}, u32[]{:S(2)}) collective-permute-start(f32[13,8,512]{2,1,0:T(8,128)S(1)} %get-tuple-element.28), channel_id=1, source_target_pairs={{0,24},{8,0},{16,8},{24,16},{1,25},{9,1},{17,9},{25,17},{2,26},{10... | collective-permute-start | bytes 638984 | tf_op jit(solution)/shard_map/ppermute | solution.py:824
  11.5 9.7 %collective-permute-start.4 = (f32[8,512]{1,0:T(8,128)S(1)}, f32[8,512]{1,0:T(8,128)S(1)}, u32[]{:S(2)}, u32[]{:S(2)}) collective-permute-start(f32[8,512]{1,0:T(8,128)S(1)} %corners.2), channel_id=1, source_target_pairs={{0,8},{8,16},{16,24},{24,0},{1,9},{9,17},{17,25},{25,1},{2,10},{10... | collective-permute-start | bytes 49160 | tf_op jit(solution)/shard_map/ppermute | solution.py:827
  15.9 5.2 %collective-permute-start.5 = (f32[8,512]{1,0:T(8,128)S(1)}, f32[8,512]{1,0:T(8,128)S(1)}, u32[]{:S(2)}, u32[]{:S(2)}) collective-permute-start(f32[8,512]{1,0:T(8,128)S(1)} %corners.3.after_ref), channel_id=1, source_target_pairs={{0,24},{8,0},{16,8},{24,16},{1,25},{9,1},{17,9},{25,17},{2,26},{10... | collective-permute-start | bytes 49160 | tf_op jit(solution)/shard_map/ppermute | solution.py:832

commit v10 on v8

--- a/solution.py
+++ b/solution.py
@@ -641,7 +641,7 @@
 def outer_kernel(
     scale, second_ref, fromleft_ref, fromright_ref, first_ref, post_ref, adjf_ref, adjg_ref,
     fluid_ref, bcell_ref,
-    cornerleft_ref, cornerright_ref, profile_ref, magnet_ref,
+    cornerright_ref, cornerleft_ref, profile_ref, magnet_ref,
     partial_ref, newf_in, newg_in, outf_in, outg_in,
     newf_ref, newg_ref, outf_ref, outg_ref, share_ref,
     new_v, out_v, halo_v, near_v, sums_v, store_sem,
@@ -744,8 +744,8 @@
         compiler_params=pltpu.CompilerParams(vmem_limit_bytes=OUTER_VMEM),
         name="outer",
     )(
-        second, fromleft, fromright, first, post, adjf, adjg, fluid, bcell, cornerleft,
-        cornerright, profile, magnet, partial, newf, newg, outf, outg,
+        second, fromleft, fromright, first, post, adjf, adjg, fluid, bcell, cornerright,
+        cornerleft, profile, magnet, partial, newf, newg, outf, outg,
     )
 
 

time: 33.4 us -> 35.2 us (1.054)
  waiting for transfers between devices: 0.76 us -> 1.72 us
  blocking collectives: 9.61 us -> 10.5 us
    ppermute x1, starting transfers between devices: 3.01 us -> 0.01 us  [on_device(): cornerleft = lax.ppermute(corner_r, 'gx', ring(around, 1))]
    ppermute x1, starting transfers between devices: 2.09 us -> 5.03 us  [on_device(): cornerright = lax.ppermute(corner_l, 'gx', ring(around, -1))]
    ppermute x1, waiting for transfers between devices: 0.75 us -> 1.71 us  [on_device(): cornerleft = lax.ppermute(corner_r, 'gx', ring(around, 1))]
    all_to_all x1, blocking collectives: 9.61 us -> 10.5 us  [on_device(): lax.all_to_all(share, ('gx', 'gy'), 0, 0, tiled=True)]
  transfers between devices with their start and end apart: 6 -> 6, of which waited for: 1 -> 1; matrix products, arithmetic and copies ran while one was open for 0% -> 0% of each run, Pallas kernels for 15% -> 14%
where the time goes in v10:
time: 35.2 us; the launch traced here: 35 us
  starting transfers between devices  12.3 us (35%)
  blocking collectives  10.5 us (30%)
  Pallas kernels  9.12 us (26%)
  waiting for transfers between devices  1.72 us (5%)
  between operations  0.8 us (2%)
  other arithmetic  0.56 us (2%)
    all_to_all x1, blocking collectives, on_device(): lax.all_to_all(share, ('gx', 'gy'), 0, 0, tiled=True)  10.5 us
    ppermute x1, starting transfers between devices, on_device(): cornerright = lax.ppermute(corner_l, 'gx', ring(around, -1))  5.03 us
    pallas_call x1, Pallas kernels, inner_call(): pl.pallas_call(inner_kernel, in_specs=[VMEM] * 9, out_specs=[ANY, ANY, AN...  3.78 us
    ppermute x1, starting transfers between devices, on_device(): second = lax.ppermute(mine2, 'gy', between)  3.4 us
    pallas_call x1, Pallas kernels, rim_call(): pl.pallas_call(rim_kernel, in_specs=[ANY] * 8, out_specs=[VMEM] * 4, out_...  2.28 us
    ppermute x1, starting transfers between devices, on_device(): fromright = lax.ppermute(left, 'gx', ring(around, -1))  2.25 us
    pallas_call x1, Pallas kernels, outer_call(): pl.pallas_call(functools.partial(outer_kernel, scale), in_specs=[VMEM] *...  1.85 us
    ppermute x1, waiting for transfers between devices, on_device(): cornerleft = lax.ppermute(corner_r, 'gx', ring(around, 1))  1.71 us
  transfers between devices with their start and end apart: 6, of which 1 were waited for; matrix products, arithmetic and copies ran while one was open for 0% of the time, Pallas kernels for 14%

profile of v10, /device:TPU:0, one launch (start us, length us, event | category | flops | bytes accessed | tf_op | source)
XLA Modules:
  0.0 35.0 jit_solution(9164640740532792449)
XLA Ops:
  0.6 0.0 copy-start.1
  0.6 0.0 copy-start.3
  0.7 0.0 copy-start.4
  0.7 2.3 %rims.1 = (f32[13,8,512]{2,1,0:T(8,128)S(1)}, f32[13,8,512]{2,1,0:T(8,128)S(1)}, f32[13,8,512]{2,1,0:T(8,128)S(1)}, f32[13,8,512]{2,1,0:T(8,128)S(1)}) custom-call(f32[19,8,8,512]{3,2,1,0:T(8,128)} %flow_ref.3, f32[7,8,8,512]{3,2,1,0:T(8,128)} %field_ref.3, f32[19,8,8,512]{3,2,1,0:T(8,128)} %adjf_ref.5, f32[7,8,8,512]{3,2,1,0:T(8,128)} %adjg_ref.5, ...), custom_call_target="tpu_custom_call" | custom-call | tf_op jit(solution)/shard_map/rims/pallas_call | solution.py:255
  3.0 0.0 copy-start
  3.0 0.0 copy-start.2
  3.0 3.4 %collective-permute-start = (f32[13,8,512]{2,1,0:T(8,128)S(1)}, f32[13,8,512]{2,1,0:T(8,128)S(1)}, u32[]{:S(2)}, u32[]{:S(2)}) collective-permute-start(f32[13,8,512]{2,1,0:T(8,128)S(1)} %get-tuple-element.24), channel_id=1, source_target_pairs={{0,7},{1,2},{2,1},{3,4},{4,3},{5,6},{6,5},{7,0},{8,15},{9,10},{10,... | collective-permute-start | bytes 638984 | tf_op jit(solution)/shard_map/ppermute | solution.py:764
  6.4 0.0 collective-permute-start.3
  6.4 1.6 %collective-permute-start.1 = (f32[13,8,512]{2,1,0:T(8,128)S(1)}, f32[13,8,512]{2,1,0:T(8,128)S(1)}, u32[]{:S(2)}, u32[]{:S(2)}) collective-permute-start(f32[13,8,512]{2,1,0:T(8,128)S(1)} %get-tuple-element.25), channel_id=1, source_target_pairs={{0,8},{8,16},{16,24},{24,0},{1,9},{9,17},{17,25},{25,1},{2,10},{10... | collective-permute-start | bytes 638984 | tf_op jit(solution)/shard_map/ppermute | solution.py:766
  8.0 2.2 %collective-permute-start.2 = (f32[13,8,512]{2,1,0:T(8,128)S(1)}, f32[13,8,512]{2,1,0:T(8,128)S(1)}, u32[]{:S(2)}, u32[]{:S(2)}) collective-permute-start(f32[13,8,512]{2,1,0:T(8,128)S(1)} %get-tuple-element.26), channel_id=1, source_target_pairs={{0,24},{8,0},{16,8},{24,16},{1,25},{9,1},{17,9},{25,17},{2,26},{10... | collective-permute-start | bytes 638984 | tf_op jit(solution)/shard_map/ppermute | solution.py:767
  10.3 1.2 %collide.1 = (f32[26,8,8,512]{3,2,1,0:T(8,128)S(1)}, f32[8,8,512]{2,1,0:T(8,128)S(1)}, f32[8,8,512]{2,1,0:T(8,128)S(1)}) custom-call(f32[19,8,8,512]{3,2,1,0:T(8,128)S(1)} %copy-done.1, f32[7,8,8,512]{3,2,1,0:T(8,128)S(1)} %copy-done.3, f32[8,8,512]{2,1,0:T(8,128)S(1)} %copy-done.4, f32[1,32]{1,0:T(1,128)S(1)} %bitcast.6, s32[8,8,512]{2,1,0:T(8,128)S(1)} %copy-done.6, ...), custom_call_target="tpu_custom_call" | custom-call | flops 9830400 | bytes 10223616 | tf_op jit(solution)/shard_map/collide/pallas_call | solution.py:302
  11.5 0.0 collective-permute-done.second_ref
  11.5 0.0 collective-permute-done.3.first_ref
  11.5 5.0 %collective-permute-start.4 = (f32[8,512]{1,0:T(8,128)S(1)}, f32[8,512]{1,0:T(8,128)S(1)}, u32[]{:S(2)}, u32[]{:S(2)}) collective-permute-start(f32[8,512]{1,0:T(8,128)S(1)} %get-tuple-element.31), channel_id=1, source_target_pairs={{0,24},{8,0},{16,8},{24,16},{1,25},{9,1},{17,9},{25,17},{2,26},{10... | collective-permute-start | bytes 49160 | tf_op jit(solution)/shard_map/ppermute | solution.py:771
  16.5 0.0 collective-permute-start.5
  16.5 0.0 copy-done
  16.6 3.8 %inner.1 = (f32[19,8,8,512]{3,2,1,0:T(8,128)}, f32[7,8,8,512]{3,2,1,0:T(8,128)}, f32[19,8,8,512]{3,2,1,0:T(8,128)}, f32[7,8,8,512]{3,2,1,0:T(8,128)}, f32[32,8,128]{2,1,0:T(8,128)S(1)}) custom-call(f32[26,8,8,512]{3,2,1,0:T(8,128)S(1)} %get-tuple-element.28.post_ref, f32[19,8,8,512]{3,2,1,0:T(8,128)S(1)} %copy-done, f32[7,8,8,512]{3,2,1,0:T(8,128)S(1)} %copy-done.2, ...), custom_call_target="tpu_custom_call" | custom-call | flops 22937600 | bytes 13631488 | tf_op jit(solution)/shard_map/inner/pallas_call | solution.py:621
  20.3 0.0 collective-permute-done.1.fromleft_ref
  20.4 0.0 collective-permute-done.2.fromright_ref
  20.4 0.0 collective-permute-done.4.cornerright_ref
  20.4 1.7 %collective-permute-done.5.cornerleft_ref = f32[8,512]{1,0:T(8,128)S(1)} collective-permute-done((f32[8,512]{1,0:T(8,128)S(1)}, f32[8,512]{1,0:T(8,128)S(1)}, u32[]{:S(2)}, u32[]{:S(2)}) %collective-permute-start.5) | collective-permute-done | bytes 16416 | tf_op jit(solution)/shard_map/ppermute | solution.py:770
  22.1 1.9 %outer.1 = (f32[19,8,8,512]{3,2,1,0:T(8,128)}, f32[7,8,8,512]{3,2,1,0:T(8,128)}, f32[19,8,8,512]{3,2,1,0:T(8,128)}, f32[7,8,8,512]{3,2,1,0:T(8,128)}, f32[32,32]{1,0:T(8,128)S(1)}) custom-call(f32[13,8,512]{2,1,0:T(8,128)S(1)} %collective-permute-done.second_ref, ...), custom_call_target="tpu_custom_call", output_to_operand_aliasing={{0}: (14, {}), {1}: (15, {}), {2}: (16, {}), {3}: (17, {})} | custom-call | tf_op jit(solution)/shard_map/outer/pallas_call | solution.py:724
  23.9 10.5 %all_to_all.9 = f32[32,1,32]{2,1,0:T(1,128)S(1)} all-to-all(f32[32,1,32]{2,1,0:T(1,128)S(1)} %bitcast.4), channel_id=1, replica_groups=mesh['gx'=4,'gy'=8] {'gx','gy'}, dimensions={0} | all-to-all | bytes 8192 | tf_op jit(solution)/shard_map/all_to_all | solution.py:780
  34.4 0.6 %reduce_sum.9 = f32[32]{0:T(128)} reduce(f32[32,1,32]{2,1,0:T(1,128)S(1)} %all_to_all.9, f32[]{:T(128)} %constant.0.clone.1), dimensions={0,1}, to_apply=%region_0.0 | reduce | flops 992 | bytes 4228 | tf_op jit(solution)/shard_map/reduce_sum | solution.py:780
  (11 shorter events, 0.0 us)
Async XLA Ops:
  0.6 9.6 %copy-start.1 = (f32[19,8,8,512]{3,2,1,0:T(8,128)S(1)}, f32[19,8,8,512]{3,2,1,0:T(8,128)}, u32[]{:S(2)}) copy-start(f32[19,8,8,512]{3,2,1,0:T(8,128)} %flow_ref.3) | copy-start | bytes 7471108
  0.6 9.6 %copy-start.3 = (f32[7,8,8,512]{3,2,1,0:T(8,128)S(1)}, f32[7,8,8,512]{3,2,1,0:T(8,128)}, u32[]{:S(2)}) copy-start(f32[7,8,8,512]{3,2,1,0:T(8,128)} %field_ref.3) | copy-start | bytes 2752516
  0.7 9.6 %copy-start.4 = (f32[8,8,512]{2,1,0:T(8,128)S(1)}, f32[8,8,512]{2,1,0:T(8,128)}, u32[]{:S(2)}) copy-start(f32[8,8,512]{2,1,0:T(8,128)} %profile_ref.7) | copy-start | bytes 393220
  0.7 9.6 %copy-start.5 = (s32[8,8,512]{2,1,0:T(8,128)S(1)}, s32[8,8,512]{2,1,0:T(8,128)}, u32[]{:S(2)}) copy-start(s32[8,8,512]{2,1,0:T(8,128)} %magnet_ref.7) | copy-start | bytes 393220
  0.7 9.6 %copy-start.6 = (s32[8,8,512]{2,1,0:T(8,128)S(1)}, s32[8,8,512]{2,1,0:T(8,128)}, u32[]{:S(2)}) copy-start(s32[8,8,512]{2,1,0:T(8,128)} %wall_ref.3) | copy-start | bytes 393220
  0.7 9.6 %copy-start.7 = (f32[32]{0:T(128)S(1)}, f32[32]{0:T(128)}, u32[]{:S(2)}) copy-start(f32[32]{0:T(128)} %param.13) | copy-start | bytes 388
  3.0 13.6 %copy-start = (f32[19,8,8,512]{3,2,1,0:T(8,128)S(1)}, f32[19,8,8,512]{3,2,1,0:T(8,128)}, u32[]{:S(2)}) copy-start(f32[19,8,8,512]{3,2,1,0:T(8,128)} %adjf_ref.5) | copy-start | bytes 7471108
  3.0 13.6 %copy-start.2 = (f32[7,8,8,512]{3,2,1,0:T(8,128)S(1)}, f32[7,8,8,512]{3,2,1,0:T(8,128)}, u32[]{:S(2)}) copy-start(f32[7,8,8,512]{3,2,1,0:T(8,128)} %adjg_ref.5) | copy-start | bytes 2752516
  3.0 8.5 %collective-permute-start = (f32[13,8,512]{2,1,0:T(8,128)S(1)}, f32[13,8,512]{2,1,0:T(8,128)S(1)}, u32[]{:S(2)}, u32[]{:S(2)}) collective-permute-start(f32[13,8,512]{2,1,0:T(8,128)S(1)} %get-tuple-element.24), channel_id=1, source_target_pairs={{0,7},{1,2},{2,1},{3,4},{4,3},{5,6},{6,5},{7,0},{8,15},{9,10},{10,... | collective-permute-start | bytes 638984 | tf_op jit(solution)/shard_map/ppermute | solution.py:764
  6.4 5.1 %collective-permute-start.3 = (f32[13,8,512]{2,1,0:T(8,128)S(1)}, f32[13,8,512]{2,1,0:T(8,128)S(1)}, u32[]{:S(2)}, u32[]{:S(2)}) collective-permute-start(f32[13,8,512]{2,1,0:T(8,128)S(1)} %get-tuple-element.27), channel_id=1, source_target_pairs={{0,1},{1,0},{2,3},{3,2},{4,5},{5,4},{6,7},{7,6},{8,9},{9,8},{10,11... | collective-permute-start | bytes 638984 | tf_op jit(solution)/shard_map/ppermute | solution.py:765
  6.4 13.9 %collective-permute-start.1 = (f32[13,8,512]{2,1,0:T(8,128)S(1)}, f32[13,8,512]{2,1,0:T(8,128)S(1)}, u32[]{:S(2)}, u32[]{:S(2)}) collective-permute-start(f32[13,8,512]{2,1,0:T(8,128)S(1)} %get-tuple-element.25), channel_id=1, source_target_pairs={{0,8},{8,16},{16,24},{24,0},{1,9},{9,17},{17,25},{25,1},{2,10},{10... | collective-permute-start | bytes 638984 | tf_op jit(solution)/shard_map/ppermute | solution.py:766
  8.0 12.4 %collective-permute-start.2 = (f32[13,8,512]{2,1,0:T(8,128)S(1)}, f32[13,8,512]{2,1,0:T(8,128)S(1)}, u32[]{:S(2)}, u32[]{:S(2)}) collective-permute-start(f32[13,8,512]{2,1,0:T(8,128)S(1)} %get-tuple-element.26), channel_id=1, source_target_pairs={{0,24},{8,0},{16,8},{24,16},{1,25},{9,1},{17,9},{25,17},{2,26},{10... | collective-permute-start | bytes 638984 | tf_op jit(solution)/shard_map/ppermute | solution.py:767
  11.5 8.9 %collective-permute-start.4 = (f32[8,512]{1,0:T(8,128)S(1)}, f32[8,512]{1,0:T(8,128)S(1)}, u32[]{:S(2)}, u32[]{:S(2)}) collective-permute-start(f32[8,512]{1,0:T(8,128)S(1)} %get-tuple-element.31), channel_id=1, source_target_pairs={{0,24},{8,0},{16,8},{24,16},{1,25},{9,1},{17,9},{25,17},{2,26},{10... | collective-permute-start | bytes 49160 | tf_op jit(solution)/shard_map/ppermute | solution.py:771
  16.5 5.5 %collective-permute-start.5 = (f32[8,512]{1,0:T(8,128)S(1)}, f32[8,512]{1,0:T(8,128)S(1)}, u32[]{:S(2)}, u32[]{:S(2)}) collective-permute-start(f32[8,512]{1,0:T(8,128)S(1)} %get-tuple-element.32), channel_id=1, source_target_pairs={{0,8},{8,16},{16,24},{24,0},{1,9},{9,17},{17,25},{25,1},{2,10},{10... | collective-permute-start | bytes 49160 | tf_op jit(solution)/shard_map/ppermute | solution.py:770

commit v11 on v8

--- a/solution.py
+++ b/solution.py
@@ -46,6 +46,7 @@
 LEFT = [2, 8, 10, 12, 14, NF + 2]
 SLOTS = 13
 MASK = 12
+TURNED = [5, 6, 11, 12, 13, 14, NF + 5, NF + 6]
 
 RIM_VMEM = 58 << 20
 COLLIDE_VMEM = 4 << 20
@@ -277,7 +278,8 @@
 
 def collide_kernel(
     flow_ref, field_ref, profile_ref, strengths_ref, wall_ref, magnet_ref,
-    post_ref, fluid_ref, bcell_ref,
+    adjf_ref, adjg_ref,
+    post_ref, fluid_ref, bcell_ref, turned_ref, zfluid_ref,
 ):
     table = lane_table(strengths_ref)
 
@@ -288,28 +290,44 @@
         bcell_ref[x] = bcell
         f = [flow_ref[i, x] for i in range(NF)]
         g = [field_ref[k, x] for k in range(NG)]
-        for i, value in collide(f, g, fluid, bcell, range(NP)).items():
+        post = collide(f, g, fluid, bcell, range(NP))
+        for i, value in post.items():
             post_ref[i, x] = value
+        sz = fluid.shape[1]
+        for n, i in enumerate(TURNED):
+            up = LATTICE[i if i < NF else i - NF][2] > 0
+            turned_ref[n, x] = pltpu.roll(post[i], 1 if up else sz - 1, 1)
+            value = adj_plane(adjf_ref, adjg_ref, i, x)
+            turned_ref[len(TURNED) + n, x] = pltpu.roll(value, sz - 1 if up else 1, 1)
+        zi = lax.broadcasted_iota(jnp.int32, fluid.shape, 1)
+        zfluid_ref[0, x] = jnp.where(zi == 0, 0.0, pltpu.roll(fluid, 1, 1))
+        zfluid_ref[1, x] = jnp.where(zi == sz - 1, 0.0, pltpu.roll(fluid, sz - 1, 1))
         return carry
 
     lax.fori_loop(0, fluid_ref.shape[0], body, 0)
 
 
-def collide_call(flow, field, profile, strengths, wall, magnet):
+def collide_call(flow, field, profile, strengths, wall, magnet, adjf, adjg):
     sx, sy, sz = profile.shape
     full = pltpu.VMEM((NP, sx, sy, sz), jnp.float32)
     cells = pltpu.VMEM((sx, sy, sz), jnp.float32)
     return pl.pallas_call(
         collide_kernel,
-        in_specs=[VMEM] * 6,
-        out_specs=[VMEM] * 3,
-        out_shape=[full, cells, cells],
+        in_specs=[VMEM] * 8,
+        out_specs=[VMEM] * 5,
+        out_shape=[
+            full,
+            cells,
+            cells,
+            pltpu.VMEM((2 * len(TURNED), sx, sy, sz), jnp.float32),
+            pltpu.VMEM((2, sx, sy, sz), jnp.float32),
+        ],
         compiler_params=pltpu.CompilerParams(vmem_limit_bytes=COLLIDE_VMEM),
         cost_estimate=pl.CostEstimate(
             flops=300 * sx * sy * sz, bytes_accessed=12 * NP * sx * sy * sz, transcendentals=0
         ),
         name="collide",
-    )(flow, field, profile, strengths, wall, magnet)
+    )(flow, field, profile, strengths, wall, magnet, adjf, adjg)
 
 
 CORNER_RIGHT = ((0, 7, 0, 8), (1, 9, 1, 10))
@@ -352,7 +370,7 @@
 
 def plane_step(
     x_index, post, post_row, adj, adj_row, mask, mask_row, fluid, bcell, profile, magnet,
-    near_ref, new_ref, out_ref, sums_ref, count,
+    near_ref, new_ref, out_ref, sums_ref, count, turned, zmask,
 ):
     sy, sz = fluid.shape
     yi = lax.broadcasted_iota(jnp.int32, (sy, sz), 0)
@@ -373,10 +391,18 @@
 
     def moved(get, get_row, i, sign):
         dx, dy, dz = (sign * c for c in LATTICE[i if i < NF else i - NF])
+        if dz and not dy:
+            value = turned(0 if sign == -1 else 1, i, dx)
+            if value is not None:
+                return value
         return shift(get(i, dx), lambda: get_row(i, dx, dy), dy, dz)
 
     def near_of(i, sign):
         dx, dy, dz = (sign * c for c in LATTICE[i])
+        if dz and not dy:
+            value = zmask(dx, dz)
+            if value is not None:
+                return value
         value = shift(mask(dx), lambda: mask_row(dx, dy), dy, dz)
         if dz == -1:
             value = jnp.where(zfirst, 0.0, value)
@@ -568,7 +594,7 @@
 
 def inner_kernel(
     post_ref, adjf_ref, adjg_ref, fluid_ref, bcell_ref, first_ref, second_ref, profile_ref,
-    magnet_ref,
+    magnet_ref, turned_ref, zfluid_ref,
     newf_ref, newg_ref, outf_ref, outg_ref, sums_ref,
     new_v, out_v, halo_v, near_v, store_sem,
 ):
@@ -604,6 +630,8 @@
             out_v,
             sums_ref,
             count,
+            lambda kind, i, dx: turned_ref[len(TURNED) * kind + TURNED.index(i), x + dx],
+            lambda dx, dz: zfluid_ref[0 if dz == -1 else 1, x + dx],
         )
         start_all(stores(x))
         return carry
@@ -613,14 +641,14 @@
         wait_all(stores(x))
 
 
-def inner_call(post, adjf, adjg, fluid, bcell, first, second, profile, magnet, count):
+def inner_call(post, adjf, adjg, fluid, bcell, first, second, profile, magnet, turned, zfluid, count):
     sx, sy, sz = profile.shape
     full = pltpu.VMEM((NP, sx, sy, sz), jnp.float32)
     flow = jax.ShapeDtypeStruct((NF, sx, sy, sz), jnp.float32)
     field = jax.ShapeDtypeStruct((NG, sx, sy, sz), jnp.float32)
     return pl.pallas_call(
         inner_kernel,
-        in_specs=[VMEM] * 9,
+        in_specs=[VMEM] * 11,
         out_specs=[ANY, ANY, ANY, ANY, VMEM],
         out_shape=[flow, field, flow, field, pltpu.VMEM((count, 8, 128), jnp.float32)],
         scratch_shapes=[
@@ -635,13 +663,13 @@
             flops=700 * sx * sy * sz, bytes_accessed=16 * NP * sx * sy * sz, transcendentals=0
         ),
         name="inner",
-    )(post, adjf, adjg, fluid, bcell, first, second, profile, magnet)
+    )(post, adjf, adjg, fluid, bcell, first, second, profile, magnet, turned, zfluid)
 
 
 def outer_kernel(
     scale, second_ref, fromleft_ref, fromright_ref, first_ref, post_ref, adjf_ref, adjg_ref,
     fluid_ref, bcell_ref,
-    cornerleft_ref, cornerright_ref, profile_ref, magnet_ref,
+    cornerleft_ref, cornerright_ref, profile_ref, magnet_ref, turned_ref, zfluid_ref,
     partial_ref, newf_in, newg_in, outf_in, outg_in,
     newf_ref, newg_ref, outf_ref, outg_ref, share_ref,
     new_v, out_v, halo_v, near_v, sums_v, store_sem,
@@ -694,6 +722,12 @@
             out_v,
             sums_v,
             count,
+            lambda kind, i, dx, x=x, away=away: (
+                None if dx == away else turned_ref[len(TURNED) * kind + TURNED.index(i), x + dx]
+            ),
+            lambda dx, dz, x=x, away=away: (
+                None if dx == away else zfluid_ref[0 if dz == -1 else 1, x + dx]
+            ),
         )
         these = plane_stores(
             n, x, new_v, out_v, newf_ref, newg_ref, outf_ref, outg_ref, store_sem
@@ -715,7 +749,7 @@
 
 def outer_call(
     post, adjf, adjg, fluid, bcell, first, second, fromleft, fromright, cornerleft, cornerright,
-    profile, magnet, partial, newf, newg, outf, outg, scale,
+    profile, magnet, turned, zfluid, partial, newf, newg, outf, outg, scale,
 ):
     sx, sy, sz = profile.shape
     count = partial.shape[0]
@@ -723,7 +757,7 @@
     field = jax.ShapeDtypeStruct(newg.shape, jnp.float32)
     return pl.pallas_call(
         functools.partial(outer_kernel, scale),
-        in_specs=[VMEM] * 14 + [ANY] * 4,
+        in_specs=[VMEM] * 16 + [ANY] * 4,
         out_specs=[ANY] * 4 + [VMEM],
         out_shape=[
             flow,
@@ -732,7 +766,7 @@
             field,
             jax.ShapeDtypeStruct((lax.axis_size(("gx", "gy")), count), jnp.float32),
         ],
-        input_output_aliases={14: 0, 15: 1, 16: 2, 17: 3},
+        input_output_aliases={16: 0, 17: 1, 18: 2, 19: 3},
         scratch_shapes=[
             pltpu.VMEM((NP, 2, sy, sz), jnp.float32),
             pltpu.VMEM((NP, 2, sy, sz), jnp.float32),
@@ -745,7 +779,7 @@
         name="outer",
     )(
         second, fromleft, fromright, first, post, adjf, adjg, fluid, bcell, cornerleft,
-        cornerright, profile, magnet, partial, newf, newg, outf, outg,
+        cornerright, profile, magnet, turned, zfluid, partial, newf, newg, outf, outg,
     )
 
 
@@ -765,17 +799,20 @@
     first = lax.ppermute(mine1, "gy", inside)
     fromleft = lax.ppermute(right, "gx", ring(around, 1))
     fromright = lax.ppermute(left, "gx", ring(around, -1))
-    post, fluid, bcell = collide_call(flow, field, profile, table, wall, magnet)
+    post, fluid, bcell, turned, zfluid = collide_call(
+        flow, field, profile, table, wall, magnet, adj_flow_in, adj_field_in
+    )
     corner_r, corner_l = corner_call(first, second, bcell)
     cornerleft = lax.ppermute(corner_r, "gx", ring(around, 1))
     cornerright = lax.ppermute(corner_l, "gx", ring(around, -1))
     newf, newg, outf, outg, partial = inner_call(
-        post, adj_flow_in, adj_field_in, fluid, bcell, first, second, profile, magnet, count
+        post, adj_flow_in, adj_field_in, fluid, bcell, first, second, profile, magnet, turned,
+        zfluid, count,
     )
     cells = flow.shape[1] * around * flow.shape[2] * across * flow.shape[3]
     newf, newg, outf, outg, share = outer_call(
         post, adj_flow_in, adj_field_in, fluid, bcell, first, second, fromleft, fromright, cornerleft, cornerright,
-        profile, magnet, partial, newf, newg, outf, outg, 1.0 / math.sqrt(cells / count),
+        profile, magnet, turned, zfluid, partial, newf, newg, outf, outg, 1.0 / math.sqrt(cells / count),
     )
     totals = jnp.sum(lax.all_to_all(share, ("gx", "gy"), 0, 0, tiled=True), axis=0)
     return (newf, newg, outf, outg, totals)

time: 33.4 us -> 33.9 us (1.015)
  local copies, waits for them, and re-layouts: 0.04 us -> 1.73 us
  starting transfers between devices: 12.3 us -> 11.1 us
  waiting for transfers between devices: 0.76 us -> 0.02 us
  Pallas kernels: 9.12 us -> 9.81 us
    ppermute x1, starting transfers between devices: 3.01 us -> 0.6 us  [on_device(): cornerleft = lax.ppermute(corner_r, 'gx', ring(around, 1))]
    unnamed x16, local copies, waits for them, and re-layouts: 0.04 us -> 1.73 us
    ppermute x1, starting transfers between devices: 2.09 us -> 3.28 us  [on_device(): cornerright = lax.ppermute(corner_l, 'gx', ring(around, -1))]
    ppermute x1, waiting for transfers between devices: 0.75 us -> 0.01 us  [on_device(): cornerleft = lax.ppermute(corner_r, 'gx', ring(around, 1))]
    pallas_call x2, Pallas kernels: 4.97 us -> 5.7 us  [the longest x1 3.82 us: inner_call(): pl.pallas_call(inner_kernel, in_specs=[VMEM] * 11, out_specs=[ANY, ANY, A...]
  transfers between devices with their start and end apart: 6 -> 6, of which waited for: 1 -> 0; matrix products, arithmetic and copies ran while one was open for 0% -> 0% of each run, Pallas kernels for 15% -> 17%
where the time goes in v11:
time: 33.9 us; the launch traced here: 33.7 us
  starting transfers between devices  11.1 us (33%)
  Pallas kernels  9.81 us (29%)
  blocking collectives  9.65 us (28%)
  local copies, waits for them, and re-layouts  1.73 us (5%)
  between operations  0.82 us (2%)
  other arithmetic  0.56 us (2%)
    all_to_all x1, blocking collectives, on_device(): lax.all_to_all(share, ('gx', 'gy'), 0, 0, tiled=True)  9.65 us
    pallas_call x1, Pallas kernels, inner_call(): pl.pallas_call(inner_kernel, in_specs=[VMEM] * 11, out_specs=[ANY, ANY, A...  3.82 us
    ppermute x1, starting transfers between devices, on_device(): second = lax.ppermute(mine2, 'gy', between)  3.4 us
    ppermute x1, starting transfers between devices, on_device(): cornerright = lax.ppermute(corner_l, 'gx', ring(around, -1))  3.28 us
    pallas_call x1, Pallas kernels, rim_call(): pl.pallas_call(rim_kernel, in_specs=[ANY] * 8, out_specs=[VMEM] * 4, out_...  2.28 us
    ppermute x1, starting transfers between devices, on_device(): fromright = lax.ppermute(left, 'gx', ring(around, -1))  2.25 us
    pallas_call x1, Pallas kernels, collide_call(): pl.pallas_call(collide_kernel, in_specs=[VMEM] * 8, out_specs=[VMEM] * 5,...  1.88 us
    pallas_call x1, Pallas kernels, outer_call(): pl.pallas_call(functools.partial(outer_kernel, scale), in_specs=[VMEM] *...  1.81 us
  transfers between devices with their start and end apart: 6, of which 0 were waited for; matrix products, arithmetic and copies ran while one was open for 0% of the time, Pallas kernels for 17%

profile of v11, /device:TPU:0, one launch (start us, length us, event | category | flops | bytes accessed | tf_op | source)
XLA Modules:
  0.0 33.7 jit_solution(2796316805840156892)
XLA Ops:
  0.6 0.0 copy-start
  0.6 0.0 copy-start.1
  0.7 0.0 copy-start.3
  0.7 0.0 copy-start.4
  0.7 2.3 %rims.1 = (f32[13,8,512]{2,1,0:T(8,128)S(1)}, f32[13,8,512]{2,1,0:T(8,128)S(1)}, f32[13,8,512]{2,1,0:T(8,128)S(1)}, f32[13,8,512]{2,1,0:T(8,128)S(1)}) custom-call(f32[19,8,8,512]{3,2,1,0:T(8,128)} %flow_ref.3, f32[7,8,8,512]{3,2,1,0:T(8,128)} %field_ref.3, f32[19,8,8,512]{3,2,1,0:T(8,128)} %adjf_ref.7, f32[7,8,8,512]{3,2,1,0:T(8,128)} %adjg_ref.7, ...), custom_call_target="tpu_custom_call" | custom-call | tf_op jit(solution)/shard_map/rims/pallas_call | solution.py:256
  3.0 3.4 %collective-permute-start = (f32[13,8,512]{2,1,0:T(8,128)S(1)}, f32[13,8,512]{2,1,0:T(8,128)S(1)}, u32[]{:S(2)}, u32[]{:S(2)}) collective-permute-start(f32[13,8,512]{2,1,0:T(8,128)S(1)} %get-tuple-element.26), channel_id=1, source_target_pairs={{0,7},{1,2},{2,1},{3,4},{4,3},{5,6},{6,5},{7,0},{8,15},{9,10},{10,... | collective-permute-start | bytes 638984 | tf_op jit(solution)/shard_map/ppermute | solution.py:798
  6.4 0.0 collective-permute-start.3
  6.4 1.6 %collective-permute-start.1 = (f32[13,8,512]{2,1,0:T(8,128)S(1)}, f32[13,8,512]{2,1,0:T(8,128)S(1)}, u32[]{:S(2)}, u32[]{:S(2)}) collective-permute-start(f32[13,8,512]{2,1,0:T(8,128)S(1)} %get-tuple-element.27), channel_id=1, source_target_pairs={{0,8},{8,16},{16,24},{24,0},{1,9},{9,17},{17,25},{25,1},{2,10},{10... | collective-permute-start | bytes 638984 | tf_op jit(solution)/shard_map/ppermute | solution.py:800
  8.0 2.2 %collective-permute-start.2 = (f32[13,8,512]{2,1,0:T(8,128)S(1)}, f32[13,8,512]{2,1,0:T(8,128)S(1)}, u32[]{:S(2)}, u32[]{:S(2)}) collective-permute-start(f32[13,8,512]{2,1,0:T(8,128)S(1)} %get-tuple-element.28), channel_id=1, source_target_pairs={{0,24},{8,0},{16,8},{24,16},{1,25},{9,1},{17,9},{25,17},{2,26},{10... | collective-permute-start | bytes 638984 | tf_op jit(solution)/shard_map/ppermute | solution.py:801
  10.3 0.0 copy-start.2
  10.3 1.7 %copy-done.2 = f32[19,8,8,512]{3,2,1,0:T(8,128)S(1)} copy-done((f32[19,8,8,512]{3,2,1,0:T(8,128)S(1)}, f32[19,8,8,512]{3,2,1,0:T(8,128)}, u32[]{:S(2)}) %copy-start.2) | copy-done | bytes 2490392
  12.0 1.9 %collide.1 = (f32[26,8,8,512]{3,2,1,0:T(8,128)S(1)}, f32[8,8,512]{2,1,0:T(8,128)S(1)}, f32[8,8,512]{2,1,0:T(8,128)S(1)}, f32[16,8,8,512]{3,2,1,0:T(8,128)S(1)}, f32[2,8,8,512]{3,2,1,0:T(8,128)S(1)}) custom-call(f32[19,8,8,512]{3,2,1,0:T(8,128)S(1)} %copy-done.2, f32[7,8,8,512]{3,2,1,0:T(8,128)S(1)} %copy-done.3, f32[8,8,512]{2,1,0:T(8,128)S(1)} %copy-done.4, ...), custom_call_target="tpu_custom_call" | custom-call | flops 9830400 | bytes 10223616 | tf_op jit(solution)/shard_map/collide/pallas_call | solution.py:314
  13.9 0.0 collective-permute-done.second_ref
  13.9 0.0 collective-permute-done.3.first_ref
  13.9 0.6 %collective-permute-start.4 = (f32[8,512]{1,0:T(8,128)S(1)}, f32[8,512]{1,0:T(8,128)S(1)}, u32[]{:S(2)}, u32[]{:S(2)}) collective-permute-start(f32[8,512]{1,0:T(8,128)S(1)} %get-tuple-element.33), channel_id=1, source_target_pairs={{0,8},{8,16},{16,24},{24,0},{1,9},{9,17},{17,25},{25,1},{2,10},{10... | collective-permute-start | bytes 49160 | tf_op jit(solution)/shard_map/ppermute | solution.py:806
  14.5 3.3 %collective-permute-start.5 = (f32[8,512]{1,0:T(8,128)S(1)}, f32[8,512]{1,0:T(8,128)S(1)}, u32[]{:S(2)}, u32[]{:S(2)}) collective-permute-start(f32[8,512]{1,0:T(8,128)S(1)} %get-tuple-element.34), channel_id=1, source_target_pairs={{0,24},{8,0},{16,8},{24,16},{1,25},{9,1},{17,9},{25,17},{2,26},{10... | collective-permute-start | bytes 49160 | tf_op jit(solution)/shard_map/ppermute | solution.py:807
  17.8 3.8 %inner.1 = (f32[19,8,8,512]{3,2,1,0:T(8,128)}, f32[7,8,8,512]{3,2,1,0:T(8,128)}, f32[19,8,8,512]{3,2,1,0:T(8,128)}, f32[7,8,8,512]{3,2,1,0:T(8,128)}, f32[32,8,128]{2,1,0:T(8,128)S(1)}) custom-call(f32[26,8,8,512]{3,2,1,0:T(8,128)S(1)} %get-tuple-element.30.post_ref, f32[19,8,8,512]{3,2,1,0:T(8,128)S(1)} %copy-done, f32[7,8,8,512]{3,2,1,0:T(8,128)S(1)} %copy-done.1, ...), custom_call_target="tpu_custom_call" | custom-call | flops 22937600 | bytes 13631488 | tf_op jit(solution)/shard_map/inner/pallas_call | solution.py:649
  21.6 0.0 collective-permute-done.1.fromleft_ref
  21.6 0.0 collective-permute-done.2.fromright_ref
  21.6 0.0 collective-permute-done.4.cornerleft_ref
  21.6 0.0 collective-permute-done.5.cornerright_ref
  21.7 1.8 %outer.1 = (f32[19,8,8,512]{3,2,1,0:T(8,128)}, f32[7,8,8,512]{3,2,1,0:T(8,128)}, f32[19,8,8,512]{3,2,1,0:T(8,128)}, f32[7,8,8,512]{3,2,1,0:T(8,128)}, f32[32,32]{1,0:T(8,128)S(1)}) custom-call(f32[13,8,512]{2,1,0:T(8,128)S(1)} %collective-permute-done.second_ref, ...), custom_call_target="tpu_custom_call", output_to_operand_aliasing={{0}: (16, {}), {1}: (17, {}), {2}: (18, {}), {3}: (19, {})} | custom-call | tf_op jit(solution)/shard_map/outer/pallas_call | solution.py:758
  23.5 9.6 %all_to_all.9 = f32[32,1,32]{2,1,0:T(1,128)S(1)} all-to-all(f32[32,1,32]{2,1,0:T(1,128)S(1)} %bitcast.4), channel_id=1, replica_groups=mesh['gx'=4,'gy'=8] {'gx','gy'}, dimensions={0} | all-to-all | bytes 8192 | tf_op jit(solution)/shard_map/all_to_all | solution.py:817
  33.1 0.6 %reduce_sum.9 = f32[32]{0:T(128)} reduce(f32[32,1,32]{2,1,0:T(1,128)S(1)} %all_to_all.9, f32[]{:T(128)} %constant.0.clone.1), dimensions={0,1}, to_apply=%region_0.0 | reduce | flops 992 | bytes 4228 | tf_op jit(solution)/shard_map/reduce_sum | solution.py:817
  (11 shorter events, 0.0 us)
Async XLA Ops:
  0.6 9.6 %copy-start = (f32[19,8,8,512]{3,2,1,0:T(8,128)S(1)}, f32[19,8,8,512]{3,2,1,0:T(8,128)}, u32[]{:S(2)}) copy-start(f32[19,8,8,512]{3,2,1,0:T(8,128)} %adjf_ref.7) | copy-start | bytes 7471108
  0.6 9.6 %copy-start.1 = (f32[7,8,8,512]{3,2,1,0:T(8,128)S(1)}, f32[7,8,8,512]{3,2,1,0:T(8,128)}, u32[]{:S(2)}) copy-start(f32[7,8,8,512]{3,2,1,0:T(8,128)} %adjg_ref.7) | copy-start | bytes 2752516
  0.7 9.6 %copy-start.3 = (f32[7,8,8,512]{3,2,1,0:T(8,128)S(1)}, f32[7,8,8,512]{3,2,1,0:T(8,128)}, u32[]{:S(2)}) copy-start(f32[7,8,8,512]{3,2,1,0:T(8,128)} %field_ref.3) | copy-start | bytes 2752516
  0.7 9.6 %copy-start.4 = (f32[8,8,512]{2,1,0:T(8,128)S(1)}, f32[8,8,512]{2,1,0:T(8,128)}, u32[]{:S(2)}) copy-start(f32[8,8,512]{2,1,0:T(8,128)} %profile_ref.7) | copy-start | bytes 393220
  0.7 9.6 %copy-start.5 = (s32[8,8,512]{2,1,0:T(8,128)S(1)}, s32[8,8,512]{2,1,0:T(8,128)}, u32[]{:S(2)}) copy-start(s32[8,8,512]{2,1,0:T(8,128)} %magnet_ref.7) | copy-start | bytes 393220
  0.7 9.6 %copy-start.6 = (s32[8,8,512]{2,1,0:T(8,128)S(1)}, s32[8,8,512]{2,1,0:T(8,128)}, u32[]{:S(2)}) copy-start(s32[8,8,512]{2,1,0:T(8,128)} %wall_ref.3) | copy-start | bytes 393220
  0.7 9.6 %copy-start.7 = (f32[32]{0:T(128)S(1)}, f32[32]{0:T(128)}, u32[]{:S(2)}) copy-start(f32[32]{0:T(128)} %param.13) | copy-start | bytes 388
  3.0 10.9 %collective-permute-start = (f32[13,8,512]{2,1,0:T(8,128)S(1)}, f32[13,8,512]{2,1,0:T(8,128)S(1)}, u32[]{:S(2)}, u32[]{:S(2)}) collective-permute-start(f32[13,8,512]{2,1,0:T(8,128)S(1)} %get-tuple-element.26), channel_id=1, source_target_pairs={{0,7},{1,2},{2,1},{3,4},{4,3},{5,6},{6,5},{7,0},{8,15},{9,10},{10,... | collective-permute-start | bytes 638984 | tf_op jit(solution)/shard_map/ppermute | solution.py:798
  6.4 7.5 %collective-permute-start.3 = (f32[13,8,512]{2,1,0:T(8,128)S(1)}, f32[13,8,512]{2,1,0:T(8,128)S(1)}, u32[]{:S(2)}, u32[]{:S(2)}) collective-permute-start(f32[13,8,512]{2,1,0:T(8,128)S(1)} %get-tuple-element.29), channel_id=1, source_target_pairs={{0,1},{1,0},{2,3},{3,2},{4,5},{5,4},{6,7},{7,6},{8,9},{9,8},{10,11... | collective-permute-start | bytes 638984 | tf_op jit(solution)/shard_map/ppermute | solution.py:799
  6.4 15.2 %collective-permute-start.1 = (f32[13,8,512]{2,1,0:T(8,128)S(1)}, f32[13,8,512]{2,1,0:T(8,128)S(1)}, u32[]{:S(2)}, u32[]{:S(2)}) collective-permute-start(f32[13,8,512]{2,1,0:T(8,128)S(1)} %get-tuple-element.27), channel_id=1, source_target_pairs={{0,8},{8,16},{16,24},{24,0},{1,9},{9,17},{17,25},{25,1},{2,10},{10... | collective-permute-start | bytes 638984 | tf_op jit(solution)/shard_map/ppermute | solution.py:800
  8.0 13.7 %collective-permute-start.2 = (f32[13,8,512]{2,1,0:T(8,128)S(1)}, f32[13,8,512]{2,1,0:T(8,128)S(1)}, u32[]{:S(2)}, u32[]{:S(2)}) collective-permute-start(f32[13,8,512]{2,1,0:T(8,128)S(1)} %get-tuple-element.28), channel_id=1, source_target_pairs={{0,24},{8,0},{16,8},{24,16},{1,25},{9,1},{17,9},{25,17},{2,26},{10... | collective-permute-start | bytes 638984 | tf_op jit(solution)/shard_map/ppermute | solution.py:801
  10.3 1.7 %copy-start.2 = (f32[19,8,8,512]{3,2,1,0:T(8,128)S(1)}, f32[19,8,8,512]{3,2,1,0:T(8,128)}, u32[]{:S(2)}) copy-start(f32[19,8,8,512]{3,2,1,0:T(8,128)} %flow_ref.3) | copy-start | bytes 7471108
  13.9 7.7 %collective-permute-start.4 = (f32[8,512]{1,0:T(8,128)S(1)}, f32[8,512]{1,0:T(8,128)S(1)}, u32[]{:S(2)}, u32[]{:S(2)}) collective-permute-start(f32[8,512]{1,0:T(8,128)S(1)} %get-tuple-element.33), channel_id=1, source_target_pairs={{0,8},{8,16},{16,24},{24,0},{1,9},{9,17},{17,25},{25,1},{2,10},{10... | collective-permute-start | bytes 49160 | tf_op jit(solution)/shard_map/ppermute | solution.py:806
  14.5 7.1 %collective-permute-start.5 = (f32[8,512]{1,0:T(8,128)S(1)}, f32[8,512]{1,0:T(8,128)S(1)}, u32[]{:S(2)}, u32[]{:S(2)}) collective-permute-start(f32[8,512]{1,0:T(8,128)S(1)} %get-tuple-element.34), channel_id=1, source_target_pairs={{0,24},{8,0},{16,8},{24,16},{1,25},{9,1},{17,9},{25,17},{2,26},{10... | collective-permute-start | bytes 49160 | tf_op jit(solution)/shard_map/ppermute | solution.py:807

commit v12 on v7

--- a/solution.py
+++ b/solution.py
@@ -676,7 +676,8 @@
 
 
 def outer_kernel(
-    scale, post_ref, adjf_ref, adjg_ref, fluid_ref, bcell_ref, first_ref, second_ref, fromleft_ref, fromright_ref,
+    scale, second_ref, fromleft_ref, fromright_ref, first_ref, post_ref, adjf_ref, adjg_ref,
+    fluid_ref, bcell_ref,
     cornerleft_ref, cornerright_ref, profile_ref, magnet_ref,
     partial_ref, newf_in, newg_in, outf_in, outg_in,
     newf_ref, newg_ref, outf_ref, outg_ref, share_ref,
@@ -781,8 +782,8 @@
         compiler_params=pltpu.CompilerParams(vmem_limit_bytes=OUTER_VMEM),
         name="outer",
     )(
-        post, adjf, adjg, fluid, bcell, first, second, fromleft, fromright, cornerleft, cornerright,
-        profile, magnet, partial, newf, newg, outf, outg,
+        second, fromleft, fromright, first, post, adjf, adjg, fluid, bcell, cornerleft,
+        cornerright, profile, magnet, partial, newf, newg, outf, outg,
     )
 
 

time: 33.6 us -> 33.6 us (level)
  starting transfers between devices: 11.8 us -> 11.1 us
  blocking collectives: 9.02 us -> 9.69 us
    all_to_all x1, blocking collectives: 9.02 us -> 9.69 us  [on_device(): lax.all_to_all(share, ('gx', 'gy'), 0, 0, tiled=True)]
    ppermute x1, starting transfers between devices: 0.06 us -> 0.73 us  [on_device(): cornerleft = lax.ppermute(corner_r, 'gx', ring(around, 1))]
    ppermute x1, starting transfers between devices: 3.81 us -> 3.15 us  [on_device(): cornerright = lax.ppermute(corner_l, 'gx', ring(around, -1))]
    ppermute x1, starting transfers between devices: 0.52 us -> 0.01 us  [on_device(): first = lax.ppermute(mine1, 'gy', inside)]
where the time goes in v12:
time: 33.6 us; the launch traced here: 33.4 us
  Pallas kernels  11.3 us (34%)
  starting transfers between devices  11.1 us (33%)
  blocking collectives  9.69 us (29%)
  between operations  0.74 us (2%)
  other arithmetic  0.56 us (2%)
    all_to_all x1, blocking collectives, on_device(): lax.all_to_all(share, ('gx', 'gy'), 0, 0, tiled=True)  9.69 us
    pallas_call x1, Pallas kernels, inner_call(): pl.pallas_call(inner_kernel, in_specs=[VMEM] * 9, out_specs=[ANY, ANY, AN...  3.78 us
    pallas_call x1, Pallas kernels, collide_call(): pl.pallas_call(collide_kernel, in_specs=[ANY] * 6, out_specs=[VMEM] * 5,...  3.5 us
    ppermute x1, starting transfers between devices, on_device(): second = lax.ppermute(mine2, 'gy', between)  3.4 us
    ppermute x1, starting transfers between devices, on_device(): cornerright = lax.ppermute(corner_l, 'gx', ring(around, -1))  3.15 us
    ppermute x1, starting transfers between devices, on_device(): fromright = lax.ppermute(left, 'gx', ring(around, -1))  2.25 us
    pallas_call x1, Pallas kernels, rim_call(): pl.pallas_call(rim_kernel, in_specs=[ANY] * 8, out_specs=[VMEM] * 4, out_...  2.14 us
    pallas_call x1, Pallas kernels, outer_call(): pl.pallas_call(functools.partial(outer_kernel, scale), in_specs=[VMEM] *...  1.86 us
  transfers between devices with their start and end apart: 6, of which 0 were waited for; matrix products, arithmetic and copies ran while one was open for 0% of the time, Pallas kernels for 22%

profile of v12, /device:TPU:0, one launch (start us, length us, event | category | flops | bytes accessed | tf_op | source)
XLA Modules:
  0.0 33.4 jit_solution(17564578782919389597)
XLA Ops:
  0.6 2.1 %rims.1 = (f32[13,8,512]{2,1,0:T(8,128)S(1)}, f32[13,8,512]{2,1,0:T(8,128)S(1)}, f32[13,8,512]{2,1,0:T(8,128)S(1)}, f32[13,8,512]{2,1,0:T(8,128)S(1)}) custom-call(f32[19,8,8,512]{3,2,1,0:T(8,128)} %flow_ref.3, f32[7,8,8,512]{3,2,1,0:T(8,128)} %field_ref.3, f32[19,8,8,512]{3,2,1,0:T(8,128)} %adjf_ref.5, f32[7,8,8,512]{3,2,1,0:T(8,128)} %adjg_ref.5, ...), custom_call_target="tpu_custom_call" | custom-call | tf_op jit(solution)/shard_map/rims/pallas_call | solution.py:255
  2.8 0.0 copy-start
  2.8 0.0 copy-start.1
  2.8 3.4 %collective-permute-start = (f32[13,8,512]{2,1,0:T(8,128)S(1)}, f32[13,8,512]{2,1,0:T(8,128)S(1)}, u32[]{:S(2)}, u32[]{:S(2)}) collective-permute-start(f32[13,8,512]{2,1,0:T(8,128)S(1)} %get-tuple-element.26), channel_id=1, source_target_pairs={{0,7},{1,2},{2,1},{3,4},{4,3},{5,6},{6,5},{7,0},{8,15},{9,10},{10,... | collective-permute-start | bytes 638984 | tf_op jit(solution)/shard_map/ppermute | solution.py:802
  6.2 0.0 collective-permute-start.3
  6.2 1.6 %collective-permute-start.1 = (f32[13,8,512]{2,1,0:T(8,128)S(1)}, f32[13,8,512]{2,1,0:T(8,128)S(1)}, u32[]{:S(2)}, u32[]{:S(2)}) collective-permute-start(f32[13,8,512]{2,1,0:T(8,128)S(1)} %get-tuple-element.27), channel_id=1, source_target_pairs={{0,8},{8,16},{16,24},{24,0},{1,9},{9,17},{17,25},{25,1},{2,10},{10... | collective-permute-start | bytes 638984 | tf_op jit(solution)/shard_map/ppermute | solution.py:804
  7.8 2.2 %collective-permute-start.2 = (f32[13,8,512]{2,1,0:T(8,128)S(1)}, f32[13,8,512]{2,1,0:T(8,128)S(1)}, u32[]{:S(2)}, u32[]{:S(2)}) collective-permute-start(f32[13,8,512]{2,1,0:T(8,128)S(1)} %get-tuple-element.28), channel_id=1, source_target_pairs={{0,24},{8,0},{16,8},{24,16},{1,25},{9,1},{17,9},{25,17},{2,26},{10... | collective-permute-start | bytes 638984 | tf_op jit(solution)/shard_map/ppermute | solution.py:805
  10.0 3.5 %collide.1 = (f32[26,8,8,512]{3,2,1,0:T(8,128)S(1)}, f32[8,8,512]{2,1,0:T(8,128)S(1)}, f32[8,8,512]{2,1,0:T(8,128)S(1)}, f32[8,8,512]{2,1,0:T(8,128)S(1)}, s32[8,8,512]{2,1,0:T(8,128)S(1)}) custom-call(f32[19,8,8,512]{3,2,1,0:T(8,128)} %flow_ref.3, f32[7,8,8,512]{3,2,1,0:T(8,128)} %field_ref.3, f32[8,8,512]{2,1,0:T(8,128)} %profile_ref.3, f32[1,32]{1,0:T(1,128)} %bitcast.6, ...), custom_call_target="tpu_custom_call" | custom-call | flops 9830400 | bytes 10223616 | tf_op jit(solution)/shard_map/collide/pallas_call | solution.py:321
  13.5 0.0 collective-permute-done.second_ref
  13.6 0.0 collective-permute-done.3.first_ref
  13.6 0.7 %collective-permute-start.4 = (f32[8,512]{1,0:T(8,128)S(1)}, f32[8,512]{1,0:T(8,128)S(1)}, u32[]{:S(2)}, u32[]{:S(2)}) collective-permute-start(f32[8,512]{1,0:T(8,128)S(1)} %get-tuple-element.33), channel_id=1, source_target_pairs={{0,8},{8,16},{16,24},{24,0},{1,9},{9,17},{17,25},{25,1},{2,10},{10... | collective-permute-start | bytes 49160 | tf_op jit(solution)/shard_map/ppermute | solution.py:808
  14.3 3.1 %collective-permute-start.5 = (f32[8,512]{1,0:T(8,128)S(1)}, f32[8,512]{1,0:T(8,128)S(1)}, u32[]{:S(2)}, u32[]{:S(2)}) collective-permute-start(f32[8,512]{1,0:T(8,128)S(1)} %get-tuple-element.34), channel_id=1, source_target_pairs={{0,24},{8,0},{16,8},{24,16},{1,25},{9,1},{17,9},{25,17},{2,26},{10... | collective-permute-start | bytes 49160 | tf_op jit(solution)/shard_map/ppermute | solution.py:809
  17.5 0.0 copy-done
  17.5 0.0 copy-done.1
  17.5 3.8 %inner.1 = (f32[19,8,8,512]{3,2,1,0:T(8,128)}, f32[7,8,8,512]{3,2,1,0:T(8,128)}, f32[19,8,8,512]{3,2,1,0:T(8,128)}, f32[7,8,8,512]{3,2,1,0:T(8,128)}, f32[32,8,128]{2,1,0:T(8,128)S(1)}) custom-call(f32[26,8,8,512]{3,2,1,0:T(8,128)S(1)} %get-tuple-element.30.post_ref, f32[19,8,8,512]{3,2,1,0:T(8,128)S(1)} %copy-done, f32[7,8,8,512]{3,2,1,0:T(8,128)S(1)} %copy-done.1, ...), custom_call_target="tpu_custom_call" | custom-call | flops 22937600 | bytes 13631488 | tf_op jit(solution)/shard_map/inner/pallas_call | solution.py:658
  21.3 0.0 collective-permute-done.1.fromleft_ref
  21.3 0.0 collective-permute-done.2.fromright_ref
  21.3 0.0 collective-permute-done.4.cornerleft_ref
  21.3 0.0 collective-permute-done.5.cornerright_ref
  21.3 1.9 %outer.1 = (f32[19,8,8,512]{3,2,1,0:T(8,128)}, f32[7,8,8,512]{3,2,1,0:T(8,128)}, f32[19,8,8,512]{3,2,1,0:T(8,128)}, f32[7,8,8,512]{3,2,1,0:T(8,128)}, f32[32,32]{1,0:T(8,128)S(1)}) custom-call(f32[13,8,512]{2,1,0:T(8,128)S(1)} %collective-permute-done.second_ref, ...), custom_call_target="tpu_custom_call", output_to_operand_aliasing={{0}: (14, {}), {1}: (15, {}), {2}: (16, {}), {3}: (17, {})} | custom-call | tf_op jit(solution)/shard_map/outer/pallas_call | solution.py:762
  23.2 9.7 %all_to_all.9 = f32[32,1,32]{2,1,0:T(1,128)S(1)} all-to-all(f32[32,1,32]{2,1,0:T(1,128)S(1)} %bitcast.4), channel_id=1, replica_groups=mesh['gx'=4,'gy'=8] {'gx','gy'}, dimensions={0} | all-to-all | bytes 8192 | tf_op jit(solution)/shard_map/all_to_all | solution.py:818
  32.9 0.6 %reduce_sum.9 = f32[32]{0:T(128)} reduce(f32[32,1,32]{2,1,0:T(1,128)S(1)} %all_to_all.9, f32[]{:T(128)} %constant.0.clone.1), dimensions={0,1}, to_apply=%region_0.0 | reduce | flops 992 | bytes 4228 | tf_op jit(solution)/shard_map/reduce_sum | solution.py:818
  (1 shorter events, 0.0 us)
Async XLA Ops:
  2.8 14.7 %copy-start = (f32[19,8,8,512]{3,2,1,0:T(8,128)S(1)}, f32[19,8,8,512]{3,2,1,0:T(8,128)}, u32[]{:S(2)}) copy-start(f32[19,8,8,512]{3,2,1,0:T(8,128)} %adjf_ref.5) | copy-start | bytes 7471108
  2.8 14.7 %copy-start.1 = (f32[7,8,8,512]{3,2,1,0:T(8,128)S(1)}, f32[7,8,8,512]{3,2,1,0:T(8,128)}, u32[]{:S(2)}) copy-start(f32[7,8,8,512]{3,2,1,0:T(8,128)} %adjg_ref.5) | copy-start | bytes 2752516
  2.8 10.7 %collective-permute-start = (f32[13,8,512]{2,1,0:T(8,128)S(1)}, f32[13,8,512]{2,1,0:T(8,128)S(1)}, u32[]{:S(2)}, u32[]{:S(2)}) collective-permute-start(f32[13,8,512]{2,1,0:T(8,128)S(1)} %get-tuple-element.26), channel_id=1, source_target_pairs={{0,7},{1,2},{2,1},{3,4},{4,3},{5,6},{6,5},{7,0},{8,15},{9,10},{10,... | collective-permute-start | bytes 638984 | tf_op jit(solution)/shard_map/ppermute | solution.py:802
  6.2 7.3 %collective-permute-start.3 = (f32[13,8,512]{2,1,0:T(8,128)S(1)}, f32[13,8,512]{2,1,0:T(8,128)S(1)}, u32[]{:S(2)}, u32[]{:S(2)}) collective-permute-start(f32[13,8,512]{2,1,0:T(8,128)S(1)} %get-tuple-element.29), channel_id=1, source_target_pairs={{0,1},{1,0},{2,3},{3,2},{4,5},{5,4},{6,7},{7,6},{8,9},{9,8},{10,11... | collective-permute-start | bytes 638984 | tf_op jit(solution)/shard_map/ppermute | solution.py:803
  6.2 15.1 %collective-permute-start.1 = (f32[13,8,512]{2,1,0:T(8,128)S(1)}, f32[13,8,512]{2,1,0:T(8,128)S(1)}, u32[]{:S(2)}, u32[]{:S(2)}) collective-permute-start(f32[13,8,512]{2,1,0:T(8,128)S(1)} %get-tuple-element.27), channel_id=1, source_target_pairs={{0,8},{8,16},{16,24},{24,0},{1,9},{9,17},{17,25},{25,1},{2,10},{10... | collective-permute-start | bytes 638984 | tf_op jit(solution)/shard_map/ppermute | solution.py:804
  7.8 13.5 %collective-permute-start.2 = (f32[13,8,512]{2,1,0:T(8,128)S(1)}, f32[13,8,512]{2,1,0:T(8,128)S(1)}, u32[]{:S(2)}, u32[]{:S(2)}) collective-permute-start(f32[13,8,512]{2,1,0:T(8,128)S(1)} %get-tuple-element.28), channel_id=1, source_target_pairs={{0,24},{8,0},{16,8},{24,16},{1,25},{9,1},{17,9},{25,17},{2,26},{10... | collective-permute-start | bytes 638984 | tf_op jit(solution)/shard_map/ppermute | solution.py:805
  13.6 7.7 %collective-permute-start.4 = (f32[8,512]{1,0:T(8,128)S(1)}, f32[8,512]{1,0:T(8,128)S(1)}, u32[]{:S(2)}, u32[]{:S(2)}) collective-permute-start(f32[8,512]{1,0:T(8,128)S(1)} %get-tuple-element.33), channel_id=1, source_target_pairs={{0,8},{8,16},{16,24},{24,0},{1,9},{9,17},{17,25},{25,1},{2,10},{10... | collective-permute-start | bytes 49160 | tf_op jit(solution)/shard_map/ppermute | solution.py:808
  14.3 7.0 %collective-permute-start.5 = (f32[8,512]{1,0:T(8,128)S(1)}, f32[8,512]{1,0:T(8,128)S(1)}, u32[]{:S(2)}, u32[]{:S(2)}) collective-permute-start(f32[8,512]{1,0:T(8,128)S(1)} %get-tuple-element.34), channel_id=1, source_target_pairs={{0,24},{8,0},{16,8},{24,16},{1,25},{9,1},{17,9},{25,17},{2,26},{10... | collective-permute-start | bytes 49160 | tf_op jit(solution)/shard_map/ppermute | solution.py:809
